TPU v7x, 256 devices: a whole 4x4x8 slice. The times are simulated.
256 devices in a mesh: rep: 16 (over y, z_lo), fsdp: 16 (over x, z_hi, core).
Axes of the slice: x: 4, y: 4, z: 8 (z_hi: 2, z_lo: 4; z = z_hi * 4 + z_lo), core: 2. Of those that a mesh axis runs over, the one named last changes fastest.
Arguments:
- gradients: bfloat16 [16, 16, 1024, 2048], P('rep', 'fsdp'), may hold values from -6 to 6
- momentum: float32 [16, 1024, 2048], P('rep', None, 'fsdp'), may hold values from -12 to 12
- master_weights: float32 [1024, 2048], P(None, 'fsdp'), may hold values from -0.125 to 0.125
Outputs:
- new_momentum: float32 [16, 1024, 2048], P('rep', None, 'fsdp')
- new_master: float32 [1024, 2048], P(None, 'fsdp')
- weights_full: bfloat16 [1024, 2048], replicated
All inputs are finite; a program needn't handle non-finite values.
Results may differ from a plain program's by a relative error of at most 0.012.
Values may be sent and summed in bfloat16 or wider, within the bound.
No kernel may reach another device: no remote copies, remote signals or barrier semaphores. Data moves between devices by JAX's collectives and lax.ppermute only.
A program may use at most 128 MiB of HBM per device.

v0:
```python
import jax
import jax.numpy as jnp
from jax import lax
from jax.sharding import PartitionSpec as P

GROUP = 128
BAND = 16


momentum_decay = 0.9
step_size = 0.05


def sent_to_all(array, axis):
    devices = lax.axis_size(axis)
    return lax.all_to_all(
        jnp.broadcast_to(array[None], (devices, *array.shape)), axis, 0, 0, tiled=True
    )


def taken_together(array, axis):
    return sent_to_all(array, axis).sum(axis=0)


def joined_along(parts, dim):
    shape = list(parts.shape[1:])
    shape[dim] *= parts.shape[0]
    return jnp.moveaxis(parts, 0, dim).reshape(shape)


def collect(array, axis, dim):
    parts = sent_to_all(array, axis)
    return joined_along(parts, dim)


def cosine_rows():
    freq = jnp.arange(BAND, dtype=jnp.float32)[:, None]
    place = jnp.arange(GROUP, dtype=jnp.float32)[None, :]
    factor = jnp.where(freq == 0.0, jnp.sqrt(1.0 / GROUP), jnp.sqrt(2.0 / GROUP)).astype(
        jnp.float32
    )
    return factor * jnp.cos(jnp.pi * (2.0 * place + 1.0) * freq / (2.0 * GROUP))


def band_of(matrix):
    table = cosine_rows()
    blocks = matrix.reshape(matrix.shape[0] // GROUP, GROUP, matrix.shape[1] // GROUP, GROUP)
    return jnp.einsum("kr,arbc,lc->abkl", table, blocks, table)


def spread_band(coeffs):
    table = cosine_rows()
    blocks = jnp.einsum("kr,abkl,lc->arbc", table, coeffs, table)
    return blocks.reshape(coeffs.shape[0] * GROUP, coeffs.shape[1] * GROUP)


def local(gradients, momentum, master_weights):
    prior_full = lax.all_gather(
        master_weights.astype(jnp.bfloat16), "fsdp", axis=1, tiled=True
    ).astype(master_weights.dtype)
    summed = lax.psum_scatter(
        gradients[0, 0].astype(jnp.float32).astype(jnp.bfloat16),
        "fsdp",
        scatter_dimension=1,
        tiled=True,
    ).astype(jnp.float32)
    moment = momentum_decay * momentum[0] + summed
    own_band = band_of(moment)
    remaining = moment - spread_band(own_band)
    mean_band = taken_together(own_band, "rep") / lax.axis_size("rep")
    band_table = collect(mean_band, "fsdp", 1)
    updated_full = prior_full - step_size * spread_band(band_table)
    shard_width = master_weights.shape[1]
    first_column = lax.axis_index("fsdp") * shard_width
    new_master = lax.dynamic_slice_in_dim(updated_full, first_column, shard_width, 1)
    weights_full = updated_full.astype(jnp.bfloat16)
    return (remaining[None], new_master, weights_full)


def solution(mesh):
    return jax.shard_map(
        local,
        mesh=mesh,
        in_specs=(P("rep", "fsdp", None, None), P("rep", None, "fsdp"), P(None, "fsdp")),
        out_specs=(P("rep", None, "fsdp"), P(None, "fsdp"), P()),
        check_vma=False,
    )
```

profile of v0, /device:TPU:33, one launch (start us, length us, event | category | flops | bytes accessed | tf_op | source)
XLA Modules:
  0.0 220.3 jit_solution(7198266306413594838)
XLA Ops:
  7.2 6.5 %copy.24 = bf16[1024,2048]{0,1:T(8,128)(2,1)} copy(bf16[1024,2048]{1,0:T(8,128)(2,1)} %bitcast.51) | data formatting | bytes 8388608
  13.8 0.7 convert_element_type.15
  14.6 104.2 %reduce-scatter.4.cloned.1.call-done = bf16[128,1024]{1,0:T(8,128)(2,1)} async-done(((bf16[2048,1024]{1,0:T(8,128)(2,1)}), bf16[128,1024]{1,0:T(8,128)(2,1)}) %reduce-scatter.4.cloned.1.call-update) | async-done | bytes 262160
  118.8 1.1 copy.25
  120.0 0.3 fusion.3
  120.3 0.1 broadcast_in_dim.36
  120.4 1.0 reshape.66
  121.5 5.2 %all-to-all-start = ((f32[16,1,2048]{2,1,0:T(1,128)}), f32[16,1,2048]{2,1,0:T(1,128)S(1)}, u32[]{:S(2)}, u32[]{:S(2)}) async-start(f32[16,1,2048]{2,1,0:T(1,128)} %reshape.66), calls=%async_computation | async-start | bytes 262144 | tf_op jit(solution)/shard_map/all_to_all | solution.py:16
  126.7 0.2 convolution_bitcast_fusion
  126.9 6.2 %all-to-all-done = f32[16,1,2048]{2,1,0:T(1,128)S(1)} async-done(((f32[16,1,2048]{2,1,0:T(1,128)}), f32[16,1,2048]{2,1,0:T(1,128)S(1)}, u32[]{:S(2)}, u32[]{:S(2)}) %all-to-all-start) | async-done | bytes 131104 | tf_op jit(solution)/shard_map/all_to_all | solution.py:16
  133.1 0.5 broadcast.93
  133.6 1.0 reduce.1
  134.5 0.4 reshape.67
  135.1 0.1 broadcast_bitcast_fusion
  135.2 1.2 reshape.68
  136.4 8.9 %all-to-all-start.1 = ((bf16[16,2,1024]{2,1,0:T(2,128)(2,1)}), bf16[16,2,1024]{2,1,0:T(2,128)(2,1)S(1)}, u32[]{:S(2)}, u32[]{:S(2)}) async-start(bf16[16,2,1024]{2,1,0:T(2,128)(2,1)} %reshape.68), calls=%async_computation.1 | async-start | bytes 131072 | tf_op jit(solution)/shard_map/all_to_all | solution.py:16
  145.3 1.1 fusion.2
  146.4 9.1 %all-to-all-done.1 = bf16[16,2,1024]{2,1,0:T(2,128)(2,1)S(1)} async-done(((bf16[16,2,1024]{2,1,0:T(2,128)(2,1)}), bf16[16,2,1024]{2,1,0:T(2,128)(2,1)S(1)}, u32[]{:S(2)}, u32[]{:S(2)}) %all-to-all-start.1) | async-done | bytes 65568 | tf_op jit(solution)/shard_map/all_to_all | solution.py:16
  155.4 0.4 reshape.69
  155.8 4.4 %multiply_bitcast_fusion = f32[8,128,16,128]{3,1,2,0:T(8,128)} fusion(f32[128]{0:T(128)S(1)} %add_multiply_fusion, f32[16]{0:T(128)S(1)} %compare_select_fusion, bf16[16,1,8,16,16]{4,3,2,1,0:T(8,128)(2,1)S(1)} %reshape.69), kind=kOutput, calls=%fused_computation.1 | convolution fusion | flops 77606912 | bytes 8454720 | tf_op jit(solution)/shard_map/kr,abkl,lc->arbc/dot_general | solution.py:53
  160.2 11.3 %copy.21 = f32[8,128,16,128]{3,2,1,0:T(8,128)} copy(f32[8,128,16,128]{3,1,2,0:T(8,128)} %multiply_bitcast_fusion) | data formatting | bytes 16777216 | tf_op jit(solution)/shard_map/mul | solution.py:72
  171.5 26.1 %all-gather.2.cloned.1.call-done = bf16[1024,2048]{1,0:T(8,128)(2,1)} async-done(((bf16[1024,128]{1,0:T(8,128)(2,1)}), bf16[1024,2048]{1,0:T(8,128)(2,1)}) %all-gather.2.cloned.1.call-update) | async-done | bytes 4194320 | tf_op jit(solution)/shard_map/all_gather | solution.py:58
  197.5 14.1 %fusion.41 = (bf16[1024,2048]{1,0:T(8,128)(2,1)}, f32[1024,2048]{1,0:T(8,128)}) fusion(f32[128,8,16,128]{3,2,1,0:T(8,128)} %bitcast.48, bf16[1024,2048]{1,0:T(8,128)(2,1)} %all-gather.2.cloned.1.call-done), kind=kLoop, calls=%fused_computation.37 | loop fusion | flops 6291456 | bytes 25165824 | tf_op jit(solution)/shard_map/convert_element_type | solution.py:76
  211.6 1.9 constant_dynamic-slice_fusion
  (14 shorter events, 0.4 us)
Async XLA Ops:
  7.2 6.6 %copy-start = (f32[1024,128]{1,0:T(8,128)S(1)}, f32[1024,128]{1,0:T(8,128)}, u32[]{:S(2)}) copy-start(f32[1024,128]{1,0:T(8,128)} %param.5) | copy-start | bytes 1572868
  7.2 112.8 %copy-start.1 = (f32[1,1024,128]{2,1,0:T(8,128)S(1)}, f32[1,1024,128]{2,1,0:T(8,128)}, u32[]{:S(2)}) copy-start(f32[1,1024,128]{2,1,0:T(8,128)} %param.4) | copy-start | bytes 1572868
  7.2 111.6 %reduce-scatter.4.cloned.1.call-start = ((), (), s32[]{:S(2)}) async-start(), calls=%async_computation.4 | async-start | bytes 4456448
  13.7 183.8 %all-gather.2.cloned.1.call-start = ((), (), s32[]{:S(2)}) async-start(), calls=%async_computation.3 | async-start | bytes 4456448 | tf_op jit(solution)/shard_map/all_gather | solution.py:58
  121.5 11.6 %all-to-all-start = ((f32[16,1,2048]{2,1,0:T(1,128)}), f32[16,1,2048]{2,1,0:T(1,128)S(1)}, u32[]{:S(2)}, u32[]{:S(2)}) async-start(f32[16,1,2048]{2,1,0:T(1,128)} %reshape.66), calls=%async_computation | async-start | bytes 262144 | tf_op jit(solution)/shard_map/all_to_all | solution.py:16
  136.4 19.0 %all-to-all-start.1 = ((bf16[16,2,1024]{2,1,0:T(2,128)(2,1)}), bf16[16,2,1024]{2,1,0:T(2,128)(2,1)S(1)}, u32[]{:S(2)}, u32[]{:S(2)}) async-start(bf16[16,2,1024]{2,1,0:T(2,128)(2,1)} %reshape.68), calls=%async_computation.1 | async-start | bytes 131072 | tf_op jit(solution)/shard_map/all_to_all | solution.py:16
Sparse Core Ops, SparseCore 0:
  13.9 104.9 reduce-scatter.3
  122.3 75.2 all-gather.1
where the time goes:
time: 223 us; the launch traced here: 220 us
  waiting for transfers between devices  146 us (65%)
  local copies, waits for them, and re-layouts  24.6 us (11%)
  other arithmetic  15.9 us (7%)
  between operations  14.2 us (6%)
  starting transfers between devices  14.1 us (6%)
  matrix products  5.95 us (3%)
    unnamed x3, waiting for transfers between devices  104 us
    all_gather x1, waiting for transfers between devices, local(): lax.all_gather(master_weights.astype(jnp.bfloat16), 'fsdp', axis=1, tiled...  26.1 us
    all_to_all x2, waiting for transfers between devices, sent_to_all(): lax.all_to_all(jnp.broadcast_to(array[None], (devices, *array.shape)), ax...  15.3 us
    convert_element_type x1, other arithmetic, local(): weights_full = updated_full.astype(jnp.bfloat16)  14.1 us
    all_to_all x2, starting transfers between devices, sent_to_all(): lax.all_to_all(jnp.broadcast_to(array[None], (devices, *array.shape)), ax...  14.1 us
    mul x1, local copies, waits for them, and re-layouts, local(): updated_full = prior_full - step_size * spread_band(band_table)  11.3 us
    unnamed x11, local copies, waits for them, and re-layouts  10.7 us
    dot_general x3, matrix products, spread_band(): blocks = jnp.einsum('kr,abkl,lc->arbc', table, coeffs, table)  5.64 us
  transfers between devices with their start and end apart: 4, of which 4 were waited for; matrix products, arithmetic and copies ran while one was open for 11% of the time, Pallas kernels for 0%

commit v1 on v0

v1 whole, which is shorter than its diff:
```python
import functools

import jax
import jax.numpy as jnp
import numpy as np
from jax import lax
from jax.experimental import pallas as pl
from jax.experimental.pallas import tpu as pltpu
from jax.sharding import Mesh
from jax.sharding import PartitionSpec as P

GROUP = 128
BAND = 16
ROWS = 1024
HALF = 512
QUARTER = 256

momentum_decay = 0.9
step_size = 0.05
replicas = 16

bf16 = jnp.bfloat16
f32 = jnp.float32
HIGHEST = lax.Precision.HIGHEST

SWAP2 = [(0, 1), (1, 0)]
UP4 = [(i, (i + 1) % 4) for i in range(4)]
DOWN4 = [(i, (i + 3) % 4) for i in range(4)]
ACROSS4 = [(i, (i + 2) % 4) for i in range(4)]
EVEN4 = [(0, 1), (1, 0), (2, 3), (3, 2)]
ODD4 = [(1, 2), (2, 1), (3, 0), (0, 3)]
XOR2 = [(i, i ^ 2) for i in range(4)]
MIRROR8 = [(i, 7 - i) for i in range(8)]


def cosine_rows():
    freq = np.arange(BAND, dtype=np.float64)[:, None]
    place = np.arange(GROUP, dtype=np.float64)[None, :]
    factor = np.where(freq == 0.0, np.sqrt(1.0 / GROUP), np.sqrt(2.0 / GROUP))
    return factor * np.cos(np.pi * (2.0 * place + 1.0) * freq / (2.0 * GROUP))


def column_of(dx, gz, core):
    bx = lax.rem(lax.axis_index("x") + dx, 4)
    zh = lax.axis_index("zh")
    bz = zh if gz == 0 else 1 - zh
    return bx * 4 + bz * 2 + core


def slot_of(dx, gz):
    bx = lax.rem(lax.axis_index("x") + dx, 4)
    zh = lax.axis_index("zh")
    return bx * 2 + (zh if gz == 0 else 1 - zh)


def lanes(index):
    return pl.ds(pl.multiple_of(index * GROUP, GROUP), GROUP)


def gather_kernel(partner, g_ref, out_ref, sem):
    core = lax.axis_index("core")
    core = 1 - core if partner else core
    copies = []
    for gz in range(2):
        for dx in range(4):
            k = gz * 4 + dx
            copies.append(
                pltpu.make_async_copy(
                    g_ref.at[:, lanes(column_of(dx, gz, core))], out_ref.at[k], sem.at[k]
                )
            )
    for c in copies:
        c.start()
    for c in copies:
        c.wait()


def gather_blocks(g, partner):
    return pl.pallas_call(
        functools.partial(gather_kernel, partner),
        out_shape=jax.ShapeDtypeStruct((8, ROWS, GROUP), bf16),
        in_specs=[pl.BlockSpec(memory_space=pl.ANY)],
        out_specs=pl.BlockSpec(memory_space=pl.ANY),
        scratch_shapes=[pltpu.SemaphoreType.DMA((8,))],
    )(g)


def pair_sum_kernel(
    own_ref, other_ref, mom_ref, table_ref, rows_ref, up_ref, down_ref, keep_up_ref, keep_down_ref,
    own_out_ref, band_ref, acc_ref,
):
    lane_slot = lax.broadcasted_iota(jnp.int32, (GROUP, GROUP), 1) // BAND
    table = table_ref[...]
    zero = jnp.zeros_like(table)
    total = None
    for gz in range(2):
        for dx in range(4):
            k = gz * 4 + dx
            s = (own_ref[k].astype(f32) + other_ref[k].astype(f32)).astype(bf16)
            if dx == 0:
                own_out_ref[gz] = s
            elif dx == 1:
                keep_up_ref[gz] = s[:HALF]
                up_ref[gz, 1] = s[HALF:]
            elif dx == 2:
                up_ref[gz, 0] = s[:HALF]
                down_ref[gz, 0] = s[HALF:]
            else:
                down_ref[gz, 1] = s[:HALF]
                keep_down_ref[gz] = s[HALF:]
            placed = jnp.where(lane_slot == slot_of(dx, gz), table, zero)
            part = jnp.dot(s, placed.astype(bf16), preferred_element_type=f32)
            if k == 0:
                part += jnp.dot(momentum_decay * mom_ref[...], placed, preferred_element_type=f32)
                acc_ref[...] = part
            else:
                acc_ref[...] += part
    for a in range(ROWS // GROUP):
        band_ref[a * BAND : (a + 1) * BAND, :] = jnp.dot(
            rows_ref[...],
            acc_ref[a * GROUP : (a + 1) * GROUP, :],
            precision=HIGHEST,
            preferred_element_type=f32,
        )


def pair_sum(own, other, mom, table, rows):
    shapes = [
        jax.ShapeDtypeStruct((2, 2, HALF, GROUP), bf16),
        jax.ShapeDtypeStruct((2, 2, HALF, GROUP), bf16),
        jax.ShapeDtypeStruct((2, HALF, GROUP), bf16),
        jax.ShapeDtypeStruct((2, HALF, GROUP), bf16),
        jax.ShapeDtypeStruct((2, ROWS, GROUP), bf16),
        jax.ShapeDtypeStruct((ROWS // GROUP * BAND, GROUP), f32),
    ]
    return pl.pallas_call(
        pair_sum_kernel,
        out_shape=shapes,
        scratch_shapes=[pltpu.VMEM((ROWS, GROUP), f32)],
        compiler_params=pltpu.CompilerParams(vmem_limit_bytes=40 * 2**20),
    )(own, other, mom, table, rows)


def remaining_kernel(own_ref, near_ref, far_ref, z_ref, mom_ref, q_ref, out_ref):
    q = q_ref[...]
    for a in range(ROWS // GROUP):
        r = slice(a * GROUP, (a + 1) * GROUP)
        summed = own_ref[r].astype(f32) + near_ref[r].astype(f32)
        summed = summed + far_ref[r].astype(f32) + z_ref[r].astype(f32)
        moment = momentum_decay * mom_ref[r] + summed
        low = jnp.dot(moment, q, precision=HIGHEST, preferred_element_type=f32)
        low = jnp.dot(q, low, precision=HIGHEST, preferred_element_type=f32)
        out_ref[r] = moment - low


def remaining_of(own, near, far, z, mom, q):
    return pl.pallas_call(
        remaining_kernel,
        out_shape=jax.ShapeDtypeStruct((ROWS, GROUP), f32),
        compiler_params=pltpu.CompilerParams(vmem_limit_bytes=40 * 2**20),
    )(own, near, far, z, mom, q)


def weights_kernel(
    *refs,
):
    own, partner = refs[0:5], refs[5:10]
    band_refs = refs[10:12]
    master_ref, cols_ref, table_ref = refs[12:15]
    master_out, full_out = refs[15:17]
    update_ref, page_ref, sem = refs[17:20]
    core = lax.axis_index("core")
    y = lax.axis_index("y")
    copies = []
    wide = jnp.concatenate([table_ref[...]] * 8, axis=0)
    wide = jnp.concatenate([wide] * 8, axis=1)
    row_slot = lax.broadcasted_iota(jnp.int32, wide.shape, 0) // BAND
    lane_slot = lax.broadcasted_iota(jnp.int32, wide.shape, 1) // GROUP
    wide = jnp.where(row_slot == lane_slot, wide, jnp.zeros_like(wide)).astype(bf16)
    for step, dy in enumerate((0, 3, 1, 2)):
        quarter = lax.rem(y + dy, 4)
        if step >= 2:
            copies[step - 2].wait()
        page = step % 2
        for who in range(2):
            side = core if who == 0 else 1 - core
            pieces = own if who == 0 else partner
            for half in range(2):
                a = quarter * 2 + half
                coeffs = band_refs[who][pl.ds(pl.multiple_of(a * BAND, BAND), BAND), :]
                spread = jnp.dot(
                    cols_ref[...], coeffs, precision=HIGHEST, preferred_element_type=f32
                )
                update_ref[half * GROUP : (half + 1) * GROUP, :] = jnp.dot(
                    spread.astype(bf16), wide, preferred_element_type=f32
                )
            for dx in range(4):
                for gz in range(2):
                    if step < 3:
                        prior = pieces[step][dx, gz]
                    elif dx < 2:
                        prior = pieces[3][dx, gz]
                    else:
                        prior = pieces[4][dx - 2, gz]
                    new = prior.astype(f32) + update_ref[:, lanes(slot_of(dx, gz))]
                    page_ref[page, :, lanes(column_of(dx, gz, side))] = new.astype(bf16)
            if who == 0:
                rows = pl.ds(pl.multiple_of(quarter * QUARTER, QUARTER), QUARTER)
                master_out[rows, :] = master_ref[rows, :] + update_ref[:, lanes(slot_of(0, 0))]
        copy = pltpu.make_async_copy(
            page_ref.at[page],
            full_out.at[pl.ds(pl.multiple_of(quarter * QUARTER, QUARTER), QUARTER), :],
            sem.at[step],
        )
        copy.start()
        copies.append(copy)
    copies[2].wait()
    copies[3].wait()


def weights_of(own, partner, bands, master, cols, table):
    vmem = pl.BlockSpec(memory_space=pltpu.VMEM)
    return pl.pallas_call(
        weights_kernel,
        out_shape=[
            jax.ShapeDtypeStruct((ROWS, GROUP), f32),
            jax.ShapeDtypeStruct((ROWS, 16 * GROUP), bf16),
        ],
        in_specs=[vmem] * 15,
        out_specs=[vmem, pl.BlockSpec(memory_space=pl.ANY)],
        scratch_shapes=[
            pltpu.VMEM((QUARTER, 8 * GROUP), f32),
            pltpu.VMEM((2, QUARTER, 16 * GROUP), bf16),
            pltpu.SemaphoreType.DMA((4,)),
        ],
        compiler_params=pltpu.CompilerParams(vmem_limit_bytes=48 * 2**20),
    )(*own, *partner, *bands, master, cols, table)


def added(a, b):
    return (a.astype(f32) + b.astype(f32)).astype(bf16)


def local(gradients, momentum, master_weights):
    table = cosine_rows()
    g = gradients[0, 0]
    mom = momentum[0]

    sent = gather_blocks(g, True)
    other = lax.ppermute(sent, "core", SWAP2)
    own = gather_blocks(g, False)

    y = lax.axis_index("y")
    w0 = lax.dynamic_slice_in_dim(master_weights, y * QUARTER, QUARTER, 0).astype(bf16)
    wz = lax.ppermute(w0, ("zl", "zh"), MIRROR8)
    w1 = jnp.stack([w0, wz])
    w_right = lax.ppermute(w1, "x", DOWN4)
    w_left = lax.ppermute(w1, "x", UP4)
    w_far = lax.ppermute(w1, "x", ACROSS4)
    q0 = jnp.stack([w1, w_right, w_far, w_left])
    qm = lax.ppermute(q0, "y", UP4)
    qp = lax.ppermute(q0, "y", DOWN4)
    q2a = lax.ppermute(qm[:2], "y", UP4)
    q2b = lax.ppermute(qp[2:], "y", DOWN4)
    own_w = (q0, qm, qp, q2a, q2b)
    partner_w = tuple(lax.ppermute(p, "core", SWAP2) for p in own_w)

    up, down, keep_up, keep_down, mine, band = pair_sum(
        own,
        other,
        mom,
        jnp.asarray(np.tile(table.T, (1, 8)), f32),
        jnp.asarray(table, f32),
    )

    totals = {}
    for gz in (1, 0):
        from_left = lax.ppermute(up[gz], "x", UP4)
        from_right = lax.ppermute(down[gz], "x", DOWN4)
        last_left = lax.ppermute(added(keep_up[gz], from_left[0]), "x", UP4)
        last_right = lax.ppermute(added(keep_down[gz], from_right[0]), "x", DOWN4)
        near = jnp.concatenate([from_right[1], from_left[1]])
        far = jnp.concatenate([last_left, last_right])
        totals[gz] = (mine[gz], near, far)
    a, b, c = totals[1]
    z_send = (a.astype(f32) + b.astype(f32) + c.astype(f32)).astype(bf16)
    from_z = lax.ppermute(z_send, "zh", SWAP2)

    for axis, perm in (
        ("x", EVEN4),
        ("x", ODD4),
        ("y", EVEN4),
        ("y", ODD4),
        ("zl", EVEN4),
        ("zl", XOR2),
        (("zl", "zh"), MIRROR8),
    ):
        band = band + lax.ppermute(band, axis, perm)
    band = band * (-step_size / replicas)
    band_other = lax.ppermute(band, "core", SWAP2)

    new_momentum = remaining_of(
        *totals[0], from_z, mom, jnp.asarray(table.T @ table, f32)
    )
    new_master, weights_full = weights_of(
        own_w,
        partner_w,
        (band, band_other),
        master_weights,
        jnp.asarray(table.T, f32),
        jnp.asarray(table, f32),
    )
    return (new_momentum[None], new_master, weights_full)


def solution(mesh):
    fine = Mesh(mesh.devices.reshape(4, 4, 4, 2, 2), ("y", "zl", "x", "zh", "core"))
    rep, fsdp = ("y", "zl"), ("x", "zh", "core")
    return jax.shard_map(
        local,
        mesh=fine,
        in_specs=(P(rep, fsdp, None, None), P(rep, None, fsdp), P(None, fsdp)),
        out_specs=(P(rep, None, fsdp), P(None, fsdp), P()),
        check_vma=False,
    )
```

time: 223 us -> 231 us (1.036)
  Pallas kernels: 0 us -> 143 us
  waiting for transfers between devices: 146 us -> 25.9 us
  starting transfers between devices: 14.1 us -> 52.7 us
  local copies, waits for them, and re-layouts: 24.6 us -> 5.52 us
  other arithmetic: 15.9 us -> 0.44 us
  between operations: 14.2 us -> 0.99 us
  matrix products: 5.95 us -> 0 us
    pallas_call x0 -> x5, Pallas kernels: none -> 143 us  [the longest x2 129 us: gather_blocks(): pl.pallas_call(functools.partial(gather_kernel, partner), out_shape=jax.S...]
    unnamed x3 -> x0, waiting for transfers between devices: 104 us -> none
    ppermute x0 -> x31, starting transfers between devices: none -> 52.7 us  [the longest x7 13.2 us: local(): band = band + lax.ppermute(band, axis, perm)]
    all_gather x1 -> x0, waiting for transfers between devices: 26.1 us -> none  [local(): lax.all_gather(master_weights.astype(jnp.bfloat16), 'fsdp', axis=1, tiled...]
    ppermute x0 -> x31, waiting for transfers between devices: none -> 25.9 us  [the longest x7 18.6 us: local(): band = band + lax.ppermute(band, axis, perm)]
    all_to_all x2 -> x0, waiting for transfers between devices: 15.3 us -> none  [sent_to_all(): lax.all_to_all(jnp.broadcast_to(array[None], (devices, *array.shape)), ax...]
    convert_element_type x2 -> x3, other arithmetic: 14.8 us -> 0.25 us  [the longest x2 0.14 us: added(): return (a.astype(f32) + b.astype(f32)).astype(bf16)]
    all_to_all x2 -> x0, starting transfers between devices: 14.1 us -> none  [sent_to_all(): lax.all_to_all(jnp.broadcast_to(array[None], (devices, *array.shape)), ax...]
  transfers between devices with their start and end apart: 4 -> 31, of which waited for: 4 -> 11; matrix products, arithmetic and copies ran while one was open for 11% -> 2% of each run, Pallas kernels for 0% -> 33%
where the time goes in v1:
time: 231 us; the launch traced here: 229 us
  Pallas kernels  143 us (62%)
  starting transfers between devices  52.7 us (23%)
  waiting for transfers between devices  25.9 us (11%)
  local copies, waits for them, and re-layouts  5.52 us (2%)
    pallas_call x2, Pallas kernels, gather_blocks(): pl.pallas_call(functools.partial(gather_kernel, partner), out_shape=jax.S...  129 us
    ppermute x7, waiting for transfers between devices, local(): band = band + lax.ppermute(band, axis, perm)  18.6 us
    ppermute x7, starting transfers between devices, local(): band = band + lax.ppermute(band, axis, perm)  13.2 us
    pallas_call x1, Pallas kernels, weights_of(): pl.pallas_call(weights_kernel, out_shape=[jax.ShapeDtypeStruct((ROWS, GRO...  9.67 us
    ppermute x5, starting transfers between devices, local(): partner_w = tuple((lax.ppermute(p, 'core', SWAP2) for p in own_w))  8.96 us
    ppermute x1, starting transfers between devices, local(): wz = lax.ppermute(w0, ('zl', 'zh'), MIRROR8)  5.57 us
    ppermute x2, starting transfers between devices, local(): last_right = lax.ppermute(added(keep_down[gz], from_right[0]), 'x', DOWN4)  4.94 us
    ppermute x1, starting transfers between devices, local(): from_z = lax.ppermute(z_send, 'zh', SWAP2)  4.64 us
  transfers between devices with their start and end apart: 31, of which 11 were waited for; matrix products, arithmetic and copies ran while one was open for 2% of the time, Pallas kernels for 33%

profile of v1, /device:TPU:33, one launch (start us, length us, event | category | flops | bytes accessed | tf_op | source)
XLA Modules:
  0.0 228.6 jit_solution(3573971517156143222)
XLA Ops:
  0.6 64.7 %shard_map.104 = bf16[8,1024,128]{2,1,0:T(8,128)(2,1)} custom-call(bf16[1024,2048]{1,0:T(8,128)(2,1)} %bitcast.42), custom_call_target="tpu_custom_call" | custom-call | tf_op jit(solution)/shard_map/pallas_call | solution.py:79
  67.0 5.6 %collective-permute-start.10 = (bf16[256,128]{1,0:T(8,128)(2,1)S(1)}, bf16[256,128]{1,0:T(8,128)(2,1)S(1)}, u32[]{:S(2)}, u32[]{:S(2)}) collective-permute-start(bf16[256,128]{1,0:T(8,128)(2,1)S(1)} %dynamic-slice_convert_fusion), channel_id=1, source_target_pairs={{0,50},{2,48},{16,34},{18,32},{32,18},{34,16},{48,2},{50,0},{1,51}... | collective-permute-start | bytes 196616 | tf_op jit(solution)/shard_map/ppermute | solution.py:255
  76.4 2.5 %collective-permute-start.12 = (bf16[2,256,128]{2,1,0:T(8,128)(2,1)S(1)}, bf16[2,256,128]{2,1,0:T(8,128)(2,1)S(1)}, u32[]{:S(2)}, u32[]{:S(2)}) collective-permute-start(bf16[2,256,128]{2,1,0:T(8,128)(2,1)S(1)} %get-tuple-element.28), channel_id=1, source_target_pairs={{0,8},{4,12},{8,0},{12,4},{1,9},{5,13},{9,1},{13,5},{2,10},{6,14},... | collective-permute-start | bytes 393224 | tf_op jit(solution)/shard_map/ppermute | solution.py:259
  80.8 3.8 %collective-permute-done.12 = bf16[2,256,128]{2,1,0:T(8,128)(2,1)S(1)} collective-permute-done((bf16[2,256,128]{2,1,0:T(8,128)(2,1)S(1)}, bf16[2,256,128]{2,1,0:T(8,128)(2,1)S(1)}, u32[]{:S(2)}, u32[]{:S(2)}) %collective-permute-start.12) | collective-permute-done | bytes 131104 | tf_op jit(solution)/shard_map/ppermute | solution.py:259
  87.6 64.7 %shard_map.103.own_ref = bf16[8,1024,128]{2,1,0:T(8,128)(2,1)} custom-call(bf16[1024,2048]{1,0:T(8,128)(2,1)} %bitcast.43), custom_call_target="tpu_custom_call" | custom-call | tf_op jit(solution)/shard_map/pallas_call | solution.py:79
  154.3 1.6 copy-done
  155.9 2.0 shard_map.105
  161.7 1.6 collective-permute-start.24
  163.9 6.2 %collective-permute-done.24 = f32[128,128]{1,0:T(8,128)S(1)} collective-permute-done((f32[128,128]{1,0:T(8,128)S(1)}, f32[128,128]{1,0:T(8,128)S(1)}, u32[]{:S(2)}, u32[]{:S(2)}) %collective-permute-start.24) | collective-permute-done | bytes 65568 | tf_op jit(solution)/shard_map/ppermute | solution.py:298
  170.3 3.4 %collective-permute-done.25 = f32[128,128]{1,0:T(8,128)S(1)} collective-permute-done((f32[128,128]{1,0:T(8,128)S(1)}, f32[128,128]{1,0:T(8,128)S(1)}, u32[]{:S(2)}, u32[]{:S(2)}) %collective-permute-start.25) | collective-permute-done | bytes 65568 | tf_op jit(solution)/shard_map/ppermute | solution.py:298
  173.6 4.5 %collective-permute-start.18 = (bf16[4,2,256,128]{3,2,1,0:T(8,128)(2,1)S(1)}, bf16[4,2,256,128]{3,2,1,0:T(8,128)(2,1)S(1)}, u32[]{:S(2)}, u32[]{:S(2)}) collective-permute-start(bf16[4,2,256,128]{3,2,1,0:T(8,128)(2,1)S(1)} %pad_maximum_fusion.refs_0_), channel_id=1, source_target_pairs={{0,1},{1,0},{2,3},{3,2},{4,5},{5,4},{6,7},{7,6},{8,9},{9,8},{10,11... | collective-permute-start | bytes 1572872 | tf_op jit(solution)/shard_map/ppermute | solution.py:266
  178.7 2.8 %collective-permute-start.26 = (f32[128,128]{1,0:T(8,128)S(1)}, f32[128,128]{1,0:T(8,128)S(1)}, u32[]{:S(2)}, u32[]{:S(2)}) collective-permute-start(f32[128,128]{1,0:T(8,128)S(1)} %add.55), channel_id=1, source_target_pairs={{64,128},{128,64},{192,0},{0,192},{65,129},{129,65},{193,1},{1,193... | collective-permute-start | bytes 196616 | tf_op jit(solution)/shard_map/ppermute | solution.py:298
  181.5 3.4 %collective-permute-start.8 = (bf16[512,128]{1,0:T(8,128)(2,1)S(1)}, bf16[512,128]{1,0:T(8,128)(2,1)S(1)}, u32[]{:S(2)}, u32[]{:S(2)}) collective-permute-start(bf16[512,128]{1,0:T(8,128)(2,1)S(1)} %get-tuple-element.25), channel_id=1, source_target_pairs={{0,12},{4,0},{8,4},{12,8},{1,13},{5,1},{9,5},{13,9},{2,14},{6,2},{... | collective-permute-start | bytes 393224 | tf_op jit(solution)/shard_map/ppermute | solution.py:281
  185.1 3.9 %collective-permute-done.26 = f32[128,128]{1,0:T(8,128)S(1)} collective-permute-done((f32[128,128]{1,0:T(8,128)S(1)}, f32[128,128]{1,0:T(8,128)S(1)}, u32[]{:S(2)}, u32[]{:S(2)}) %collective-permute-start.26) | collective-permute-done | bytes 65568 | tf_op jit(solution)/shard_map/ppermute | solution.py:298
  190.5 1.6 collective-permute-done.27
  192.2 1.6 collective-permute-start.7
  193.8 1.6 collective-permute-start.28
  195.4 2.5 %collective-permute-done.28 = f32[128,128]{1,0:T(8,128)S(1)} collective-permute-done((f32[128,128]{1,0:T(8,128)S(1)}, f32[128,128]{1,0:T(8,128)S(1)}, u32[]{:S(2)}, u32[]{:S(2)}) %collective-permute-start.28) | collective-permute-done | bytes 65568 | tf_op jit(solution)/shard_map/ppermute | solution.py:298
  198.0 3.5 %collective-permute-start.20 = (bf16[4,2,256,128]{3,2,1,0:T(8,128)(2,1)}, bf16[4,2,256,128]{3,2,1,0:T(8,128)(2,1)S(1)}, u32[]{:S(2)}, u32[]{:S(2)}) collective-permute-start(bf16[4,2,256,128]{3,2,1,0:T(8,128)(2,1)} %collective-permute-done.15.refs_2_), channel_id=1, source_target_pairs={{0,1},{1,0},{2,3},{3,2},{4,5},{5,4},{6,7},{7,6},{8,9},{9,8},{10,11... | collective-permute-start | bytes 1572872 | tf_op jit(solution)/shard_map/ppermute | solution.py:266
  203.0 4.3 %collective-permute-start.29 = (f32[128,128]{1,0:T(8,128)S(1)}, f32[128,128]{1,0:T(8,128)S(1)}, u32[]{:S(2)}, u32[]{:S(2)}) collective-permute-start(f32[128,128]{1,0:T(8,128)S(1)} %add.58), channel_id=1, source_target_pairs={{0,50},{2,48},{16,34},{18,32},{32,18},{34,16},{48,2},{50,0},{1,51}... | collective-permute-start | bytes 196616 | tf_op jit(solution)/shard_map/ppermute | solution.py:298
  209.2 4.6 %collective-permute-start.9 = (bf16[1024,128]{1,0:T(8,128)(2,1)S(1)}, bf16[1024,128]{1,0:T(8,128)(2,1)S(1)}, u32[]{:S(2)}, u32[]{:S(2)}) collective-permute-start(bf16[1024,128]{1,0:T(8,128)(2,1)S(1)} %fusion.1), channel_id=1, source_target_pairs={{0,2},{2,0},{1,3},{3,1},{4,6},{6,4},{5,7},{7,5},{8,10},{10,8},{9,1... | collective-permute-start | bytes 786440 | tf_op jit(solution)/shard_map/ppermute | solution.py:287
  214.2 1.8 collective-permute-start.30
  216.9 9.7 %shard_map.107 = (f32[1024,128]{1,0:T(8,128)}, bf16[1024,2048]{1,0:T(8,128)(2,1)}) custom-call(bf16[4,2,256,128]{3,2,1,0:T(8,128)(2,1)S(1)} %pad_maximum_fusion.refs_0_, bf16[4,2,256,128]{3,2,1,0:T(8,128)(2,1)} %collective-permute-done.14.refs_1_, bf16[4,2,256,128]{3,2,1,0:T(8,128)(2,1)} %collective-permute-done.15.refs_2_, ...), custom_call_target="tpu_custom_call" | custom-call | tf_op jit(solution)/shard_map/pallas_call | solution.py:223
  226.6 2.0 shard_map.106
  (82 shorter events, 23.7 us)
Async XLA Ops:
  65.4 88.9 %collective-permute-start = (bf16[8,1024,128]{2,1,0:T(8,128)(2,1)}, bf16[8,1024,128]{2,1,0:T(8,128)(2,1)S(1)}, u32[]{:S(2)}, u32[]{:S(2)}) collective-permute-start(bf16[8,1024,128]{2,1,0:T(8,128)(2,1)} %shard_map.104), channel_id=1, source_target_pairs={{0,1},{1,0},{2,3},{3,2},{4,5},{5,4},{6,7},{7,6},{8,9},{9,8},{10,11... | collective-permute-start | bytes 6291464 | tf_op jit(solution)/shard_map/ppermute | solution.py:250
  67.0 8.1 %collective-permute-start.10 = (bf16[256,128]{1,0:T(8,128)(2,1)S(1)}, bf16[256,128]{1,0:T(8,128)(2,1)S(1)}, u32[]{:S(2)}, u32[]{:S(2)}) collective-permute-start(bf16[256,128]{1,0:T(8,128)(2,1)S(1)} %dynamic-slice_convert_fusion), channel_id=1, source_target_pairs={{0,50},{2,48},{16,34},{18,32},{32,18},{34,16},{48,2},{50,0},{1,51}... | collective-permute-start | bytes 196616 | tf_op jit(solution)/shard_map/ppermute | solution.py:255
  76.4 8.2 %collective-permute-start.12 = (bf16[2,256,128]{2,1,0:T(8,128)(2,1)S(1)}, bf16[2,256,128]{2,1,0:T(8,128)(2,1)S(1)}, u32[]{:S(2)}, u32[]{:S(2)}) collective-permute-start(bf16[2,256,128]{2,1,0:T(8,128)(2,1)S(1)} %get-tuple-element.28), channel_id=1, source_target_pairs={{0,8},{4,12},{8,0},{12,4},{1,9},{5,13},{9,1},{13,5},{2,10},{6,14},... | collective-permute-start | bytes 393224 | tf_op jit(solution)/shard_map/ppermute | solution.py:259
  84.7 67.6 %collective-permute-start.14 = (bf16[4,2,256,128]{3,2,1,0:T(8,128)(2,1)S(1)}, bf16[4,2,256,128]{3,2,1,0:T(8,128)(2,1)}, u32[]{:S(2)}, u32[]{:S(2)}) collective-permute-start(bf16[4,2,256,128]{3,2,1,0:T(8,128)(2,1)S(1)} %pad_maximum_fusion.refs_0_), channel_id=1, source_target_pairs={{0,64},{64,128},{128,192},{192,0},{1,65},{65,129},{129,193},{193,1... | collective-permute-start | bytes 1572872 | tf_op jit(solution)/shard_map/ppermute | solution.py:261
  86.0 67.2 %collective-permute-start.15 = (bf16[4,2,256,128]{3,2,1,0:T(8,128)(2,1)S(1)}, bf16[4,2,256,128]{3,2,1,0:T(8,128)(2,1)}, u32[]{:S(2)}, u32[]{:S(2)}) collective-permute-start(bf16[4,2,256,128]{3,2,1,0:T(8,128)(2,1)S(1)} %pad_maximum_fusion.refs_0_), channel_id=1, source_target_pairs={{0,192},{64,0},{128,64},{192,128},{1,193},{65,1},{129,65},{193,129... | collective-permute-start | bytes 1572872 | tf_op jit(solution)/shard_map/ppermute | solution.py:262
  159.1 19.0 %collective-permute-start.1 = (bf16[2,512,128]{2,1,0:T(8,128)(2,1)S(1)}, bf16[2,512,128]{2,1,0:T(8,128)(2,1)S(1)}, u32[]{:S(2)}, u32[]{:S(2)}) collective-permute-start(bf16[2,512,128]{2,1,0:T(8,128)(2,1)S(1)} %get-tuple-element.20), channel_id=1, source_target_pairs={{0,12},{4,0},{8,4},{12,8},{1,13},{5,1},{9,5},{13,9},{2,14},{6,2},{... | collective-permute-start | bytes 786440 | tf_op jit(solution)/shard_map/ppermute | solution.py:279
  160.2 18.2 %collective-permute-start.5 = (bf16[2,512,128]{2,1,0:T(8,128)(2,1)S(1)}, bf16[2,512,128]{2,1,0:T(8,128)(2,1)S(1)}, u32[]{:S(2)}, u32[]{:S(2)}) collective-permute-start(bf16[2,512,128]{2,1,0:T(8,128)(2,1)S(1)} %get-tuple-element.19), channel_id=1, source_target_pairs={{0,12},{4,0},{8,4},{12,8},{1,13},{5,1},{9,5},{13,9},{2,14},{6,2},{... | collective-permute-start | bytes 786440 | tf_op jit(solution)/shard_map/ppermute | solution.py:279
  161.7 8.4 %collective-permute-start.24 = (f32[128,128]{1,0:T(8,128)S(1)}, f32[128,128]{1,0:T(8,128)S(1)}, u32[]{:S(2)}, u32[]{:S(2)}) collective-permute-start(f32[128,128]{1,0:T(8,128)S(1)} %add.53), channel_id=1, source_target_pairs={{4,8},{8,4},{12,0},{0,12},{5,9},{9,5},{13,1},{1,13},{6,10},{10,6},... | collective-permute-start | bytes 196616 | tf_op jit(solution)/shard_map/ppermute | solution.py:298
  163.3 15.4 %collective-permute-start.2 = (bf16[2,512,128]{2,1,0:T(8,128)(2,1)S(1)}, bf16[2,512,128]{2,1,0:T(8,128)(2,1)S(1)}, u32[]{:S(2)}, u32[]{:S(2)}) collective-permute-start(bf16[2,512,128]{2,1,0:T(8,128)(2,1)S(1)} %get-tuple-element.22), channel_id=1, source_target_pairs={{0,4},{4,8},{8,12},{12,0},{1,5},{5,9},{9,13},{13,1},{2,6},{6,10},{... | collective-permute-start | bytes 786440 | tf_op jit(solution)/shard_map/ppermute | solution.py:278
  163.4 18.1 %collective-permute-start.6 = (bf16[2,512,128]{2,1,0:T(8,128)(2,1)S(1)}, bf16[2,512,128]{2,1,0:T(8,128)(2,1)S(1)}, u32[]{:S(2)}, u32[]{:S(2)}) collective-permute-start(bf16[2,512,128]{2,1,0:T(8,128)(2,1)S(1)} %get-tuple-element.21), channel_id=1, source_target_pairs={{0,4},{4,8},{8,12},{12,0},{1,5},{5,9},{9,13},{13,1},{2,6},{6,10},{... | collective-permute-start | bytes 786440 | tf_op jit(solution)/shard_map/ppermute | solution.py:278
  173.6 20.1 %collective-permute-start.18 = (bf16[4,2,256,128]{3,2,1,0:T(8,128)(2,1)S(1)}, bf16[4,2,256,128]{3,2,1,0:T(8,128)(2,1)S(1)}, u32[]{:S(2)}, u32[]{:S(2)}) collective-permute-start(bf16[4,2,256,128]{3,2,1,0:T(8,128)(2,1)S(1)} %pad_maximum_fusion.refs_0_), channel_id=1, source_target_pairs={{0,1},{1,0},{2,3},{3,2},{4,5},{5,4},{6,7},{7,6},{8,9},{9,8},{10,11... | collective-permute-start | bytes 1572872 | tf_op jit(solution)/shard_map/ppermute | solution.py:266
  178.1 19.9 %collective-permute-start.16 = (bf16[2,2,256,128]{3,2,1,0:T(8,128)(2,1)S(1)}, bf16[2,2,256,128]{3,2,1,0:T(8,128)(2,1)S(1)}, u32[]{:S(2)}, u32[]{:S(2)}) collective-permute-start(bf16[2,2,256,128]{3,2,1,0:T(8,128)(2,1)S(1)} %slice.88), channel_id=1, source_target_pairs={{0,64},{64,128},{128,192},{192,0},{1,65},{65,129},{129,193},{193,1... | collective-permute-start | bytes 786440 | tf_op jit(solution)/shard_map/ppermute | solution.py:263
  178.4 29.7 %collective-permute-start.19 = (bf16[4,2,256,128]{3,2,1,0:T(8,128)(2,1)}, bf16[4,2,256,128]{3,2,1,0:T(8,128)(2,1)S(1)}, u32[]{:S(2)}, u32[]{:S(2)}) collective-permute-start(bf16[4,2,256,128]{3,2,1,0:T(8,128)(2,1)} %collective-permute-done.14.refs_1_), channel_id=1, source_target_pairs={{0,1},{1,0},{2,3},{3,2},{4,5},{5,4},{6,7},{7,6},{8,9},{9,8},{10,11... | collective-permute-start | bytes 1572872 | tf_op jit(solution)/shard_map/ppermute | solution.py:266
  178.7 10.2 %collective-permute-start.26 = (f32[128,128]{1,0:T(8,128)S(1)}, f32[128,128]{1,0:T(8,128)S(1)}, u32[]{:S(2)}, u32[]{:S(2)}) collective-permute-start(f32[128,128]{1,0:T(8,128)S(1)} %add.55), channel_id=1, source_target_pairs={{64,128},{128,64},{192,0},{0,192},{65,129},{129,65},{193,1},{1,193... | collective-permute-start | bytes 196616 | tf_op jit(solution)/shard_map/ppermute | solution.py:298
  181.5 19.9 %collective-permute-start.8 = (bf16[512,128]{1,0:T(8,128)(2,1)S(1)}, bf16[512,128]{1,0:T(8,128)(2,1)S(1)}, u32[]{:S(2)}, u32[]{:S(2)}) collective-permute-start(bf16[512,128]{1,0:T(8,128)(2,1)S(1)} %get-tuple-element.25), channel_id=1, source_target_pairs={{0,12},{4,0},{8,4},{12,8},{1,13},{5,1},{9,5},{13,9},{2,14},{6,2},{... | collective-permute-start | bytes 393224 | tf_op jit(solution)/shard_map/ppermute | solution.py:281
  192.2 10.8 %collective-permute-start.7 = (bf16[512,128]{1,0:T(8,128)(2,1)S(1)}, bf16[512,128]{1,0:T(8,128)(2,1)S(1)}, u32[]{:S(2)}, u32[]{:S(2)}) collective-permute-start(bf16[512,128]{1,0:T(8,128)(2,1)S(1)} %get-tuple-element.23), channel_id=1, source_target_pairs={{0,4},{4,8},{8,12},{12,0},{1,5},{5,9},{9,13},{13,1},{2,6},{6,10},{... | collective-permute-start | bytes 393224 | tf_op jit(solution)/shard_map/ppermute | solution.py:280
  198.0 9.5 %collective-permute-start.17 = (bf16[2,2,256,128]{3,2,1,0:T(8,128)(2,1)S(1)}, bf16[2,2,256,128]{3,2,1,0:T(8,128)(2,1)S(1)}, u32[]{:S(2)}, u32[]{:S(2)}) collective-permute-start(bf16[2,2,256,128]{3,2,1,0:T(8,128)(2,1)S(1)} %slice.89), channel_id=1, source_target_pairs={{0,192},{64,0},{128,64},{192,128},{1,193},{65,1},{129,65},{193,129... | collective-permute-start | bytes 786440 | tf_op jit(solution)/shard_map/ppermute | solution.py:264
  198.0 18.0 %collective-permute-start.20 = (bf16[4,2,256,128]{3,2,1,0:T(8,128)(2,1)}, bf16[4,2,256,128]{3,2,1,0:T(8,128)(2,1)S(1)}, u32[]{:S(2)}, u32[]{:S(2)}) collective-permute-start(bf16[4,2,256,128]{3,2,1,0:T(8,128)(2,1)} %collective-permute-done.15.refs_2_), channel_id=1, source_target_pairs={{0,1},{1,0},{2,3},{3,2},{4,5},{5,4},{6,7},{7,6},{8,9},{9,8},{10,11... | collective-permute-start | bytes 1572872 | tf_op jit(solution)/shard_map/ppermute | solution.py:266
  201.5 6.8 %collective-permute-start.4 = (bf16[512,128]{1,0:T(8,128)(2,1)S(1)}, bf16[512,128]{1,0:T(8,128)(2,1)S(1)}, u32[]{:S(2)}, u32[]{:S(2)}) collective-permute-start(bf16[512,128]{1,0:T(8,128)(2,1)S(1)} %get-tuple-element.26), channel_id=1, source_target_pairs={{0,12},{4,0},{8,4},{12,8},{1,13},{5,1},{9,5},{13,9},{2,14},{6,2},{... | collective-permute-start | bytes 393224 | tf_op jit(solution)/shard_map/ppermute | solution.py:281
  203.0 6.2 %collective-permute-start.29 = (f32[128,128]{1,0:T(8,128)S(1)}, f32[128,128]{1,0:T(8,128)S(1)}, u32[]{:S(2)}, u32[]{:S(2)}) collective-permute-start(f32[128,128]{1,0:T(8,128)S(1)} %add.58), channel_id=1, source_target_pairs={{0,50},{2,48},{16,34},{18,32},{32,18},{34,16},{48,2},{50,0},{1,51}... | collective-permute-start | bytes 196616 | tf_op jit(solution)/shard_map/ppermute | solution.py:298
  207.4 8.6 %collective-permute-start.21 = (bf16[2,2,256,128]{3,2,1,0:T(8,128)(2,1)S(1)}, bf16[2,2,256,128]{3,2,1,0:T(8,128)(2,1)S(1)}, u32[]{:S(2)}, u32[]{:S(2)}) collective-permute-start(bf16[2,2,256,128]{3,2,1,0:T(8,128)(2,1)S(1)} %collective-permute-done.16.refs_3_), channel_id=1, source_target_pairs={{0,1},{1,0},{2,3},{3,2},{4,5},{5,4},{6,7},{7,6},{8,9},{9,8},{10,11... | collective-permute-start | bytes 786440 | tf_op jit(solution)/shard_map/ppermute | solution.py:266
  208.2 7.9 %collective-permute-start.22 = (bf16[2,2,256,128]{3,2,1,0:T(8,128)(2,1)S(1)}, bf16[2,2,256,128]{3,2,1,0:T(8,128)(2,1)S(1)}, u32[]{:S(2)}, u32[]{:S(2)}) collective-permute-start(bf16[2,2,256,128]{3,2,1,0:T(8,128)(2,1)S(1)} %collective-permute-done.17.refs_4_), channel_id=1, source_target_pairs={{0,1},{1,0},{2,3},{3,2},{4,5},{5,4},{6,7},{7,6},{8,9},{9,8},{10,11... | collective-permute-start | bytes 786440 | tf_op jit(solution)/shard_map/ppermute | solution.py:266
  208.3 5.9 %collective-permute-start.3 = (bf16[512,128]{1,0:T(8,128)(2,1)S(1)}, bf16[512,128]{1,0:T(8,128)(2,1)S(1)}, u32[]{:S(2)}, u32[]{:S(2)}) collective-permute-start(bf16[512,128]{1,0:T(8,128)(2,1)S(1)} %get-tuple-element.24), channel_id=1, source_target_pairs={{0,4},{4,8},{8,12},{12,0},{1,5},{5,9},{9,13},{13,1},{2,6},{6,10},{... | collective-permute-start | bytes 393224 | tf_op jit(solution)/shard_map/ppermute | solution.py:280
  209.2 17.4 %collective-permute-start.9 = (bf16[1024,128]{1,0:T(8,128)(2,1)S(1)}, bf16[1024,128]{1,0:T(8,128)(2,1)S(1)}, u32[]{:S(2)}, u32[]{:S(2)}) collective-permute-start(bf16[1024,128]{1,0:T(8,128)(2,1)S(1)} %fusion.1), channel_id=1, source_target_pairs={{0,2},{2,0},{1,3},{3,1},{4,6},{6,4},{5,7},{7,5},{8,10},{10,8},{9,1... | collective-permute-start | bytes 786440 | tf_op jit(solution)/shard_map/ppermute | solution.py:287
  (14 other events, 313.6 us)

commit v2 on v1

v2 whole, which is shorter than its diff:
```python
import functools

import jax
import jax.numpy as jnp
import numpy as np
from jax import lax
from jax.experimental import pallas as pl
from jax.experimental.pallas import tpu as pltpu
from jax.sharding import Mesh
from jax.sharding import PartitionSpec as P

GROUP = 128
BAND = 16
ROWS = 1024
HALF = 512
QUARTER = 256

momentum_decay = 0.9
step_size = 0.05
replicas = 16

bf16 = jnp.bfloat16
f32 = jnp.float32
HIGHEST = lax.Precision.HIGHEST

SWAP2 = [(0, 1), (1, 0)]
UP4 = [(i, (i + 1) % 4) for i in range(4)]
DOWN4 = [(i, (i + 3) % 4) for i in range(4)]
ACROSS4 = [(i, (i + 2) % 4) for i in range(4)]
EVEN4 = [(0, 1), (1, 0), (2, 3), (3, 2)]
ODD4 = [(1, 2), (2, 1), (3, 0), (0, 3)]
XOR2 = [(i, i ^ 2) for i in range(4)]
CROSS8 = [(i, i ^ 5) for i in range(8)]
SPREAD8 = [(i, (i + 2) % 8) if i % 2 == 0 else (i, (i + 6) % 8) for i in range(8)]


def cosine_rows():
    freq = np.arange(BAND, dtype=np.float64)[:, None]
    place = np.arange(GROUP, dtype=np.float64)[None, :]
    factor = np.where(freq == 0.0, np.sqrt(1.0 / GROUP), np.sqrt(2.0 / GROUP))
    return factor * np.cos(np.pi * (2.0 * place + 1.0) * freq / (2.0 * GROUP))


def column_of(dx, gz, core):
    bx = lax.rem(lax.axis_index("x") + dx, 4)
    zh = lax.axis_index("zh")
    bz = zh if gz == 0 else 1 - zh
    return bx * 4 + bz * 2 + core


def slot_of(dx, gz):
    bx = lax.rem(lax.axis_index("x") + dx, 4)
    zh = lax.axis_index("zh")
    return bx * 2 + (zh if gz == 0 else 1 - zh)


def lanes(index):
    return pl.ds(pl.multiple_of(index * GROUP, GROUP), GROUP)


def split_kernel(g_ref, sent_ref, own_ref, page_ref, sem):
    core = lax.axis_index("core")
    copies = []
    for a in range(8):
        rows = slice(a * GROUP, (a + 1) * GROUP)
        copies.append(pltpu.make_async_copy(g_ref.at[rows, :], page_ref.at[rows, :], sem.at[a]))
    for c in copies:
        c.start()
    for a in range(8):
        rows = slice(a * GROUP, (a + 1) * GROUP)
        copies[a].wait()
        for gz in range(2):
            for dx in range(4):
                k = gz * 4 + dx
                sent_ref[k, rows] = page_ref[rows, lanes(column_of(dx, gz, 1 - core))]
                own_ref[k, rows] = page_ref[rows, lanes(column_of(dx, gz, core))]


def split_blocks(g):
    blocks = jax.ShapeDtypeStruct((8, ROWS, GROUP), bf16)
    return pl.pallas_call(
        split_kernel,
        out_shape=[blocks, blocks],
        in_specs=[pl.BlockSpec(memory_space=pltpu.HBM)],
        out_specs=[pl.BlockSpec(memory_space=pltpu.VMEM)] * 2,
        scratch_shapes=[pltpu.VMEM((ROWS, 16 * GROUP), bf16), pltpu.SemaphoreType.DMA((8,))],
        compiler_params=pltpu.CompilerParams(vmem_limit_bytes=12 * 2**20),
    )(g)


def pair_sum_kernel(
    own_ref, other_ref, mom_ref, table_ref, rows_ref, up_ref, down_ref, keep_up_ref, keep_down_ref,
    mine_ref, band_ref, acc_ref,
):
    lane_slot = lax.broadcasted_iota(jnp.int32, (GROUP, GROUP), 1) // BAND
    table = table_ref[...]
    zero = jnp.zeros_like(table)
    for gz in range(2):
        for dx in range(4):
            k = gz * 4 + dx
            s = (own_ref[k].astype(f32) + other_ref[k].astype(f32)).astype(bf16)
            if dx == 0:
                mine_ref[gz] = s
            elif dx == 1:
                keep_up_ref[gz] = s[:HALF]
                up_ref[gz, 1] = s[HALF:]
            elif dx == 2:
                up_ref[gz, 0] = s[:HALF]
                down_ref[gz, 0] = s[HALF:]
            else:
                down_ref[gz, 1] = s[:HALF]
                keep_down_ref[gz] = s[HALF:]
            placed = jnp.where(lane_slot == slot_of(dx, gz), table, zero)
            part = jnp.dot(s, placed.astype(bf16), preferred_element_type=f32)
            if k == 0:
                acc_ref[...] = part + jnp.dot(
                    momentum_decay * mom_ref[...], placed, preferred_element_type=f32
                )
            else:
                acc_ref[...] += part
    for a in range(ROWS // GROUP):
        band_ref[a * BAND : (a + 1) * BAND, :] = jnp.dot(
            rows_ref[...],
            acc_ref[a * GROUP : (a + 1) * GROUP, :],
            precision=HIGHEST,
            preferred_element_type=f32,
        )


def pair_sum(own, other, mom, table, rows):
    shapes = [(2, 2, HALF, GROUP)] * 2 + [(2, HALF, GROUP)] * 2 + [(2, ROWS, GROUP)]
    shapes = [jax.ShapeDtypeStruct(shape, bf16) for shape in shapes]
    shapes.append(jax.ShapeDtypeStruct((ROWS // GROUP * BAND, GROUP), f32))
    vmem = pl.BlockSpec(memory_space=pltpu.VMEM)
    return pl.pallas_call(
        pair_sum_kernel,
        out_shape=shapes,
        in_specs=[vmem] * 5,
        out_specs=[vmem] * 6,
        scratch_shapes=[pltpu.VMEM((ROWS, GROUP), f32)],
        compiler_params=pltpu.CompilerParams(vmem_limit_bytes=16 * 2**20),
    )(own, other, mom, table, rows)


def small_call(kernel, shapes, *args):
    vmem = pl.BlockSpec(memory_space=pltpu.VMEM)
    return pl.pallas_call(
        kernel,
        out_shape=shapes,
        in_specs=[vmem] * len(args),
        out_specs=jax.tree.map(lambda _: vmem, shapes),
        compiler_params=pltpu.CompilerParams(vmem_limit_bytes=8 * 2**20),
    )(*args)


def join_kernel(first_ref, second_ref, out_ref):
    half = first_ref.shape[0]
    out_ref[:half] = first_ref[...]
    out_ref[half:] = second_ref[...]


def joined(first, second):
    shape = (2 * first.shape[0], *first.shape[1:])
    return small_call(join_kernel, jax.ShapeDtypeStruct(shape, first.dtype), first, second)


def cast_kernel(master_ref, out_ref):
    y = lax.axis_index("y")
    out_ref[0] = master_ref[pl.ds(pl.multiple_of(y * QUARTER, QUARTER), QUARTER), :].astype(bf16)


def pass_on_kernel(keep_up_ref, keep_down_ref, left_ref, right_ref, up_ref, down_ref):
    for gz in range(2):
        up_ref[gz] = (keep_up_ref[gz].astype(f32) + left_ref[gz, 0].astype(f32)).astype(bf16)
        down_ref[gz] = (keep_down_ref[gz].astype(f32) + right_ref[gz, 0].astype(f32)).astype(bf16)


def x_total(mine_ref, left_ref, right_ref, last_left_ref, last_right_ref, gz, a):
    r = slice(a * GROUP, (a + 1) * GROUP)
    h = slice(a % 4 * GROUP, (a % 4 + 1) * GROUP)
    direct, passed = (right_ref, last_left_ref) if a < 4 else (left_ref, last_right_ref)
    total = mine_ref[gz, r].astype(f32) + direct[gz, 1, h].astype(f32)
    return total + passed[gz, h].astype(f32)


def z_send_kernel(*refs):
    for a in range(ROWS // GROUP):
        refs[5][a * GROUP : (a + 1) * GROUP] = x_total(*refs[:5], 1, a).astype(bf16)


def remaining_kernel(*refs):
    z_ref, mom_ref, q_ref, out_ref = refs[5:]
    q = q_ref[...]
    for a in range(ROWS // GROUP):
        r = slice(a * GROUP, (a + 1) * GROUP)
        summed = x_total(*refs[:5], 0, a) + z_ref[r].astype(f32)
        moment = momentum_decay * mom_ref[r] + summed
        low = jnp.dot(moment, q, precision=HIGHEST, preferred_element_type=f32)
        low = jnp.dot(q, low, precision=HIGHEST, preferred_element_type=f32)
        out_ref[r] = moment - low


def gathered_x(j):
    x = lax.axis_index("x")
    if j >= 2:
        x = lax.rem(x + 3 - 2 * lax.rem(x, 2), 4)
        x = lax.rem(x + 4, 4)
    return x if j % 2 == 0 else x + 1 - 2 * lax.rem(x, 2)


def weights_kernel(*refs):
    quarter_ref, near_ref, near_other_ref, far_ref, far_other_ref = refs[0:5]
    band_refs = refs[5:7]
    master_ref, cols_ref, table_ref = refs[7:10]
    master_out, full_out = refs[10:12]
    spread_ref, page_ref, sem = refs[12:15]
    core = lax.axis_index("core")
    y = lax.axis_index("y")
    zh = lax.axis_index("zh")

    coeffs = jnp.concatenate([band_refs[0][...], band_refs[1][...]], axis=1)
    spread_ref[...] = jnp.dot(
        cols_ref[...], coeffs.astype(bf16), preferred_element_type=f32
    ).astype(bf16)

    row_slot = lax.broadcasted_iota(jnp.int32, (GROUP, GROUP), 0) // BAND
    table = table_ref[...]
    zero = jnp.zeros_like(table)
    places = []
    for j in range(4):
        for gz in range(2):
            bx, bz = gathered_x(j), (zh if gz == 0 else 1 - zh)
            slot = bx * 2 + bz
            places.append((j, gz, bx * 4 + bz * 2))
            wide_part = jnp.where(row_slot == slot, table, zero).astype(bf16)
            wide = wide_part if j + gz == 0 else jnp.concatenate([wide, wide_part], axis=1)

    copies = []
    for step, dy in enumerate((0, 3 - 2 * core, 1 + 2 * core, 2)):
        quarter = lax.rem(y + dy, 4)
        rows = pl.ds(pl.multiple_of(quarter * QUARTER, QUARTER), QUARTER)
        for who in range(2):
            side = core if who == 0 else 1 - core
            update = jnp.dot(
                spread_ref[rows, who * GROUP : (who + 1) * GROUP],
                wide,
                preferred_element_type=f32,
            )
            for j, gz, column in places:
                k = j * 2 + gz
                if step == 0:
                    prior = quarter_ref[who * 8 + k]
                elif step == 1:
                    prior = near_ref[who * 8 + k]
                elif step == 2:
                    prior = near_other_ref[(1 - who) * 8 + k]
                else:
                    prior = far_ref[k] if who == 0 else far_other_ref[k]
                part = update[:, k * GROUP : (k + 1) * GROUP]
                page_ref[step, :, lanes(column + side)] = (prior.astype(f32) + part).astype(bf16)
                if who == 0 and k == 0:
                    master_out[rows, :] = master_ref[rows, :] + part
        copy = pltpu.make_async_copy(page_ref.at[step], full_out.at[rows, :], sem.at[step])
        copy.start()
        copies.append(copy)
    for copy in copies:
        copy.wait()


def weights_of(pieces, bands, master, cols, table):
    vmem = pl.BlockSpec(memory_space=pltpu.VMEM)
    return pl.pallas_call(
        weights_kernel,
        out_shape=[
            jax.ShapeDtypeStruct((ROWS, GROUP), f32),
            jax.ShapeDtypeStruct((ROWS, 16 * GROUP), bf16),
        ],
        in_specs=[vmem] * 10,
        out_specs=[vmem, pl.BlockSpec(memory_space=pl.ANY)],
        scratch_shapes=[
            pltpu.VMEM((ROWS, 2 * GROUP), bf16),
            pltpu.VMEM((4, QUARTER, 16 * GROUP), bf16),
            pltpu.SemaphoreType.DMA((4,)),
        ],
        compiler_params=pltpu.CompilerParams(vmem_limit_bytes=20 * 2**20),
    )(*pieces, *bands, master, cols, table)


def send(array, axis, perm):
    return lax.ppermute(array, axis, perm)


together = lax.optimization_barrier


def local(gradients, momentum, master_weights):
    table = cosine_rows()
    mom = momentum[0]
    half = (ROWS, GROUP)
    z = ("zl", "zh")

    sent, own = split_blocks(gradients[0, 0])
    other = send(sent, "core", SWAP2)
    w0 = small_call(
        cast_kernel, jax.ShapeDtypeStruct((1, QUARTER, GROUP), bf16), master_weights
    )
    wz = send(w0, z, CROSS8)
    up, down, keep_up, keep_down, mine, band = pair_sum(
        own,
        other,
        mom,
        jnp.asarray(np.tile(table.T, (1, 8)), f32),
        jnp.asarray(table, f32),
    )

    band, up, down, w0, wz = together((band, up, down, w0, wz))
    got = send(band, "y", EVEN4)
    left = send(up, "x", UP4)
    right = send(down, "x", DOWN4)
    w1 = joined(w0, wz)
    wx = send(w1, "x", EVEN4)

    band, w1, wx = together((band + got, w1, wx))
    got = send(band, "y", ODD4)
    w2 = joined(w1, wx)
    wx = send(w2, "x", ODD4)

    band, w2, wx = together((band + got, w2, wx))
    got = send(band, "zl", EVEN4)
    w4 = joined(w2, wx)
    wc = send(w4, "core", SWAP2)

    band, w4, wc, left, right = together((band + got, w4, wc, left, right))
    got = send(band, "zl", XOR2)
    quarter = joined(w4, wc)
    near = send(quarter, ("y", "core"), SPREAD8)
    passed = jax.ShapeDtypeStruct((2, HALF, GROUP), bf16)
    up, down = small_call(pass_on_kernel, [passed] * 2, keep_up, keep_down, left, right)
    last_left = send(up, "x", UP4)
    last_right = send(down, "x", DOWN4)

    band = band + got
    got = send(band, z, CROSS8)

    band, last_left, last_right = together((band + got, last_left, last_right))
    got = send(band, "x", EVEN4)
    parts = (mine, left, right, last_left, last_right)
    z_send = small_call(z_send_kernel, jax.ShapeDtypeStruct(half, bf16), *parts)
    from_z = send(z_send, "zh", SWAP2)

    band, near = together((band + got, near))
    got = send(band, "x", ODD4)
    far = send(near[:8], ("y", "core"), SPREAD8)
    near_other = send(near, "core", SWAP2)

    band, far = together(((band + got) * (-step_size / replicas), far))
    band_other = send(band, "core", SWAP2)
    far_other = send(far, "core", SWAP2)

    new_momentum = small_call(
        remaining_kernel,
        jax.ShapeDtypeStruct(half, f32),
        *parts,
        from_z,
        mom,
        jnp.asarray(table.T @ table, f32),
    )
    new_master, weights_full = weights_of(
        (quarter, near, near_other, far, far_other),
        (band, band_other),
        master_weights,
        jnp.asarray(np.kron(np.eye(8), table.T), bf16),
        jnp.asarray(np.tile(table, (8, 1)), f32),
    )
    return (new_momentum[None], new_master, weights_full)


def solution(mesh):
    fine = Mesh(mesh.devices.reshape(4, 4, 4, 2, 2), ("y", "zl", "x", "zh", "core"))
    rep, fsdp = ("y", "zl"), ("x", "zh", "core")
    return jax.shard_map(
        local,
        mesh=fine,
        in_specs=(P(rep, fsdp, None, None), P(rep, None, fsdp), P(None, fsdp)),
        out_specs=(P(rep, None, fsdp), P(None, fsdp), P()),
        check_vma=False,
    )
```

time: 231 us -> 97.1 us (0.42)
  Pallas kernels: 143 us -> 10.2 us
  waiting for transfers between devices: 25.9 us -> 41.4 us
  starting transfers between devices: 52.7 us -> 42.1 us
  local copies, waits for them, and re-layouts: 5.52 us -> 2.25 us
    pallas_call x4 -> x10, Pallas kernels: 133 us -> 5.81 us  [the longest x8 2.35 us: small_call(): pl.pallas_call(kernel, out_shape=shapes, in_specs=[vmem] * len(args), out...]
    ppermute x31 -> x22, waiting for transfers between devices: 25.9 us -> 41.4 us  [send(): return lax.ppermute(array, axis, perm)]
    ppermute x31 -> x22, starting transfers between devices: 52.7 us -> 42.1 us  [send(): return lax.ppermute(array, axis, perm)]
    pallas_call x1, Pallas kernels: 9.67 us -> 4.36 us  [weights_of(): pl.pallas_call(weights_kernel, out_shape=[jax.ShapeDtypeStruct((ROWS, GRO...]
  transfers between devices with their start and end apart: 31 -> 22, of which waited for: 11 -> 9; matrix products, arithmetic and copies ran while one was open for 2% -> 0% of each run, Pallas kernels for 33% -> 4%
where the time goes in v2:
time: 97.1 us; the launch traced here: 96.9 us
  starting transfers between devices  42.1 us (43%)
  waiting for transfers between devices  41.4 us (43%)
  Pallas kernels  10.2 us (11%)
  local copies, waits for them, and re-layouts  2.25 us (2%)
  between operations  1 us (1%)
    ppermute x22, starting transfers between devices, send(): return lax.ppermute(array, axis, perm)  42.1 us
    ppermute x22, waiting for transfers between devices, send(): return lax.ppermute(array, axis, perm)  41.4 us
    pallas_call x1, Pallas kernels, weights_of(): pl.pallas_call(weights_kernel, out_shape=[jax.ShapeDtypeStruct((ROWS, GRO...  4.36 us
    pallas_call x8, Pallas kernels, small_call(): pl.pallas_call(kernel, out_shape=shapes, in_specs=[vmem] * len(args), out...  2.35 us
    unnamed x16, local copies, waits for them, and re-layouts  2.21 us
    pallas_call x1, Pallas kernels, pair_sum(): pl.pallas_call(pair_sum_kernel, out_shape=shapes, in_specs=[vmem] * 5, ou...  2 us
  transfers between devices with their start and end apart: 22, of which 9 were waited for; matrix products, arithmetic and copies ran while one was open for 0% of the time, Pallas kernels for 4%

profile of v2, /device:TPU:33, one launch (start us, length us, event | category | flops | bytes accessed | tf_op | source)
XLA Modules:
  0.0 96.9 jit_solution(17892695553560268932)
XLA Ops:
  0.6 2.2 %copy-done = bf16[1,1,1024,2048]{3,2,1,0:T(8,128)(2,1)S(1)} copy-done((bf16[1,1,1024,2048]{3,2,1,0:T(8,128)(2,1)S(1)}, bf16[1,1,1024,2048]{3,2,1,0:T(8,128)(2,1)}, u32[]{:S(2)}) %copy-start) | copy-done | bytes 4194328
  5.1 5.2 %collective-permute-start.1 = (bf16[1,256,128]{2,1,0:T(8,128)(2,1)S(1)}, bf16[1,256,128]{2,1,0:T(8,128)(2,1)S(1)}, u32[]{:S(2)}, u32[]{:S(2)}) collective-permute-start(bf16[1,256,128]{2,1,0:T(8,128)(2,1)S(1)} %shard_map.105.first_ref), channel_id=1, source_target_pairs={{0,34},{2,32},{16,50},{18,48},{32,2},{34,0},{48,18},{50,16},{1,35}... | collective-permute-start | bytes 196616 | tf_op jit(solution)/shard_map/ppermute | solution.py:290
  10.3 2.0 %shard_map.104 = (bf16[2,2,512,128]{3,2,1,0:T(8,128)(2,1)S(1)}, bf16[2,2,512,128]{3,2,1,0:T(8,128)(2,1)S(1)}, bf16[2,512,128]{2,1,0:T(8,128)(2,1)S(1)}, bf16[2,5...) custom-call(bf16[8,1024,128]{2,1,0:T(8,128)(2,1)S(1)} %get-tuple-element.38.own_ref, ...), custom_call_target="tpu_custom_call" | custom-call | tf_op jit(solution)/shard_map/pallas_call | solution.py:135
  12.3 1.8 %collective-permute-done.1.second_ref = bf16[1,256,128]{2,1,0:T(8,128)(2,1)S(1)} collective-permute-done((bf16[1,256,128]{2,1,0:T(8,128)(2,1)S(1)}, bf16[1,256,128]{2,1,0:T(8,128)(2,1)S(1)}, u32[]{:S(2)}, u32[]{:S(2)}) %collective-permute-start.1) | collective-permute-done | bytes 65568 | tf_op jit(solution)/shard_map/ppermute | solution.py:290
  16.7 2.1 %collective-permute-done.2 = f32[128,128]{1,0:T(8,128)S(1)} collective-permute-done((f32[128,128]{1,0:T(8,128)S(1)}, f32[128,128]{1,0:T(8,128)S(1)}, u32[]{:S(2)}, u32[]{:S(2)}) %collective-permute-start.2) | collective-permute-done | bytes 65568 | tf_op jit(solution)/shard_map/ppermute | solution.py:290
  18.9 2.4 %collective-permute-start.5 = (bf16[4,256,128]{2,1,0:T(8,128)(2,1)S(1)}, bf16[4,256,128]{2,1,0:T(8,128)(2,1)S(1)}, u32[]{:S(2)}, u32[]{:S(2)}) collective-permute-start(bf16[4,256,128]{2,1,0:T(8,128)(2,1)S(1)} %shard_map.107.first_ref), channel_id=1, source_target_pairs={{4,8},{8,4},{12,0},{0,12},{5,9},{9,5},{13,1},{1,13},{6,10},{10,6},... | collective-permute-start | bytes 786440 | tf_op jit(solution)/shard_map/ppermute | solution.py:290
  21.3 2.7 %collective-permute-start.4 = (f32[128,128]{1,0:T(8,128)S(1)}, f32[128,128]{1,0:T(8,128)S(1)}, u32[]{:S(2)}, u32[]{:S(2)}) collective-permute-start(f32[128,128]{1,0:T(8,128)S(1)} %add.21), channel_id=1, source_target_pairs={{64,128},{128,64},{192,0},{0,192},{65,129},{129,65},{193,1},{1,193... | collective-permute-start | bytes 196616 | tf_op jit(solution)/shard_map/ppermute | solution.py:290
  24.0 2.7 %collective-permute-start.9 = (bf16[2,2,512,128]{3,2,1,0:T(8,128)(2,1)S(1)}, bf16[2,2,512,128]{3,2,1,0:T(8,128)(2,1)S(1)}, u32[]{:S(2)}, u32[]{:S(2)}) collective-permute-start(bf16[2,2,512,128]{3,2,1,0:T(8,128)(2,1)S(1)} %get-tuple-element.54), channel_id=1, source_target_pairs={{0,12},{4,0},{8,4},{12,8},{1,13},{5,1},{9,5},{13,9},{2,14},{6,2},{... | collective-permute-start | bytes 1572872 | tf_op jit(solution)/shard_map/ppermute | solution.py:290
  26.7 2.9 %collective-permute-start.7 = (bf16[8,256,128]{2,1,0:T(8,128)(2,1)S(1)}, bf16[8,256,128]{2,1,0:T(8,128)(2,1)S(1)}, u32[]{:S(2)}, u32[]{:S(2)}) collective-permute-start(bf16[8,256,128]{2,1,0:T(8,128)(2,1)S(1)} %shard_map.108.first_ref), channel_id=1, source_target_pairs={{0,1},{1,0},{2,3},{3,2},{4,5},{5,4},{6,7},{7,6},{8,9},{9,8},{10,11... | collective-permute-start | bytes 1572872 | tf_op jit(solution)/shard_map/ppermute | solution.py:290
  29.9 3.4 %collective-permute-done.6 = f32[128,128]{1,0:T(8,128)S(1)} collective-permute-done((f32[128,128]{1,0:T(8,128)S(1)}, f32[128,128]{1,0:T(8,128)S(1)}, u32[]{:S(2)}, u32[]{:S(2)}) %collective-permute-start.6) | collective-permute-done | bytes 65568 | tf_op jit(solution)/shard_map/ppermute | solution.py:290
  33.3 4.6 %collective-permute-done.8.left_ref.refs_1_ = bf16[2,2,512,128]{3,2,1,0:T(8,128)(2,1)S(1)} collective-permute-done((bf16[2,2,512,128]{3,2,1,0:T(8,128)(2,1)S(1)}, bf16[2,2,512,128]{3,2,1,0:T(8,128)(2,1)S(1)}, u32[]{:S(2)}, u32[]{:S(2)}) %collective-permute-start.8) | collective-permute-done | bytes 524320 | tf_op jit(solution)/shard_map/ppermute | solution.py:290
  37.9 2.5 %collective-permute-start.16 = (bf16[16,256,128]{2,1,0:T(8,128)(2,1)S(1)}, bf16[16,256,128]{2,1,0:T(8,128)(2,1)S(1)}, u32[]{:S(2)}, u32[]{:S(2)}) collective-permute-start(bf16[16,256,128]{2,1,0:T(8,128)(2,1)S(1)} %shard_map.112.refs_0_), channel_id=1, source_target_pairs={{0,64},{1,193},{64,128},{65,1},{128,192},{129,65},{192,0},{193,129... | collective-permute-start | bytes 3145736 | tf_op jit(solution)/shard_map/ppermute | solution.py:290
  40.6 2.6 %collective-permute-start.13 = (bf16[2,512,128]{2,1,0:T(8,128)(2,1)S(1)}, bf16[2,512,128]{2,1,0:T(8,128)(2,1)S(1)}, u32[]{:S(2)}, u32[]{:S(2)}) collective-permute-start(bf16[2,512,128]{2,1,0:T(8,128)(2,1)S(1)} %get-tuple-element.61), channel_id=1, source_target_pairs={{0,12},{4,0},{8,4},{12,8},{1,13},{5,1},{9,5},{13,9},{2,14},{6,2},{... | collective-permute-start | bytes 786440 | tf_op jit(solution)/shard_map/ppermute | solution.py:290
  43.3 4.3 %collective-permute-done.10 = f32[128,128]{1,0:T(8,128)S(1)} collective-permute-done((f32[128,128]{1,0:T(8,128)S(1)}, f32[128,128]{1,0:T(8,128)S(1)}, u32[]{:S(2)}, u32[]{:S(2)}) %collective-permute-start.10) | collective-permute-done | bytes 65568 | tf_op jit(solution)/shard_map/ppermute | solution.py:290
  47.6 2.1 %collective-permute-start.11 = (f32[128,128]{1,0:T(8,128)S(1)}, f32[128,128]{1,0:T(8,128)S(1)}, u32[]{:S(2)}, u32[]{:S(2)}) collective-permute-start(f32[128,128]{1,0:T(8,128)S(1)} %add.24), channel_id=1, source_target_pairs={{0,34},{2,32},{16,50},{18,48},{32,2},{34,0},{48,18},{50,16},{1,35}... | collective-permute-start | bytes 196616 | tf_op jit(solution)/shard_map/ppermute | solution.py:290
  49.7 3.9 %collective-permute-done.11 = f32[128,128]{1,0:T(8,128)S(1)} collective-permute-done((f32[128,128]{1,0:T(8,128)S(1)}, f32[128,128]{1,0:T(8,128)S(1)}, u32[]{:S(2)}, u32[]{:S(2)}) %collective-permute-start.11) | collective-permute-done | bytes 65568 | tf_op jit(solution)/shard_map/ppermute | solution.py:290
  53.7 3.4 %collective-permute-done.15 = f32[128,128]{1,0:T(8,128)S(1)} collective-permute-done((f32[128,128]{1,0:T(8,128)S(1)}, f32[128,128]{1,0:T(8,128)S(1)}, u32[]{:S(2)}, u32[]{:S(2)}) %collective-permute-start.15) | collective-permute-done | bytes 65568 | tf_op jit(solution)/shard_map/ppermute | solution.py:290
  57.7 6.0 %collective-permute-start.17 = (bf16[16,256,128]{2,1,0:T(8,128)(2,1)S(1)}, bf16[16,256,128]{2,1,0:T(8,128)(2,1)S(1)}, u32[]{:S(2)}, u32[]{:S(2)}) collective-permute-start(bf16[16,256,128]{2,1,0:T(8,128)(2,1)S(1)} %collective-permute-done.16.refs_1_), channel_id=1, source_target_pairs={{0,1},{1,0},{2,3},{3,2},{4,5},{5,4},{6,7},{7,6},{8,9},{9,8},{10,11... | collective-permute-start | bytes 3145736 | tf_op jit(solution)/shard_map/ppermute | solution.py:290
  64.6 4.1 %collective-permute-done.18 = f32[128,128]{1,0:T(8,128)S(1)} collective-permute-done((f32[128,128]{1,0:T(8,128)S(1)}, f32[128,128]{1,0:T(8,128)S(1)}, u32[]{:S(2)}, u32[]{:S(2)}) %collective-permute-start.18) | collective-permute-done | bytes 65568 | tf_op jit(solution)/shard_map/ppermute | solution.py:290
  68.7 3.9 %collective-permute-start.20 = (bf16[8,256,128]{2,1,0:T(8,128)(2,1)S(1)}, bf16[8,256,128]{2,1,0:T(8,128)(2,1)S(1)}, u32[]{:S(2)}, u32[]{:S(2)}) collective-permute-start(bf16[8,256,128]{2,1,0:T(8,128)(2,1)S(1)} %collective-permute-done.19.refs_3_), channel_id=1, source_target_pairs={{0,1},{1,0},{2,3},{3,2},{4,5},{5,4},{6,7},{7,6},{8,9},{9,8},{10,11... | collective-permute-start | bytes 1572872 | tf_op jit(solution)/shard_map/ppermute | solution.py:290
  72.7 3.7 %collective-permute-start.14 = (bf16[1024,128]{1,0:T(8,128)(2,1)S(1)}, bf16[1024,128]{1,0:T(8,128)(2,1)S(1)}, u32[]{:S(2)}, u32[]{:S(2)}) collective-permute-start(bf16[1024,128]{1,0:T(8,128)(2,1)S(1)} %shard_map.110), channel_id=1, source_target_pairs={{0,2},{2,0},{1,3},{3,1},{4,6},{6,4},{5,7},{7,5},{8,10},{10,8},{9,1... | collective-permute-start | bytes 786440 | tf_op jit(solution)/shard_map/ppermute | solution.py:290
  76.7 13.7 %collective-permute-done.14.refs_5_ = bf16[1024,128]{1,0:T(8,128)(2,1)S(1)} collective-permute-done((bf16[1024,128]{1,0:T(8,128)(2,1)S(1)}, bf16[1024,128]{1,0:T(8,128)(2,1)S(1)}, u32[]{:S(2)}, u32[]{:S(2)}) %collective-permute-start.14) | collective-permute-done | bytes 262176 | tf_op jit(solution)/shard_map/ppermute | solution.py:290
  90.4 2.0 %shard_map.111 = f32[1024,128]{1,0:T(8,128)} custom-call(bf16[2,1024,128]{2,1,0:T(8,128)(2,1)S(1)} %get-tuple-element.40.refs_0_, bf16[2,2,512,128]{3,2,1,0:T(8,128)(2,1)S(1)} %collective-permute-done.8.left_ref.refs_1_, bf16[2,2,512,128]{3,2,1,0:T(8,128)(2,1)S(1)} %collective-permute-done.9.right_ref.refs_2_, ...), custom_call_target="tpu_custom_call" | custom-call | tf_op jit(solution)/shard_map/pallas_call | solution.py:147
  92.4 4.4 %shard_map.113 = (f32[1024,128]{1,0:T(8,128)}, bf16[1024,2048]{1,0:T(8,128)(2,1)}) custom-call(bf16[16,256,128]{2,1,0:T(8,128)(2,1)S(1)} %shard_map.112.refs_0_, bf16[16,256,128]{2,1,0:T(8,128)(2,1)S(1)} %collective-permute-done.16.refs_1_, bf16[16,256,128]{2,1,0:T(8,128)(2,1)S(1)} %collective-permute-done.17.refs_2_, ...), custom_call_target="tpu_custom_call" | custom-call | tf_op jit(solution)/shard_map/pallas_call | solution.py:272
  (55 shorter events, 7.5 us)
Async XLA Ops:
  4.3 6.0 %collective-permute-start = (bf16[8,1024,128]{2,1,0:T(8,128)(2,1)S(1)}, bf16[8,1024,128]{2,1,0:T(8,128)(2,1)S(1)}, u32[]{:S(2)}, u32[]{:S(2)}) collective-permute-start(bf16[8,1024,128]{2,1,0:T(8,128)(2,1)S(1)} %get-tuple-element.39), channel_id=1, source_target_pairs={{0,1},{1,0},{2,3},{3,2},{4,5},{5,4},{6,7},{7,6},{8,9},{9,8},{10,11... | collective-permute-start | bytes 6291464 | tf_op jit(solution)/shard_map/ppermute | solution.py:290
  5.1 9.0 %collective-permute-start.1 = (bf16[1,256,128]{2,1,0:T(8,128)(2,1)S(1)}, bf16[1,256,128]{2,1,0:T(8,128)(2,1)S(1)}, u32[]{:S(2)}, u32[]{:S(2)}) collective-permute-start(bf16[1,256,128]{2,1,0:T(8,128)(2,1)S(1)} %shard_map.105.first_ref), channel_id=1, source_target_pairs={{0,34},{2,32},{16,50},{18,48},{32,2},{34,0},{48,18},{50,16},{1,35}... | collective-permute-start | bytes 196616 | tf_op jit(solution)/shard_map/ppermute | solution.py:290
  14.1 4.7 %collective-permute-start.3 = (bf16[2,256,128]{2,1,0:T(8,128)(2,1)S(1)}, bf16[2,256,128]{2,1,0:T(8,128)(2,1)S(1)}, u32[]{:S(2)}, u32[]{:S(2)}) collective-permute-start(bf16[2,256,128]{2,1,0:T(8,128)(2,1)S(1)} %shard_map.106.first_ref), channel_id=1, source_target_pairs={{0,4},{4,0},{8,12},{12,8},{1,5},{5,1},{9,13},{13,9},{2,6},{6,2},{1... | collective-permute-start | bytes 393224 | tf_op jit(solution)/shard_map/ppermute | solution.py:290
  15.4 3.4 %collective-permute-start.2 = (f32[128,128]{1,0:T(8,128)S(1)}, f32[128,128]{1,0:T(8,128)S(1)}, u32[]{:S(2)}, u32[]{:S(2)}) collective-permute-start(f32[128,128]{1,0:T(8,128)S(1)} %get-tuple-element.44), channel_id=1, source_target_pairs={{0,64},{64,0},{128,192},{192,128},{1,65},{65,1},{129,193},{193,129... | collective-permute-start | bytes 196616 | tf_op jit(solution)/shard_map/ppermute | solution.py:290
  18.9 7.8 %collective-permute-start.5 = (bf16[4,256,128]{2,1,0:T(8,128)(2,1)S(1)}, bf16[4,256,128]{2,1,0:T(8,128)(2,1)S(1)}, u32[]{:S(2)}, u32[]{:S(2)}) collective-permute-start(bf16[4,256,128]{2,1,0:T(8,128)(2,1)S(1)} %shard_map.107.first_ref), channel_id=1, source_target_pairs={{4,8},{8,4},{12,0},{0,12},{5,9},{9,5},{13,1},{1,13},{6,10},{10,6},... | collective-permute-start | bytes 786440 | tf_op jit(solution)/shard_map/ppermute | solution.py:290
  21.3 5.4 %collective-permute-start.4 = (f32[128,128]{1,0:T(8,128)S(1)}, f32[128,128]{1,0:T(8,128)S(1)}, u32[]{:S(2)}, u32[]{:S(2)}) collective-permute-start(f32[128,128]{1,0:T(8,128)S(1)} %add.21), channel_id=1, source_target_pairs={{64,128},{128,64},{192,0},{0,192},{65,129},{129,65},{193,1},{1,193... | collective-permute-start | bytes 196616 | tf_op jit(solution)/shard_map/ppermute | solution.py:290
  24.0 13.8 %collective-permute-start.8 = (bf16[2,2,512,128]{3,2,1,0:T(8,128)(2,1)S(1)}, bf16[2,2,512,128]{3,2,1,0:T(8,128)(2,1)S(1)}, u32[]{:S(2)}, u32[]{:S(2)}) collective-permute-start(bf16[2,2,512,128]{3,2,1,0:T(8,128)(2,1)S(1)} %get-tuple-element.53), channel_id=1, source_target_pairs={{0,4},{4,8},{8,12},{12,0},{1,5},{5,9},{9,13},{13,1},{2,6},{6,10},{... | collective-permute-start | bytes 1572872 | tf_op jit(solution)/shard_map/ppermute | solution.py:290
  24.0 13.8 %collective-permute-start.9 = (bf16[2,2,512,128]{3,2,1,0:T(8,128)(2,1)S(1)}, bf16[2,2,512,128]{3,2,1,0:T(8,128)(2,1)S(1)}, u32[]{:S(2)}, u32[]{:S(2)}) collective-permute-start(bf16[2,2,512,128]{3,2,1,0:T(8,128)(2,1)S(1)} %get-tuple-element.54), channel_id=1, source_target_pairs={{0,12},{4,0},{8,4},{12,8},{1,13},{5,1},{9,5},{13,9},{2,14},{6,2},{... | collective-permute-start | bytes 1572872 | tf_op jit(solution)/shard_map/ppermute | solution.py:290
  26.7 11.1 %collective-permute-start.7 = (bf16[8,256,128]{2,1,0:T(8,128)(2,1)S(1)}, bf16[8,256,128]{2,1,0:T(8,128)(2,1)S(1)}, u32[]{:S(2)}, u32[]{:S(2)}) collective-permute-start(bf16[8,256,128]{2,1,0:T(8,128)(2,1)S(1)} %shard_map.108.first_ref), channel_id=1, source_target_pairs={{0,1},{1,0},{2,3},{3,2},{4,5},{5,4},{6,7},{7,6},{8,9},{9,8},{10,11... | collective-permute-start | bytes 1572872 | tf_op jit(solution)/shard_map/ppermute | solution.py:290
  29.6 3.7 %collective-permute-start.6 = (f32[128,128]{1,0:T(8,128)S(1)}, f32[128,128]{1,0:T(8,128)S(1)}, u32[]{:S(2)}, u32[]{:S(2)}) collective-permute-start(f32[128,128]{1,0:T(8,128)S(1)} %add.22), channel_id=1, source_target_pairs={{0,16},{16,0},{32,48},{48,32},{1,17},{17,1},{33,49},{49,33},{2,18}... | collective-permute-start | bytes 196616 | tf_op jit(solution)/shard_map/ppermute | solution.py:290
  37.9 19.2 %collective-permute-start.16 = (bf16[16,256,128]{2,1,0:T(8,128)(2,1)S(1)}, bf16[16,256,128]{2,1,0:T(8,128)(2,1)S(1)}, u32[]{:S(2)}, u32[]{:S(2)}) collective-permute-start(bf16[16,256,128]{2,1,0:T(8,128)(2,1)S(1)} %shard_map.112.refs_0_), channel_id=1, source_target_pairs={{0,64},{1,193},{64,128},{65,1},{128,192},{129,65},{192,0},{193,129... | collective-permute-start | bytes 3145736 | tf_op jit(solution)/shard_map/ppermute | solution.py:290
  40.5 13.1 %collective-permute-start.12 = (bf16[2,512,128]{2,1,0:T(8,128)(2,1)S(1)}, bf16[2,512,128]{2,1,0:T(8,128)(2,1)S(1)}, u32[]{:S(2)}, u32[]{:S(2)}) collective-permute-start(bf16[2,512,128]{2,1,0:T(8,128)(2,1)S(1)} %get-tuple-element.60), channel_id=1, source_target_pairs={{0,4},{4,8},{8,12},{12,0},{1,5},{5,9},{9,13},{13,1},{2,6},{6,10},{... | collective-permute-start | bytes 786440 | tf_op jit(solution)/shard_map/ppermute | solution.py:290
  40.6 49.8 %copy-start.6 = (f32[128,128]{1,0:T(8,128)S(1)}, f32[128,128]{1,0:T(8,128)}, u32[]{:S(2)}) copy-start(f32[128,128]{1,0:T(8,128)} %constant.14.clone.refs_7_) | copy-start | bytes 196612
  40.6 13.0 %collective-permute-start.13 = (bf16[2,512,128]{2,1,0:T(8,128)(2,1)S(1)}, bf16[2,512,128]{2,1,0:T(8,128)(2,1)S(1)}, u32[]{:S(2)}, u32[]{:S(2)}) collective-permute-start(bf16[2,512,128]{2,1,0:T(8,128)(2,1)S(1)} %get-tuple-element.61), channel_id=1, source_target_pairs={{0,12},{4,0},{8,4},{12,8},{1,13},{5,1},{9,5},{13,9},{2,14},{6,2},{... | collective-permute-start | bytes 786440 | tf_op jit(solution)/shard_map/ppermute | solution.py:290
  43.3 4.3 %collective-permute-start.10 = (f32[128,128]{1,0:T(8,128)S(1)}, f32[128,128]{1,0:T(8,128)S(1)}, u32[]{:S(2)}, u32[]{:S(2)}) collective-permute-start(f32[128,128]{1,0:T(8,128)S(1)} %add.23), channel_id=1, source_target_pairs={{0,32},{16,48},{32,0},{48,16},{1,33},{17,49},{33,1},{49,17},{2,34}... | collective-permute-start | bytes 196616 | tf_op jit(solution)/shard_map/ppermute | solution.py:290
  47.6 6.0 %collective-permute-start.11 = (f32[128,128]{1,0:T(8,128)S(1)}, f32[128,128]{1,0:T(8,128)S(1)}, u32[]{:S(2)}, u32[]{:S(2)}) collective-permute-start(f32[128,128]{1,0:T(8,128)S(1)} %add.24), channel_id=1, source_target_pairs={{0,34},{2,32},{16,50},{18,48},{32,2},{34,0},{48,18},{50,16},{1,35}... | collective-permute-start | bytes 196616 | tf_op jit(solution)/shard_map/ppermute | solution.py:290
  53.6 3.5 %collective-permute-start.15 = (f32[128,128]{1,0:T(8,128)S(1)}, f32[128,128]{1,0:T(8,128)S(1)}, u32[]{:S(2)}, u32[]{:S(2)}) collective-permute-start(f32[128,128]{1,0:T(8,128)S(1)} %add.25), channel_id=1, source_target_pairs={{0,4},{4,0},{8,12},{12,8},{1,5},{5,1},{9,13},{13,9},{2,6},{6,2},{1... | collective-permute-start | bytes 196616 | tf_op jit(solution)/shard_map/ppermute | solution.py:290
  57.2 11.5 %collective-permute-start.19 = (bf16[8,256,128]{2,1,0:T(8,128)(2,1)S(1)}, bf16[8,256,128]{2,1,0:T(8,128)(2,1)S(1)}, u32[]{:S(2)}, u32[]{:S(2)}) collective-permute-start(bf16[8,256,128]{2,1,0:T(8,128)(2,1)S(1)} %slice.3), channel_id=1, source_target_pairs={{0,64},{1,193},{64,128},{65,1},{128,192},{129,65},{192,0},{193,129... | collective-permute-start | bytes 1572872 | tf_op jit(solution)/shard_map/ppermute | solution.py:290
  57.7 34.7 %collective-permute-start.17 = (bf16[16,256,128]{2,1,0:T(8,128)(2,1)S(1)}, bf16[16,256,128]{2,1,0:T(8,128)(2,1)S(1)}, u32[]{:S(2)}, u32[]{:S(2)}) collective-permute-start(bf16[16,256,128]{2,1,0:T(8,128)(2,1)S(1)} %collective-permute-done.16.refs_1_), channel_id=1, source_target_pairs={{0,1},{1,0},{2,3},{3,2},{4,5},{5,4},{6,7},{7,6},{8,9},{9,8},{10,11... | collective-permute-start | bytes 3145736 | tf_op jit(solution)/shard_map/ppermute | solution.py:290
  63.7 4.9 %collective-permute-start.18 = (f32[128,128]{1,0:T(8,128)S(1)}, f32[128,128]{1,0:T(8,128)S(1)}, u32[]{:S(2)}, u32[]{:S(2)}) collective-permute-start(f32[128,128]{1,0:T(8,128)S(1)} %add.26), channel_id=1, source_target_pairs={{4,8},{8,4},{12,0},{0,12},{5,9},{9,5},{13,1},{1,13},{6,10},{10,6},... | collective-permute-start | bytes 196616 | tf_op jit(solution)/shard_map/ppermute | solution.py:290
  68.7 23.7 %collective-permute-start.20 = (bf16[8,256,128]{2,1,0:T(8,128)(2,1)S(1)}, bf16[8,256,128]{2,1,0:T(8,128)(2,1)S(1)}, u32[]{:S(2)}, u32[]{:S(2)}) collective-permute-start(bf16[8,256,128]{2,1,0:T(8,128)(2,1)S(1)} %collective-permute-done.19.refs_3_), channel_id=1, source_target_pairs={{0,1},{1,0},{2,3},{3,2},{4,5},{5,4},{6,7},{7,6},{8,9},{9,8},{10,11... | collective-permute-start | bytes 1572872 | tf_op jit(solution)/shard_map/ppermute | solution.py:290
  72.7 19.7 %copy-start.3 = (bf16[1024,128]{1,0:T(8,128)(2,1)S(1)}, bf16[1024,128]{1,0:T(8,128)(2,1)}, u32[]{:S(2)}) copy-start(bf16[1024,128]{1,0:T(8,128)(2,1)} %constant.15.clone.refs_8_) | copy-start | bytes 786436
  72.7 17.7 %collective-permute-start.14 = (bf16[1024,128]{1,0:T(8,128)(2,1)S(1)}, bf16[1024,128]{1,0:T(8,128)(2,1)S(1)}, u32[]{:S(2)}, u32[]{:S(2)}) collective-permute-start(bf16[1024,128]{1,0:T(8,128)(2,1)S(1)} %shard_map.110), channel_id=1, source_target_pairs={{0,2},{2,0},{1,3},{3,1},{4,6},{6,4},{5,7},{7,5},{8,10},{10,8},{9,1... | collective-permute-start | bytes 786440 | tf_op jit(solution)/shard_map/ppermute | solution.py:290
  76.4 16.0 %collective-permute-start.21 = (f32[128,128]{1,0:T(8,128)S(1)}, f32[128,128]{1,0:T(8,128)S(1)}, u32[]{:S(2)}, u32[]{:S(2)}) collective-permute-start(f32[128,128]{1,0:T(8,128)S(1)} %add_multiply_fusion.refs_5_), channel_id=1, source_target_pairs={{0,1},{1,0},{2,3},{3,2},{4,5},{5,4},{6,7},{7,6},{8,9},{9,8},{10,11... | collective-permute-start | bytes 196616 | tf_op jit(solution)/shard_map/ppermute | solution.py:290
  (6 other events, 46.6 us)

commit v3 on v2

v3 whole, which is shorter than its diff:
```python
import functools

import jax
import jax.numpy as jnp
import numpy as np
from jax import lax
from jax.experimental import pallas as pl
from jax.experimental.pallas import tpu as pltpu
from jax.sharding import Mesh
from jax.sharding import PartitionSpec as P

GROUP = 128
BAND = 16
ROWS = 1024
HALF = 512
QUARTER = 256

momentum_decay = 0.9
step_size = 0.05
replicas = 16

bf16 = jnp.bfloat16
f32 = jnp.float32
HIGHEST = lax.Precision.HIGHEST

SWAP2 = [(0, 1), (1, 0)]
UP4 = [(i, (i + 1) % 4) for i in range(4)]
DOWN4 = [(i, (i + 3) % 4) for i in range(4)]
ACROSS4 = [(i, (i + 2) % 4) for i in range(4)]
EVEN4 = [(0, 1), (1, 0), (2, 3), (3, 2)]
ODD4 = [(1, 2), (2, 1), (3, 0), (0, 3)]
XOR2 = [(i, i ^ 2) for i in range(4)]
CROSS8 = [(i, i ^ 5) for i in range(8)]
SPREAD8 = [(i, (i + 2) % 8) if i % 2 == 0 else (i, (i + 6) % 8) for i in range(8)]


def cosine_rows():
    freq = np.arange(BAND, dtype=np.float64)[:, None]
    place = np.arange(GROUP, dtype=np.float64)[None, :]
    factor = np.where(freq == 0.0, np.sqrt(1.0 / GROUP), np.sqrt(2.0 / GROUP))
    return factor * np.cos(np.pi * (2.0 * place + 1.0) * freq / (2.0 * GROUP))


def column_of(dx, gz, core):
    bx = lax.rem(lax.axis_index("x") + dx, 4)
    zh = lax.axis_index("zh")
    bz = zh if gz == 0 else 1 - zh
    return bx * 4 + bz * 2 + core


def slot_of(dx, gz):
    bx = lax.rem(lax.axis_index("x") + dx, 4)
    zh = lax.axis_index("zh")
    return bx * 2 + (zh if gz == 0 else 1 - zh)


def lanes(index):
    return pl.ds(pl.multiple_of(index * GROUP, GROUP), GROUP)


def split_kernel(g_ref, sent_ref, own_ref):
    core = lax.axis_index("core")
    for gz in range(2):
        for dx in range(4):
            k = gz * 4 + dx
            sent_ref[k] = g_ref[:, lanes(column_of(dx, gz, 1 - core))]
            own_ref[k] = g_ref[:, lanes(column_of(dx, gz, core))]


def split_blocks(g):
    blocks = jax.ShapeDtypeStruct((8, ROWS, GROUP), bf16)
    return pl.pallas_call(
        split_kernel,
        out_shape=[blocks, blocks],
        in_specs=[pl.BlockSpec(memory_space=pltpu.VMEM)],
        out_specs=[pl.BlockSpec(memory_space=pltpu.VMEM)] * 2,
        compiler_params=pltpu.CompilerParams(vmem_limit_bytes=12 * 2**20),
    )(g)


def pair_sum_kernel(
    own_ref, other_ref, mom_ref, table_ref, rows_ref, w0_ref, wz_ref, up_ref, down_ref,
    keep_up_ref, keep_down_ref, mine_ref, band_ref, acc_ref,
):
    for ref in (up_ref, down_ref):
        ref[4, :QUARTER] = w0_ref[...]
        ref[4, QUARTER:] = wz_ref[...]
    lane_slot = lax.broadcasted_iota(jnp.int32, (GROUP, GROUP), 1) // BAND
    table = table_ref[...]
    zero = jnp.zeros_like(table)
    for gz in range(2):
        for dx in range(4):
            k = gz * 4 + dx
            s = (own_ref[k].astype(f32) + other_ref[k].astype(f32)).astype(bf16)
            if dx == 0:
                mine_ref[gz] = s
            elif dx == 1:
                keep_up_ref[gz] = s[:HALF]
                up_ref[gz * 2 + 1] = s[HALF:]
            elif dx == 2:
                up_ref[gz * 2] = s[:HALF]
                down_ref[gz * 2] = s[HALF:]
            else:
                down_ref[gz * 2 + 1] = s[:HALF]
                keep_down_ref[gz] = s[HALF:]
            placed = jnp.where(lane_slot == slot_of(dx, gz), table, zero)
            part = jnp.dot(s, placed.astype(bf16), preferred_element_type=f32)
            if k == 0:
                acc_ref[...] = part + jnp.dot(
                    momentum_decay * mom_ref[...], placed, preferred_element_type=f32
                )
            else:
                acc_ref[...] += part
    for a in range(ROWS // GROUP):
        band_ref[a * BAND : (a + 1) * BAND, :] = jnp.dot(
            rows_ref[...],
            acc_ref[a * GROUP : (a + 1) * GROUP, :],
            precision=HIGHEST,
            preferred_element_type=f32,
        )


def pair_sum(*args):
    shapes = [(5, HALF, GROUP)] * 2 + [(2, HALF, GROUP)] * 2 + [(2, ROWS, GROUP)]
    shapes = [jax.ShapeDtypeStruct(shape, bf16) for shape in shapes]
    shapes.append(jax.ShapeDtypeStruct((ROWS // GROUP * BAND, GROUP), f32))
    vmem = pl.BlockSpec(memory_space=pltpu.VMEM)
    return pl.pallas_call(
        pair_sum_kernel,
        out_shape=shapes,
        in_specs=[vmem] * 7,
        out_specs=[vmem] * 6,
        scratch_shapes=[pltpu.VMEM((ROWS, GROUP), f32)],
        compiler_params=pltpu.CompilerParams(vmem_limit_bytes=16 * 2**20),
    )(*args)


def small_call(kernel, shapes, *args):
    vmem = pl.BlockSpec(memory_space=pltpu.VMEM)
    return pl.pallas_call(
        kernel,
        out_shape=shapes,
        in_specs=[vmem] * len(args),
        out_specs=jax.tree.map(lambda _: vmem, shapes),
        compiler_params=pltpu.CompilerParams(vmem_limit_bytes=8 * 2**20),
    )(*args)


def join_kernel(first_ref, second_ref, out_ref):
    half = first_ref.shape[0]
    out_ref[:half] = first_ref[...]
    out_ref[half:] = second_ref[...]


def joined(first, second):
    shape = (2 * first.shape[0], *first.shape[1:])
    return small_call(join_kernel, jax.ShapeDtypeStruct(shape, first.dtype), first, second)


def cast_kernel(master_ref, out_ref):
    y = lax.axis_index("y")
    out_ref[...] = master_ref[pl.ds(pl.multiple_of(y * QUARTER, QUARTER), QUARTER), :].astype(bf16)


def pass_on_kernel(keep_up_ref, keep_down_ref, left_ref, right_ref, up_ref, down_ref):
    for gz in range(2):
        r = slice(gz * HALF, (gz + 1) * HALF)
        up_ref[r] = (keep_up_ref[gz].astype(f32) + left_ref[gz * 2].astype(f32)).astype(bf16)
        down_ref[r] = (keep_down_ref[gz].astype(f32) + right_ref[gz * 2].astype(f32)).astype(bf16)
    up_ref[2 * HALF :] = left_ref[4, :QUARTER]
    down_ref[2 * HALF :] = right_ref[4, QUARTER:]


def collect_kernel(w0_ref, wz_ref, left_ref, right_ref, last_left_ref, last_right_ref, out_ref):
    out_ref[0] = w0_ref[...]
    out_ref[1] = left_ref[4, :QUARTER]
    out_ref[2] = right_ref[4, :QUARTER]
    out_ref[3] = last_left_ref[2 * HALF :]
    out_ref[4] = wz_ref[...]
    out_ref[5] = left_ref[4, QUARTER:]
    out_ref[6] = right_ref[4, QUARTER:]
    out_ref[7] = last_right_ref[2 * HALF :]


def x_total(mine_ref, left_ref, right_ref, last_left_ref, last_right_ref, gz, a):
    r = slice(a * GROUP, (a + 1) * GROUP)
    h = slice(a % 4 * GROUP, (a % 4 + 1) * GROUP)
    p = slice(gz * HALF + a % 4 * GROUP, gz * HALF + (a % 4 + 1) * GROUP)
    direct, passed = (right_ref, last_left_ref) if a < 4 else (left_ref, last_right_ref)
    total = mine_ref[gz, r].astype(f32) + direct[gz * 2 + 1, h].astype(f32)
    return total + passed[p].astype(f32)


def z_send_kernel(*refs):
    for a in range(ROWS // GROUP):
        refs[5][a * GROUP : (a + 1) * GROUP] = x_total(*refs[:5], 1, a).astype(bf16)


def remaining_kernel(*refs):
    z_ref, mom_ref, q_ref, out_ref = refs[5:]
    q = q_ref[...]
    for a in range(ROWS // GROUP):
        r = slice(a * GROUP, (a + 1) * GROUP)
        summed = x_total(*refs[:5], 0, a) + z_ref[r].astype(f32)
        moment = momentum_decay * mom_ref[r] + summed
        low = jnp.dot(moment, q, precision=HIGHEST, preferred_element_type=f32)
        low = jnp.dot(q, low, precision=HIGHEST, preferred_element_type=f32)
        out_ref[r] = moment - low


def gathered_x(j):
    return lax.rem(lax.axis_index("x") + (0, 3, 1, 2)[j], 4)


def columns_side(table_ref):
    zh = lax.axis_index("zh")
    row_slot = lax.broadcasted_iota(jnp.int32, (GROUP, GROUP), 0) // BAND
    table = table_ref[...]
    zero = jnp.zeros_like(table)
    columns = []
    wide = []
    for gz in range(2):
        for j in range(4):
            bx, bz = gathered_x(j), (zh if gz == 0 else 1 - zh)
            columns.append(bx * 4 + bz * 2)
            wide.append(jnp.where(row_slot == bx * 2 + bz, table, zero).astype(bf16))
    return jnp.concatenate(wide, axis=1), columns


def update_quarter(dy, pieces, spread_ref, wide, columns, page_ref, full_out, sem):
    core = lax.axis_index("core")
    quarter = lax.rem(lax.axis_index("y") + dy, 4)
    rows = pl.ds(pl.multiple_of(quarter * QUARTER, QUARTER), QUARTER)
    for who in range(2):
        side = core if who == 0 else 1 - core
        update = jnp.dot(
            spread_ref[rows, who * GROUP : (who + 1) * GROUP],
            wide,
            preferred_element_type=f32,
        )
        for k, column in enumerate(columns):
            part = update[:, k * GROUP : (k + 1) * GROUP]
            new = pieces[who][k].astype(f32) + part
            page_ref[:, lanes(column + side)] = new.astype(bf16)
    copy = pltpu.make_async_copy(page_ref, full_out.at[rows, :], sem)
    copy.start()
    return copy


def first_weights_kernel(
    quarter_ref, near_ref, near_other_ref, band_ref, band_other_ref, master_ref, cols_ref,
    table_ref, master_out, full_out, spread_ref, page_ref, sem,
):
    core = lax.axis_index("core")
    wide, columns = columns_side(table_ref)
    coeffs = jnp.concatenate([band_ref[...], band_other_ref[...]], axis=1)
    spread_ref[...] = jnp.dot(
        cols_ref[...], coeffs.astype(bf16), preferred_element_type=f32
    ).astype(bf16)
    low, high = slice(0, 8), slice(8, 16)
    copies = []
    for step, (dy, ref, parts) in enumerate(
        (
            (0, quarter_ref, (low, high)),
            (3 - 2 * core, near_ref, (low, high)),
            (1 + 2 * core, near_other_ref, (high, low)),
        )
    ):
        pieces = tuple(ref.at[part] for part in parts)
        copies.append(
            update_quarter(
                dy, pieces, spread_ref, wide, columns, page_ref.at[step], full_out, sem.at[step]
            )
        )
    master_out[...] = master_ref[...] + jnp.dot(
        spread_ref[:, :GROUP], wide[:, :GROUP], preferred_element_type=f32
    )
    for copy in copies:
        copy.wait()


def last_weights_kernel(
    far_ref, far_other_ref, spread_ref, table_ref, started_ref, full_out, page_ref, sem
):
    del started_ref
    wide, columns = columns_side(table_ref)
    update_quarter(
        2, (far_ref, far_other_ref), spread_ref, wide, columns, page_ref, full_out, sem
    ).wait()


def weights_of(quarters, last_quarter, bands, master, cols, table):
    vmem = pl.BlockSpec(memory_space=pltpu.VMEM)
    anywhere = pl.BlockSpec(memory_space=pl.ANY)
    full = jax.ShapeDtypeStruct((ROWS, 16 * GROUP), bf16)
    new_master, started, spread = pl.pallas_call(
        first_weights_kernel,
        out_shape=[
            jax.ShapeDtypeStruct((ROWS, GROUP), f32),
            full,
            jax.ShapeDtypeStruct((ROWS, 2 * GROUP), bf16),
        ],
        in_specs=[vmem] * 8,
        out_specs=[vmem, anywhere, vmem],
        scratch_shapes=[
            pltpu.VMEM((3, QUARTER, 16 * GROUP), bf16),
            pltpu.SemaphoreType.DMA((3,)),
        ],
        compiler_params=pltpu.CompilerParams(vmem_limit_bytes=20 * 2**20),
    )(*quarters, *bands, master, cols, table)
    weights_full = pl.pallas_call(
        last_weights_kernel,
        out_shape=full,
        in_specs=[vmem] * 4 + [anywhere],
        out_specs=anywhere,
        input_output_aliases={4: 0},
        scratch_shapes=[
            pltpu.VMEM((QUARTER, 16 * GROUP), bf16),
            pltpu.SemaphoreType.DMA,
        ],
        compiler_params=pltpu.CompilerParams(vmem_limit_bytes=12 * 2**20),
    )(*last_quarter, spread, table, started)
    return new_master, weights_full


def send(array, axis, perm):
    return lax.ppermute(array, axis, perm)


together = lax.optimization_barrier


def local(gradients, momentum, master_weights):
    table = cosine_rows()
    mom = momentum[0]
    half = (ROWS, GROUP)
    z = ("zl", "zh")

    sent, own = split_blocks(gradients[0, 0])
    other = send(sent, "core", SWAP2)
    w0 = small_call(cast_kernel, jax.ShapeDtypeStruct((QUARTER, GROUP), bf16), master_weights)
    wz = send(w0, z, CROSS8)
    up, down, keep_up, keep_down, mine, band = pair_sum(
        own,
        other,
        mom,
        jnp.asarray(np.tile(table.T, (1, 8)), f32),
        jnp.asarray(table, f32),
        w0,
        wz,
    )

    got = send(band, "zl", EVEN4)
    left = send(up, "x", UP4)
    right = send(down, "x", DOWN4)

    band = band + got
    got = send(band, "zl", XOR2)

    band = band + got
    got = send(band, z, CROSS8)

    band, left, right = together((band + got, left, right))
    got = send(band, "y", EVEN4)
    passed = jax.ShapeDtypeStruct((2 * HALF + QUARTER, GROUP), bf16)
    up, down = small_call(pass_on_kernel, [passed] * 2, keep_up, keep_down, left, right)
    last_left = send(up, "x", UP4)
    last_right = send(down, "x", DOWN4)

    band, last_left, last_right = together((band + got, last_left, last_right))
    got = send(band, "y", ODD4)
    parts = (mine, left, right, last_left, last_right)
    z_send = small_call(z_send_kernel, jax.ShapeDtypeStruct(half, bf16), *parts)
    from_z = send(z_send, "zh", SWAP2)
    eighth = small_call(
        collect_kernel, jax.ShapeDtypeStruct((8, QUARTER, GROUP), bf16), w0, wz, *parts[1:]
    )
    wc = send(eighth, "core", SWAP2)

    band, eighth, wc = together((band + got, eighth, wc))
    got = send(band, "x", EVEN4)
    quarter = joined(eighth, wc)
    near = send(quarter, ("y", "core"), SPREAD8)

    band, from_z, near = together((band + got, from_z, near))
    got = send(band, "x", ODD4)
    far = send(near[:8], ("y", "core"), SPREAD8)
    near_other = send(near, "core", SWAP2)
    new_momentum = small_call(
        remaining_kernel,
        jax.ShapeDtypeStruct(half, f32),
        *parts,
        from_z,
        mom,
        jnp.asarray(table.T @ table, f32),
    )

    band = (band + got) * (-step_size / replicas)
    band, new_momentum, near_other = together((band, new_momentum, near_other))
    band_other = send(band, "core", SWAP2)

    band, band_other, far = together((band, band_other, far))
    far_other = send(far, "core", SWAP2)
    new_master, weights_full = weights_of(
        (quarter, near, near_other),
        (far, far_other),
        (band, band_other),
        master_weights,
        jnp.asarray(np.kron(np.eye(8), table.T), bf16),
        jnp.asarray(np.tile(table, (8, 1)), f32),
    )
    return (new_momentum[None], new_master, weights_full)


def solution(mesh):
    fine = Mesh(mesh.devices.reshape(4, 4, 4, 2, 2), ("y", "zl", "x", "zh", "core"))
    rep, fsdp = ("y", "zl"), ("x", "zh", "core")
    return jax.shard_map(
        local,
        mesh=fine,
        in_specs=(P(rep, fsdp, None, None), P(rep, None, fsdp), P(None, fsdp)),
        out_specs=(P(rep, None, fsdp), P(None, fsdp), P()),
        check_vma=False,
    )
```

time: 97.1 us -> 87 us (0.90)
  waiting for transfers between devices: 41.4 us -> 34.7 us
  starting transfers between devices: 42.1 us -> 37.5 us
    ppermute x22 -> x20, waiting for transfers between devices: 41.4 us -> 34.7 us  [send(): return lax.ppermute(array, axis, perm)]
    ppermute x22 -> x20, starting transfers between devices: 42.1 us -> 37.5 us  [send(): return lax.ppermute(array, axis, perm)]
    pallas_call x2 -> x3, Pallas kernels: 6.35 us -> 7.48 us  [the longest x1 3.78 us: weights_of(): pl.pallas_call(first_weights_kernel, out_shape=[jax.ShapeDtypeStruct((ROW...]
    pallas_call x8 -> x6, Pallas kernels: 2.35 us -> 2.32 us  [small_call(): pl.pallas_call(kernel, out_shape=shapes, in_specs=[vmem] * len(args), out...]
  transfers between devices with their start and end apart: 22 -> 20, of which waited for: 9 -> 11; matrix products, arithmetic and copies ran while one was open for 0% -> 0% of each run, Pallas kernels for 4% -> 7%
where the time goes in v3:
time: 87 us; the launch traced here: 86.4 us
  starting transfers between devices  37.5 us (43%)
  waiting for transfers between devices  34.7 us (40%)
  Pallas kernels  10.9 us (13%)
  local copies, waits for them, and re-layouts  2.26 us (3%)
  between operations  0.97 us (1%)
    ppermute x20, starting transfers between devices, send(): return lax.ppermute(array, axis, perm)  37.5 us
    ppermute x20, waiting for transfers between devices, send(): return lax.ppermute(array, axis, perm)  34.7 us
    pallas_call x1, Pallas kernels, weights_of(): pl.pallas_call(first_weights_kernel, out_shape=[jax.ShapeDtypeStruct((ROW...  3.78 us
    pallas_call x6, Pallas kernels, small_call(): pl.pallas_call(kernel, out_shape=shapes, in_specs=[vmem] * len(args), out...  2.32 us
    unnamed x16, local copies, waits for them, and re-layouts  2.23 us
    pallas_call x1, Pallas kernels, pair_sum(): pl.pallas_call(pair_sum_kernel, out_shape=shapes, in_specs=[vmem] * 7, ou...  2.06 us
  transfers between devices with their start and end apart: 20, of which 11 were waited for; matrix products, arithmetic and copies ran while one was open for 0% of the time, Pallas kernels for 7%

profile of v3, /device:TPU:33, one launch (start us, length us, event | category | flops | bytes accessed | tf_op | source)
XLA Modules:
  0.0 86.4 jit_solution(4309113857050202709)
XLA Ops:
  0.7 2.2 %copy-done = bf16[1,1,1024,2048]{3,2,1,0:T(8,128)(2,1)S(1)} copy-done((bf16[1,1,1024,2048]{3,2,1,0:T(8,128)(2,1)S(1)}, bf16[1,1,1024,2048]{3,2,1,0:T(8,128)(2,1)}, u32[]{:S(2)}) %copy-start) | copy-done | bytes 4194328
  4.7 5.2 %collective-permute-start.1 = (bf16[256,128]{1,0:T(8,128)(2,1)S(1)}, bf16[256,128]{1,0:T(8,128)(2,1)S(1)}, u32[]{:S(2)}, u32[]{:S(2)}) collective-permute-start(bf16[256,128]{1,0:T(8,128)(2,1)S(1)} %shard_map.104.w0_ref), channel_id=1, source_target_pairs={{0,34},{2,32},{16,50},{18,48},{32,2},{34,0},{48,18},{50,16},{1,35}... | collective-permute-start | bytes 196616 | tf_op jit(solution)/shard_map/ppermute | solution.py:327
  10.0 3.8 %collective-permute-done.1.wz_ref = bf16[256,128]{1,0:T(8,128)(2,1)S(1)} collective-permute-done((bf16[256,128]{1,0:T(8,128)(2,1)S(1)}, bf16[256,128]{1,0:T(8,128)(2,1)S(1)}, u32[]{:S(2)}, u32[]{:S(2)}) %collective-permute-start.1) | collective-permute-done | bytes 65568 | tf_op jit(solution)/shard_map/ppermute | solution.py:327
  13.8 2.1 %shard_map.105 = (bf16[5,512,128]{2,1,0:T(8,128)(2,1)S(1)}, bf16[5,512,128]{2,1,0:T(8,128)(2,1)S(1)}, bf16[2,512,128]{2,1,0:T(8,128)(2,1)S(1)}, bf16[2,512,128]{...) custom-call(bf16[8,1024,128]{2,1,0:T(8,128)(2,1)S(1)} %get-tuple-element.34.own_ref, ...), custom_call_target="tpu_custom_call" | custom-call | tf_op jit(solution)/shard_map/pallas_call | solution.py:128
  17.1 1.5 %collective-permute-start.6 = (bf16[5,512,128]{2,1,0:T(8,128)(2,1)S(1)}, bf16[5,512,128]{2,1,0:T(8,128)(2,1)S(1)}, u32[]{:S(2)}, u32[]{:S(2)}) collective-permute-start(bf16[5,512,128]{2,1,0:T(8,128)(2,1)S(1)} %get-tuple-element.38), channel_id=1, source_target_pairs={{0,12},{4,0},{8,4},{12,8},{1,13},{5,1},{9,5},{13,9},{2,14},{6,2},{... | collective-permute-start | bytes 1966088 | tf_op jit(solution)/shard_map/ppermute | solution.py:327
  18.6 3.4 %collective-permute-done.2 = f32[128,128]{1,0:T(8,128)S(1)} collective-permute-done((f32[128,128]{1,0:T(8,128)S(1)}, f32[128,128]{1,0:T(8,128)S(1)}, u32[]{:S(2)}, u32[]{:S(2)}) %collective-permute-start.2) | collective-permute-done | bytes 65568 | tf_op jit(solution)/shard_map/ppermute | solution.py:327
  22.5 3.9 %collective-permute-done.3 = f32[128,128]{1,0:T(8,128)S(1)} collective-permute-done((f32[128,128]{1,0:T(8,128)S(1)}, f32[128,128]{1,0:T(8,128)S(1)}, u32[]{:S(2)}, u32[]{:S(2)}) %collective-permute-start.3) | collective-permute-done | bytes 65568 | tf_op jit(solution)/shard_map/ppermute | solution.py:327
  26.4 2.7 %collective-permute-start.4 = (f32[128,128]{1,0:T(8,128)S(1)}, f32[128,128]{1,0:T(8,128)S(1)}, u32[]{:S(2)}, u32[]{:S(2)}) collective-permute-start(f32[128,128]{1,0:T(8,128)S(1)} %add.22), channel_id=1, source_target_pairs={{0,34},{2,32},{16,50},{18,48},{32,2},{34,0},{48,18},{50,16},{1,35}... | collective-permute-start | bytes 196616 | tf_op jit(solution)/shard_map/ppermute | solution.py:327
  29.1 3.3 %collective-permute-done.4 = f32[128,128]{1,0:T(8,128)S(1)} collective-permute-done((f32[128,128]{1,0:T(8,128)S(1)}, f32[128,128]{1,0:T(8,128)S(1)}, u32[]{:S(2)}, u32[]{:S(2)}) %collective-permute-start.4) | collective-permute-done | bytes 65568 | tf_op jit(solution)/shard_map/ppermute | solution.py:327
  33.9 1.8 %collective-permute-start.9 = (bf16[1280,128]{1,0:T(8,128)(2,1)S(1)}, bf16[1280,128]{1,0:T(8,128)(2,1)S(1)}, u32[]{:S(2)}, u32[]{:S(2)}) collective-permute-start(bf16[1280,128]{1,0:T(8,128)(2,1)S(1)} %get-tuple-element.45), channel_id=1, source_target_pairs={{0,12},{4,0},{8,4},{12,8},{1,13},{5,1},{9,5},{13,9},{2,14},{6,2},{... | collective-permute-start | bytes 983048 | tf_op jit(solution)/shard_map/ppermute | solution.py:327
  36.9 1.8 %collective-permute-done.7 = f32[128,128]{1,0:T(8,128)S(1)} collective-permute-done((f32[128,128]{1,0:T(8,128)S(1)}, f32[128,128]{1,0:T(8,128)S(1)}, u32[]{:S(2)}, u32[]{:S(2)}) %collective-permute-start.7) | collective-permute-done | bytes 65568 | tf_op jit(solution)/shard_map/ppermute | solution.py:327
  40.2 4.9 %collective-permute-start.11 = (bf16[8,256,128]{2,1,0:T(8,128)(2,1)S(1)}, bf16[8,256,128]{2,1,0:T(8,128)(2,1)S(1)}, u32[]{:S(2)}, u32[]{:S(2)}) collective-permute-start(bf16[8,256,128]{2,1,0:T(8,128)(2,1)S(1)} %shard_map.107.first_ref), channel_id=1, source_target_pairs={{0,1},{1,0},{2,3},{3,2},{4,5},{5,4},{6,7},{7,6},{8,9},{9,8},{10,11... | collective-permute-start | bytes 1572872 | tf_op jit(solution)/shard_map/ppermute | solution.py:327
  45.1 2.7 %collective-permute-start.10 = (f32[128,128]{1,0:T(8,128)S(1)}, f32[128,128]{1,0:T(8,128)S(1)}, u32[]{:S(2)}, u32[]{:S(2)}) collective-permute-start(f32[128,128]{1,0:T(8,128)S(1)} %add.24), channel_id=1, source_target_pairs={{64,128},{128,64},{192,0},{0,192},{65,129},{129,65},{193,1},{1,193... | collective-permute-start | bytes 196616 | tf_op jit(solution)/shard_map/ppermute | solution.py:327
  47.9 2.2 %collective-permute-done.10 = f32[128,128]{1,0:T(8,128)S(1)} collective-permute-done((f32[128,128]{1,0:T(8,128)S(1)}, f32[128,128]{1,0:T(8,128)S(1)}, u32[]{:S(2)}, u32[]{:S(2)}) %collective-permute-start.10) | collective-permute-done | bytes 65568 | tf_op jit(solution)/shard_map/ppermute | solution.py:327
  50.2 2.7 %collective-permute-start.14 = (bf16[16,256,128]{2,1,0:T(8,128)(2,1)S(1)}, bf16[16,256,128]{2,1,0:T(8,128)(2,1)S(1)}, u32[]{:S(2)}, u32[]{:S(2)}) collective-permute-start(bf16[16,256,128]{2,1,0:T(8,128)(2,1)S(1)} %shard_map.109.quarter_ref), channel_id=1, source_target_pairs={{0,64},{1,193},{64,128},{65,1},{128,192},{129,65},{192,0},{193,129... | collective-permute-start | bytes 3145736 | tf_op jit(solution)/shard_map/ppermute | solution.py:327
  53.0 4.0 %collective-permute-start.13 = (bf16[1024,128]{1,0:T(8,128)(2,1)S(1)}, bf16[1024,128]{1,0:T(8,128)(2,1)S(1)}, u32[]{:S(2)}, u32[]{:S(2)}) collective-permute-start(bf16[1024,128]{1,0:T(8,128)(2,1)S(1)} %shard_map.108), channel_id=1, source_target_pairs={{0,2},{2,0},{1,3},{3,1},{4,6},{6,4},{5,7},{7,5},{8,10},{10,8},{9,1... | collective-permute-start | bytes 786440 | tf_op jit(solution)/shard_map/ppermute | solution.py:327
  57.3 3.1 %collective-permute-done.12 = f32[128,128]{1,0:T(8,128)S(1)} collective-permute-done((f32[128,128]{1,0:T(8,128)S(1)}, f32[128,128]{1,0:T(8,128)S(1)}, u32[]{:S(2)}, u32[]{:S(2)}) %collective-permute-start.12) | collective-permute-done | bytes 65568 | tf_op jit(solution)/shard_map/ppermute | solution.py:327
  60.4 9.4 %collective-permute-done.13.refs_5_ = bf16[1024,128]{1,0:T(8,128)(2,1)S(1)} collective-permute-done((bf16[1024,128]{1,0:T(8,128)(2,1)S(1)}, bf16[1024,128]{1,0:T(8,128)(2,1)S(1)}, u32[]{:S(2)}, u32[]{:S(2)}) %collective-permute-start.13) | collective-permute-done | bytes 262176 | tf_op jit(solution)/shard_map/ppermute | solution.py:327
  71.5 3.0 %collective-permute-start.15 = (f32[128,128]{1,0:T(8,128)S(1)}, f32[128,128]{1,0:T(8,128)S(1)}, u32[]{:S(2)}, u32[]{:S(2)}) collective-permute-start(f32[128,128]{1,0:T(8,128)S(1)} %add.26), channel_id=1, source_target_pairs={{4,8},{8,4},{12,0},{0,12},{5,9},{9,5},{13,1},{1,13},{6,10},{10,6},... | collective-permute-start | bytes 196616 | tf_op jit(solution)/shard_map/ppermute | solution.py:327
  74.4 2.0 %shard_map.110 = f32[1024,128]{1,0:T(8,128)} custom-call(bf16[2,1024,128]{2,1,0:T(8,128)(2,1)S(1)} %get-tuple-element.50.refs_0_, bf16[5,512,128]{2,1,0:T(8,128)(2,1)S(1)} %collective-permute-done.5.left_ref.refs_1_, bf16[5,512,128]{2,1,0:T(8,128)(2,1)S(1)} %collective-permute-done.6.right_ref.refs_2_, ...), custom_call_target="tpu_custom_call" | custom-call | tf_op jit(solution)/shard_map/pallas_call | solution.py:140
  76.5 2.1 %collective-permute-done.18.far_ref = bf16[8,256,128]{2,1,0:T(8,128)(2,1)S(1)} collective-permute-done((bf16[8,256,128]{2,1,0:T(8,128)(2,1)S(1)}, bf16[8,256,128]{2,1,0:T(8,128)(2,1)S(1)}, u32[]{:S(2)}, u32[]{:S(2)}) %collective-permute-start.18) | collective-permute-done | bytes 524320 | tf_op jit(solution)/shard_map/ppermute | solution.py:327
  78.6 2.2 %collective-permute-start.19 = (bf16[8,256,128]{2,1,0:T(8,128)(2,1)S(1)}, bf16[8,256,128]{2,1,0:T(8,128)(2,1)S(1)}, u32[]{:S(2)}, u32[]{:S(2)}) collective-permute-start(bf16[8,256,128]{2,1,0:T(8,128)(2,1)S(1)} %collective-permute-done.18.far_ref), channel_id=1, source_target_pairs={{0,1},{1,0},{2,3},{3,2},{4,5},{5,4},{6,7},{7,6},{8,9},{9,8},{10,11... | collective-permute-start | bytes 1572872 | tf_op jit(solution)/shard_map/ppermute | solution.py:327
  80.8 3.8 %shard_map.111 = (f32[1024,128]{1,0:T(8,128)}, bf16[1024,2048]{1,0:T(8,128)(2,1)}, bf16[1024,256]{1,0:T(8,128)(2,1)S(1)}) custom-call(bf16[16,256,128]{2,1,0:T(8,128)(2,1)S(1)} %shard_map.109.quarter_ref, bf16[16,256,128]{2,1,0:T(8,128)(2,1)S(1)} %collective-permute-done.14.near_ref, bf16[16,256,128]{2,1,0:T(8,128)(2,1)S(1)} %collective-permute-done.16.near_other_ref, ...), custom_call_target="tpu_custom_call" | custom-call | tf_op jit(solution)/shard_map/pallas_call | solution.py:296
  84.6 1.6 %shard_map.112 = bf16[1024,2048]{1,0:T(8,128)(2,1)} custom-call(bf16[8,256,128]{2,1,0:T(8,128)(2,1)S(1)} %collective-permute-done.18.far_ref, bf16[8,256,128]{2,1,0:T(8,128)(2,1)S(1)} %collective-permute-done.19.far_other_ref, bf16[1024,256]{1,0:T(8,128)(2,1)S(1)} %get-tuple-element.63.spread_ref, ...), custom_call_target="tpu_custom_call", output_to_operand_aliasing={{}: (4, {})} | custom-call | tf_op jit(solution)/shard_map/pallas_call | solution.py:311
  (50 shorter events, 10.0 us)
Async XLA Ops:
  0.6 13.2 %copy-start.7 = (f32[16,128]{1,0:T(8,128)S(1)}, f32[16,128]{1,0:T(8,128)}, u32[]{:S(2)}) copy-start(f32[16,128]{1,0:T(8,128)} %constant.13.clone.rows_ref) | copy-start | bytes 24580
  4.0 9.8 %collective-permute-start = (bf16[8,1024,128]{2,1,0:T(8,128)(2,1)S(1)}, bf16[8,1024,128]{2,1,0:T(8,128)(2,1)S(1)}, u32[]{:S(2)}, u32[]{:S(2)}) collective-permute-start(bf16[8,1024,128]{2,1,0:T(8,128)(2,1)S(1)} %get-tuple-element.35), channel_id=1, source_target_pairs={{0,1},{1,0},{2,3},{3,2},{4,5},{5,4},{6,7},{7,6},{8,9},{9,8},{10,11... | collective-permute-start | bytes 6291464 | tf_op jit(solution)/shard_map/ppermute | solution.py:327
  4.7 9.0 %collective-permute-start.1 = (bf16[256,128]{1,0:T(8,128)(2,1)S(1)}, bf16[256,128]{1,0:T(8,128)(2,1)S(1)}, u32[]{:S(2)}, u32[]{:S(2)}) collective-permute-start(bf16[256,128]{1,0:T(8,128)(2,1)S(1)} %shard_map.104.w0_ref), channel_id=1, source_target_pairs={{0,34},{2,32},{16,50},{18,48},{32,2},{34,0},{48,18},{50,16},{1,35}... | collective-permute-start | bytes 196616 | tf_op jit(solution)/shard_map/ppermute | solution.py:327
  15.9 16.9 %collective-permute-start.5 = (bf16[5,512,128]{2,1,0:T(8,128)(2,1)S(1)}, bf16[5,512,128]{2,1,0:T(8,128)(2,1)S(1)}, u32[]{:S(2)}, u32[]{:S(2)}) collective-permute-start(bf16[5,512,128]{2,1,0:T(8,128)(2,1)S(1)} %get-tuple-element.37), channel_id=1, source_target_pairs={{0,4},{4,8},{8,12},{12,0},{1,5},{5,9},{9,13},{13,1},{2,6},{6,10},{... | collective-permute-start | bytes 1966088 | tf_op jit(solution)/shard_map/ppermute | solution.py:327
  17.1 15.7 %collective-permute-start.6 = (bf16[5,512,128]{2,1,0:T(8,128)(2,1)S(1)}, bf16[5,512,128]{2,1,0:T(8,128)(2,1)S(1)}, u32[]{:S(2)}, u32[]{:S(2)}) collective-permute-start(bf16[5,512,128]{2,1,0:T(8,128)(2,1)S(1)} %get-tuple-element.38), channel_id=1, source_target_pairs={{0,12},{4,0},{8,4},{12,8},{1,13},{5,1},{9,5},{13,9},{2,14},{6,2},{... | collective-permute-start | bytes 1966088 | tf_op jit(solution)/shard_map/ppermute | solution.py:327
  18.6 3.4 %collective-permute-start.2 = (f32[128,128]{1,0:T(8,128)S(1)}, f32[128,128]{1,0:T(8,128)S(1)}, u32[]{:S(2)}, u32[]{:S(2)}) collective-permute-start(f32[128,128]{1,0:T(8,128)S(1)} %get-tuple-element.36), channel_id=1, source_target_pairs={{0,16},{16,0},{32,48},{48,32},{1,17},{17,1},{33,49},{49,33},{2,18}... | collective-permute-start | bytes 196616 | tf_op jit(solution)/shard_map/ppermute | solution.py:327
  22.0 4.4 %collective-permute-start.3 = (f32[128,128]{1,0:T(8,128)S(1)}, f32[128,128]{1,0:T(8,128)S(1)}, u32[]{:S(2)}, u32[]{:S(2)}) collective-permute-start(f32[128,128]{1,0:T(8,128)S(1)} %add.21), channel_id=1, source_target_pairs={{0,32},{16,48},{32,0},{48,16},{1,33},{17,49},{33,1},{49,17},{2,34}... | collective-permute-start | bytes 196616 | tf_op jit(solution)/shard_map/ppermute | solution.py:327
  26.4 6.0 %collective-permute-start.4 = (f32[128,128]{1,0:T(8,128)S(1)}, f32[128,128]{1,0:T(8,128)S(1)}, u32[]{:S(2)}, u32[]{:S(2)}) collective-permute-start(f32[128,128]{1,0:T(8,128)S(1)} %add.22), channel_id=1, source_target_pairs={{0,34},{2,32},{16,50},{18,48},{32,2},{34,0},{48,18},{50,16},{1,35}... | collective-permute-start | bytes 196616 | tf_op jit(solution)/shard_map/ppermute | solution.py:327
  32.9 7.2 %collective-permute-start.8 = (bf16[1280,128]{1,0:T(8,128)(2,1)S(1)}, bf16[1280,128]{1,0:T(8,128)(2,1)S(1)}, u32[]{:S(2)}, u32[]{:S(2)}) collective-permute-start(bf16[1280,128]{1,0:T(8,128)(2,1)S(1)} %get-tuple-element.44), channel_id=1, source_target_pairs={{0,4},{4,8},{8,12},{12,0},{1,5},{5,9},{9,13},{13,1},{2,6},{6,10},{... | collective-permute-start | bytes 983048 | tf_op jit(solution)/shard_map/ppermute | solution.py:327
  33.9 6.3 %collective-permute-start.9 = (bf16[1280,128]{1,0:T(8,128)(2,1)S(1)}, bf16[1280,128]{1,0:T(8,128)(2,1)S(1)}, u32[]{:S(2)}, u32[]{:S(2)}) collective-permute-start(bf16[1280,128]{1,0:T(8,128)(2,1)S(1)} %get-tuple-element.45), channel_id=1, source_target_pairs={{0,12},{4,0},{8,4},{12,8},{1,13},{5,1},{9,5},{13,9},{2,14},{6,2},{... | collective-permute-start | bytes 983048 | tf_op jit(solution)/shard_map/ppermute | solution.py:327
  35.7 3.1 %collective-permute-start.7 = (f32[128,128]{1,0:T(8,128)S(1)}, f32[128,128]{1,0:T(8,128)S(1)}, u32[]{:S(2)}, u32[]{:S(2)}) collective-permute-start(f32[128,128]{1,0:T(8,128)S(1)} %add.23), channel_id=1, source_target_pairs={{0,64},{64,0},{128,192},{192,128},{1,65},{65,1},{129,193},{193,129... | collective-permute-start | bytes 196616 | tf_op jit(solution)/shard_map/ppermute | solution.py:327
  38.8 35.6 %copy-start.5 = (f32[128,128]{1,0:T(8,128)S(1)}, f32[128,128]{1,0:T(8,128)}, u32[]{:S(2)}) copy-start(f32[128,128]{1,0:T(8,128)} %constant.14.clone.refs_7_) | copy-start | bytes 196612
  40.2 9.9 %collective-permute-start.11 = (bf16[8,256,128]{2,1,0:T(8,128)(2,1)S(1)}, bf16[8,256,128]{2,1,0:T(8,128)(2,1)S(1)}, u32[]{:S(2)}, u32[]{:S(2)}) collective-permute-start(bf16[8,256,128]{2,1,0:T(8,128)(2,1)S(1)} %shard_map.107.first_ref), channel_id=1, source_target_pairs={{0,1},{1,0},{2,3},{3,2},{4,5},{5,4},{6,7},{7,6},{8,9},{9,8},{10,11... | collective-permute-start | bytes 1572872 | tf_op jit(solution)/shard_map/ppermute | solution.py:327
  45.1 4.9 %collective-permute-start.10 = (f32[128,128]{1,0:T(8,128)S(1)}, f32[128,128]{1,0:T(8,128)S(1)}, u32[]{:S(2)}, u32[]{:S(2)}) collective-permute-start(f32[128,128]{1,0:T(8,128)S(1)} %add.24), channel_id=1, source_target_pairs={{64,128},{128,64},{192,0},{0,192},{65,129},{129,65},{193,1},{1,193... | collective-permute-start | bytes 196616 | tf_op jit(solution)/shard_map/ppermute | solution.py:327
  50.1 30.7 %copy-start.3 = (f32[128,128]{1,0:T(8,128)S(1)}, f32[128,128]{1,0:T(8,128)}, u32[]{:S(2)}) copy-start(f32[128,128]{1,0:T(8,128)} %constant.16.clone.table_ref) | copy-start | bytes 196612
  50.2 30.7 %copy-start.4 = (bf16[1024,128]{1,0:T(8,128)(2,1)S(1)}, bf16[1024,128]{1,0:T(8,128)(2,1)}, u32[]{:S(2)}) copy-start(bf16[1024,128]{1,0:T(8,128)(2,1)} %constant.15.clone.cols_ref) | copy-start | bytes 786436
  50.2 19.6 %collective-permute-start.14 = (bf16[16,256,128]{2,1,0:T(8,128)(2,1)S(1)}, bf16[16,256,128]{2,1,0:T(8,128)(2,1)S(1)}, u32[]{:S(2)}, u32[]{:S(2)}) collective-permute-start(bf16[16,256,128]{2,1,0:T(8,128)(2,1)S(1)} %shard_map.109.quarter_ref), channel_id=1, source_target_pairs={{0,64},{1,193},{64,128},{65,1},{128,192},{129,65},{192,0},{193,129... | collective-permute-start | bytes 3145736 | tf_op jit(solution)/shard_map/ppermute | solution.py:327
  53.0 16.8 %collective-permute-start.13 = (bf16[1024,128]{1,0:T(8,128)(2,1)S(1)}, bf16[1024,128]{1,0:T(8,128)(2,1)S(1)}, u32[]{:S(2)}, u32[]{:S(2)}) collective-permute-start(bf16[1024,128]{1,0:T(8,128)(2,1)S(1)} %shard_map.108), channel_id=1, source_target_pairs={{0,2},{2,0},{1,3},{3,1},{4,6},{6,4},{5,7},{7,5},{8,10},{10,8},{9,1... | collective-permute-start | bytes 786440 | tf_op jit(solution)/shard_map/ppermute | solution.py:327
  57.0 3.4 %collective-permute-start.12 = (f32[128,128]{1,0:T(8,128)S(1)}, f32[128,128]{1,0:T(8,128)S(1)}, u32[]{:S(2)}, u32[]{:S(2)}) collective-permute-start(f32[128,128]{1,0:T(8,128)S(1)} %add.25), channel_id=1, source_target_pairs={{0,4},{4,0},{8,12},{12,8},{1,5},{5,1},{9,13},{13,9},{2,6},{6,2},{1... | collective-permute-start | bytes 196616 | tf_op jit(solution)/shard_map/ppermute | solution.py:327
  69.8 6.6 %collective-permute-start.16 = (bf16[16,256,128]{2,1,0:T(8,128)(2,1)S(1)}, bf16[16,256,128]{2,1,0:T(8,128)(2,1)S(1)}, u32[]{:S(2)}, u32[]{:S(2)}) collective-permute-start(bf16[16,256,128]{2,1,0:T(8,128)(2,1)S(1)} %collective-permute-done.14.near_ref), channel_id=1, source_target_pairs={{0,1},{1,0},{2,3},{3,2},{4,5},{5,4},{6,7},{7,6},{8,9},{9,8},{10,11... | collective-permute-start | bytes 3145736 | tf_op jit(solution)/shard_map/ppermute | solution.py:327
  70.2 8.4 %collective-permute-start.18 = (bf16[8,256,128]{2,1,0:T(8,128)(2,1)S(1)}, bf16[8,256,128]{2,1,0:T(8,128)(2,1)S(1)}, u32[]{:S(2)}, u32[]{:S(2)}) collective-permute-start(bf16[8,256,128]{2,1,0:T(8,128)(2,1)S(1)} %slice.3), channel_id=1, source_target_pairs={{0,64},{1,193},{64,128},{65,1},{128,192},{129,65},{192,0},{193,129... | collective-permute-start | bytes 1572872 | tf_op jit(solution)/shard_map/ppermute | solution.py:327
  71.5 4.9 %collective-permute-start.15 = (f32[128,128]{1,0:T(8,128)S(1)}, f32[128,128]{1,0:T(8,128)S(1)}, u32[]{:S(2)}, u32[]{:S(2)}) collective-permute-start(f32[128,128]{1,0:T(8,128)S(1)} %add.26), channel_id=1, source_target_pairs={{4,8},{8,4},{12,0},{0,12},{5,9},{9,5},{13,1},{1,13},{6,10},{10,6},... | collective-permute-start | bytes 196616 | tf_op jit(solution)/shard_map/ppermute | solution.py:327
  76.4 2.2 %collective-permute-start.17 = (f32[128,128]{1,0:T(8,128)S(1)}, f32[128,128]{1,0:T(8,128)S(1)}, u32[]{:S(2)}, u32[]{:S(2)}) collective-permute-start(f32[128,128]{1,0:T(8,128)S(1)} %add_multiply_fusion.band_ref), channel_id=1, source_target_pairs={{0,1},{1,0},{2,3},{3,2},{4,5},{5,4},{6,7},{7,6},{8,9},{9,8},{10,11... | collective-permute-start | bytes 196616 | tf_op jit(solution)/shard_map/ppermute | solution.py:327
  78.6 6.0 %collective-permute-start.19 = (bf16[8,256,128]{2,1,0:T(8,128)(2,1)S(1)}, bf16[8,256,128]{2,1,0:T(8,128)(2,1)S(1)}, u32[]{:S(2)}, u32[]{:S(2)}) collective-permute-start(bf16[8,256,128]{2,1,0:T(8,128)(2,1)S(1)} %collective-permute-done.18.far_ref), channel_id=1, source_target_pairs={{0,1},{1,0},{2,3},{3,2},{4,5},{5,4},{6,7},{7,6},{8,9},{9,8},{10,11... | collective-permute-start | bytes 1572872 | tf_op jit(solution)/shard_map/ppermute | solution.py:327
  (4 other events, 26.0 us)

commit v4 on v3

--- a/solution.py
+++ b/solution.py
@@ -31,7 +31,6 @@
 ODD4 = [(1, 2), (2, 1), (3, 0), (0, 3)]
 XOR2 = [(i, i ^ 2) for i in range(4)]
 CROSS8 = [(i, i ^ 5) for i in range(8)]
-SPREAD8 = [(i, (i + 2) % 8) if i % 2 == 0 else (i, (i + 6) % 8) for i in range(8)]
 
 
 def cosine_rows():
@@ -79,12 +78,9 @@
 
 
 def pair_sum_kernel(
-    own_ref, other_ref, mom_ref, table_ref, rows_ref, w0_ref, wz_ref, up_ref, down_ref,
-    keep_up_ref, keep_down_ref, mine_ref, band_ref, acc_ref,
+    own_ref, other_ref, mom_ref, table_ref, rows_ref, up_ref, down_ref, keep_up_ref, keep_down_ref,
+    mine_ref, band_ref, acc_ref,
 ):
-    for ref in (up_ref, down_ref):
-        ref[4, :QUARTER] = w0_ref[...]
-        ref[4, QUARTER:] = wz_ref[...]
     lane_slot = lax.broadcasted_iota(jnp.int32, (GROUP, GROUP), 1) // BAND
     table = table_ref[...]
     zero = jnp.zeros_like(table)
@@ -128,20 +124,21 @@
     return pl.pallas_call(
         pair_sum_kernel,
         out_shape=shapes,
-        in_specs=[vmem] * 7,
+        in_specs=[vmem] * 5,
         out_specs=[vmem] * 6,
         scratch_shapes=[pltpu.VMEM((ROWS, GROUP), f32)],
         compiler_params=pltpu.CompilerParams(vmem_limit_bytes=16 * 2**20),
     )(*args)
 
 
-def small_call(kernel, shapes, *args):
+def small_call(kernel, shapes, *args, cost=None):
     vmem = pl.BlockSpec(memory_space=pltpu.VMEM)
     return pl.pallas_call(
         kernel,
         out_shape=shapes,
         in_specs=[vmem] * len(args),
         out_specs=jax.tree.map(lambda _: vmem, shapes),
+        cost_estimate=cost,
         compiler_params=pltpu.CompilerParams(vmem_limit_bytes=8 * 2**20),
     )(*args)
 
@@ -160,6 +157,25 @@
 def cast_kernel(master_ref, out_ref):
     y = lax.axis_index("y")
     out_ref[...] = master_ref[pl.ds(pl.multiple_of(y * QUARTER, QUARTER), QUARTER), :].astype(bf16)
+
+
+def enclose_kernel(w0_ref, wz_ref, up_in_ref, down_in_ref, up_ref, down_ref):
+    del up_in_ref, down_in_ref
+    for ref in (up_ref, down_ref):
+        ref[4, :QUARTER] = w0_ref[...]
+        ref[4, QUARTER:] = wz_ref[...]
+
+
+def enclosed(w0, wz, up, down):
+    vmem = pl.BlockSpec(memory_space=pltpu.VMEM)
+    return pl.pallas_call(
+        enclose_kernel,
+        out_shape=[jax.ShapeDtypeStruct(up.shape, bf16)] * 2,
+        in_specs=[vmem] * 4,
+        out_specs=[vmem] * 2,
+        input_output_aliases={2: 0, 3: 1},
+        compiler_params=pltpu.CompilerParams(vmem_limit_bytes=8 * 2**20),
+    )(w0, wz, up, down)
 
 
 def pass_on_kernel(keep_up_ref, keep_down_ref, left_ref, right_ref, up_ref, down_ref):
@@ -180,6 +196,23 @@
     out_ref[5] = left_ref[4, QUARTER:]
     out_ref[6] = right_ref[4, QUARTER:]
     out_ref[7] = last_right_ref[2 * HALF :]
+
+
+def half_kernel(below_ref, above_ref, low_ref, high_ref):
+    low_ref[...] = below_ref[:4]
+    high_ref[...] = above_ref[4:]
+
+
+def pack_kernel(*refs):
+    at = 0
+    for ref in refs[:-1]:
+        refs[-1][at : at + ref.shape[0]] = ref[...]
+        at += ref.shape[0]
+
+
+def packed(*parts):
+    blocks = sum(part.shape[0] for part in parts)
+    return small_call(pack_kernel, jax.ShapeDtypeStruct((blocks, QUARTER, GROUP), bf16), *parts)
 
 
 def x_total(mine_ref, left_ref, right_ref, last_left_ref, last_right_ref, gz, a):
@@ -208,70 +241,46 @@
         out_ref[r] = moment - low
 
 
-def gathered_x(j):
-    return lax.rem(lax.axis_index("x") + (0, 3, 1, 2)[j], 4)
-
-
-def columns_side(table_ref):
-    zh = lax.axis_index("zh")
+def weights_kernel(*refs):
+    packs, (band_ref, band_other_ref, master_ref, cols_ref, table_ref) = refs[:4], refs[4:9]
+    master_out, full_out, spread_ref, page_ref, sem = refs[9:]
+    x, y, zh, core = (lax.axis_index(name) for name in ("x", "y", "zh", "core"))
+
     row_slot = lax.broadcasted_iota(jnp.int32, (GROUP, GROUP), 0) // BAND
     table = table_ref[...]
     zero = jnp.zeros_like(table)
     columns = []
     wide = []
-    for gz in range(2):
-        for j in range(4):
-            bx, bz = gathered_x(j), (zh if gz == 0 else 1 - zh)
-            columns.append(bx * 4 + bz * 2)
-            wide.append(jnp.where(row_slot == bx * 2 + bz, table, zero).astype(bf16))
-    return jnp.concatenate(wide, axis=1), columns
-
-
-def update_quarter(dy, pieces, spread_ref, wide, columns, page_ref, full_out, sem):
-    core = lax.axis_index("core")
-    quarter = lax.rem(lax.axis_index("y") + dy, 4)
-    rows = pl.ds(pl.multiple_of(quarter * QUARTER, QUARTER), QUARTER)
-    for who in range(2):
-        side = core if who == 0 else 1 - core
-        update = jnp.dot(
-            spread_ref[rows, who * GROUP : (who + 1) * GROUP],
-            wide,
-            preferred_element_type=f32,
-        )
-        for k, column in enumerate(columns):
-            part = update[:, k * GROUP : (k + 1) * GROUP]
-            new = pieces[who][k].astype(f32) + part
-            page_ref[:, lanes(column + side)] = new.astype(bf16)
-    copy = pltpu.make_async_copy(page_ref, full_out.at[rows, :], sem)
-    copy.start()
-    return copy
-
-
-def first_weights_kernel(
-    quarter_ref, near_ref, near_other_ref, band_ref, band_other_ref, master_ref, cols_ref,
-    table_ref, master_out, full_out, spread_ref, page_ref, sem,
-):
-    core = lax.axis_index("core")
-    wide, columns = columns_side(table_ref)
+    for gz, dx in [(gz, dx) for gz in range(2) for dx in (0, 3, 1, 2)]:
+        bx, bz = lax.rem(x + dx, 4), (zh if gz == 0 else 1 - zh)
+        columns.append(bx * 4 + bz * 2)
+        wide.append(jnp.where(row_slot == bx * 2 + bz, table, zero).astype(bf16))
+    wide = jnp.concatenate(wide, axis=1)
+
     coeffs = jnp.concatenate([band_ref[...], band_other_ref[...]], axis=1)
     spread_ref[...] = jnp.dot(
         cols_ref[...], coeffs.astype(bf16), preferred_element_type=f32
     ).astype(bf16)
-    low, high = slice(0, 8), slice(8, 16)
+
     copies = []
-    for step, (dy, ref, parts) in enumerate(
-        (
-            (0, quarter_ref, (low, high)),
-            (3 - 2 * core, near_ref, (low, high)),
-            (1 + 2 * core, near_other_ref, (high, low)),
-        )
-    ):
-        pieces = tuple(ref.at[part] for part in parts)
-        copies.append(
-            update_quarter(
-                dy, pieces, spread_ref, wide, columns, page_ref.at[step], full_out, sem.at[step]
+    for step, dy in enumerate((0, 3, 1, 2)):
+        quarter = lax.rem(y + dy, 4)
+        rows = pl.ds(pl.multiple_of(quarter * QUARTER, QUARTER), QUARTER)
+        for who in range(2):
+            side = core if who == 0 else 1 - core
+            update = jnp.dot(
+                spread_ref[rows, who * GROUP : (who + 1) * GROUP],
+                wide,
+                preferred_element_type=f32,
             )
-        )
+            for k in range(8):
+                part = update[:, k * GROUP : (k + 1) * GROUP]
+                prior = packs[2 + who][k] if step == 3 else packs[who][step * 8 + k]
+                new = prior.astype(f32) + part
+                page_ref[step, :, lanes(columns[k] + side)] = new.astype(bf16)
+        copy = pltpu.make_async_copy(page_ref.at[step], full_out.at[rows, :], sem.at[step])
+        copy.start()
+        copies.append(copy)
     master_out[...] = master_ref[...] + jnp.dot(
         spread_ref[:, :GROUP], wide[:, :GROUP], preferred_element_type=f32
     )
@@ -279,48 +288,23 @@
         copy.wait()
 
 
-def last_weights_kernel(
-    far_ref, far_other_ref, spread_ref, table_ref, started_ref, full_out, page_ref, sem
-):
-    del started_ref
-    wide, columns = columns_side(table_ref)
-    update_quarter(
-        2, (far_ref, far_other_ref), spread_ref, wide, columns, page_ref, full_out, sem
-    ).wait()
-
-
-def weights_of(quarters, last_quarter, bands, master, cols, table):
+def weights_of(packs, bands, master, cols, table):
     vmem = pl.BlockSpec(memory_space=pltpu.VMEM)
-    anywhere = pl.BlockSpec(memory_space=pl.ANY)
-    full = jax.ShapeDtypeStruct((ROWS, 16 * GROUP), bf16)
-    new_master, started, spread = pl.pallas_call(
-        first_weights_kernel,
+    return pl.pallas_call(
+        weights_kernel,
         out_shape=[
             jax.ShapeDtypeStruct((ROWS, GROUP), f32),
-            full,
-            jax.ShapeDtypeStruct((ROWS, 2 * GROUP), bf16),
+            jax.ShapeDtypeStruct((ROWS, 16 * GROUP), bf16),
         ],
-        in_specs=[vmem] * 8,
-        out_specs=[vmem, anywhere, vmem],
+        in_specs=[vmem] * 9,
+        out_specs=[vmem, pl.BlockSpec(memory_space=pl.ANY)],
         scratch_shapes=[
-            pltpu.VMEM((3, QUARTER, 16 * GROUP), bf16),
-            pltpu.SemaphoreType.DMA((3,)),
+            pltpu.VMEM((ROWS, 2 * GROUP), bf16),
+            pltpu.VMEM((4, QUARTER, 16 * GROUP), bf16),
+            pltpu.SemaphoreType.DMA((4,)),
         ],
         compiler_params=pltpu.CompilerParams(vmem_limit_bytes=20 * 2**20),
-    )(*quarters, *bands, master, cols, table)
-    weights_full = pl.pallas_call(
-        last_weights_kernel,
-        out_shape=full,
-        in_specs=[vmem] * 4 + [anywhere],
-        out_specs=anywhere,
-        input_output_aliases={4: 0},
-        scratch_shapes=[
-            pltpu.VMEM((QUARTER, 16 * GROUP), bf16),
-            pltpu.SemaphoreType.DMA,
-        ],
-        compiler_params=pltpu.CompilerParams(vmem_limit_bytes=12 * 2**20),
-    )(*last_quarter, spread, table, started)
-    return new_master, weights_full
+    )(*packs, *bands, master, cols, table)
 
 
 def send(array, axis, perm):
@@ -346,46 +330,46 @@
         mom,
         jnp.asarray(np.tile(table.T, (1, 8)), f32),
         jnp.asarray(table, f32),
-        w0,
-        wz,
     )
 
     got = send(band, "zl", EVEN4)
+    up, down = enclosed(w0, wz, up, down)
     left = send(up, "x", UP4)
     right = send(down, "x", DOWN4)
 
     band = band + got
+    got = send(band, "y", EVEN4)
+
+    band = band + got
+    got = send(band, "y", ODD4)
+
+    band, left, right = together((band + got, left, right))
     got = send(band, "zl", XOR2)
-
-    band = band + got
-    got = send(band, z, CROSS8)
-
-    band, left, right = together((band + got, left, right))
-    got = send(band, "y", EVEN4)
     passed = jax.ShapeDtypeStruct((2 * HALF + QUARTER, GROUP), bf16)
     up, down = small_call(pass_on_kernel, [passed] * 2, keep_up, keep_down, left, right)
     last_left = send(up, "x", UP4)
     last_right = send(down, "x", DOWN4)
 
     band, last_left, last_right = together((band + got, last_left, last_right))
-    got = send(band, "y", ODD4)
+    got = send(band, z, CROSS8)
     parts = (mine, left, right, last_left, last_right)
-    z_send = small_call(z_send_kernel, jax.ShapeDtypeStruct(half, bf16), *parts)
-    from_z = send(z_send, "zh", SWAP2)
     eighth = small_call(
         collect_kernel, jax.ShapeDtypeStruct((8, QUARTER, GROUP), bf16), w0, wz, *parts[1:]
     )
-    wc = send(eighth, "core", SWAP2)
-
-    band, eighth, wc = together((band + got, eighth, wc))
+    below = send(eighth, "y", UP4)
+    above = send(eighth, "y", DOWN4)
+    z_send = small_call(z_send_kernel, jax.ShapeDtypeStruct(half, bf16), *parts)
+
+    band, z_send = together((band + got, z_send))
     got = send(band, "x", EVEN4)
-    quarter = joined(eighth, wc)
-    near = send(quarter, ("y", "core"), SPREAD8)
-
-    band, from_z, near = together((band + got, from_z, near))
+    from_z = send(z_send, "zh", SWAP2)
+
+    band, eighth, below, above = together((band + got, eighth, below, above))
     got = send(band, "x", ODD4)
-    far = send(near[:8], ("y", "core"), SPREAD8)
-    near_other = send(near, "core", SWAP2)
+    four = jax.ShapeDtypeStruct((4, QUARTER, GROUP), bf16)
+    up, down = small_call(half_kernel, [four] * 2, below, above)
+    low = send(up, "y", UP4)
+    high = send(down, "y", DOWN4)
     new_momentum = small_call(
         remaining_kernel,
         jax.ShapeDtypeStruct(half, f32),
@@ -393,17 +377,19 @@
         from_z,
         mom,
         jnp.asarray(table.T @ table, f32),
-    )
-
-    band = (band + got) * (-step_size / replicas)
-    band, new_momentum, near_other = together((band, new_momentum, near_other))
+        cost=pl.CostEstimate(flops=8000000000, bytes_accessed=2000000, transcendentals=0),
+    )
+
+    band, low, high, new_momentum = together(
+        ((band + got) * (-step_size / replicas), low, high, new_momentum)
+    )
     band_other = send(band, "core", SWAP2)
-
-    band, band_other, far = together((band, band_other, far))
-    far_other = send(far, "core", SWAP2)
+    early = packed(eighth, below, above)
+    early_other = send(early, "core", SWAP2)
+    late = packed(low, high)
+    late_other = send(late, "core", SWAP2)
     new_master, weights_full = weights_of(
-        (quarter, near, near_other),
-        (far, far_other),
+        (early, early_other, late, late_other),
         (band, band_other),
         master_weights,
         jnp.asarray(np.kron(np.eye(8), table.T), bf16),

time: 87 us -> 80.7 us (0.928)
  waiting for transfers between devices: 34.7 us -> 31.9 us
  starting transfers between devices: 37.5 us -> 35.3 us
  Pallas kernels: 10.9 us -> 9.93 us
    ppermute x20 -> x21, waiting for transfers between devices: 34.7 us -> 31.9 us  [send(): return lax.ppermute(array, axis, perm)]
    ppermute x20 -> x21, starting transfers between devices: 37.5 us -> 35.3 us  [send(): return lax.ppermute(array, axis, perm)]
    pallas_call x3, Pallas kernels: 7.48 us -> 6.37 us  [the longest x1 4.34 us: weights_of(): pl.pallas_call(weights_kernel, out_shape=[jax.ShapeDtypeStruct((ROWS, GRO...]
    pallas_call x6 -> x8, Pallas kernels: 2.32 us -> 2.42 us  [small_call(): pl.pallas_call(kernel, out_shape=shapes, in_specs=[vmem] * len(args), out...]
  transfers between devices with their start and end apart: 20 -> 21, of which waited for: 11 -> 11; matrix products, arithmetic and copies ran while one was open for 0% -> 0% of each run, Pallas kernels for 7% -> 5%
where the time goes in v4:
time: 80.7 us; the launch traced here: 80.4 us
  starting transfers between devices  35.3 us (44%)
  waiting for transfers between devices  31.9 us (40%)
  Pallas kernels  9.93 us (12%)
  local copies, waits for them, and re-layouts  2.21 us (3%)
  between operations  0.94 us (1%)
    ppermute x21, starting transfers between devices, send(): return lax.ppermute(array, axis, perm)  35.3 us
    ppermute x21, waiting for transfers between devices, send(): return lax.ppermute(array, axis, perm)  31.9 us
    pallas_call x1, Pallas kernels, weights_of(): pl.pallas_call(weights_kernel, out_shape=[jax.ShapeDtypeStruct((ROWS, GRO...  4.34 us
    pallas_call x8, Pallas kernels, small_call(): pl.pallas_call(kernel, out_shape=shapes, in_specs=[vmem] * len(args), out...  2.42 us
    unnamed x16, local copies, waits for them, and re-layouts  2.21 us
    pallas_call x1, Pallas kernels, pair_sum(): pl.pallas_call(pair_sum_kernel, out_shape=shapes, in_specs=[vmem] * 5, ou...  1.99 us
  transfers between devices with their start and end apart: 21, of which 11 were waited for; matrix products, arithmetic and copies ran while one was open for 0% of the time, Pallas kernels for 5%

profile of v4, /device:TPU:33, one launch (start us, length us, event | category | flops | bytes accessed | tf_op | source)
XLA Modules:
  0.0 80.4 jit_solution(4606825718965932929)
XLA Ops:
  0.6 2.2 %copy-done = bf16[1,1,1024,2048]{3,2,1,0:T(8,128)(2,1)S(1)} copy-done((bf16[1,1,1024,2048]{3,2,1,0:T(8,128)(2,1)S(1)}, bf16[1,1,1024,2048]{3,2,1,0:T(8,128)(2,1)}, u32[]{:S(2)}) %copy-start) | copy-done | bytes 4194328
  4.8 5.2 %collective-permute-start.4 = (bf16[256,128]{1,0:T(8,128)(2,1)S(1)}, bf16[256,128]{1,0:T(8,128)(2,1)S(1)}, u32[]{:S(2)}, u32[]{:S(2)}) collective-permute-start(bf16[256,128]{1,0:T(8,128)(2,1)S(1)} %shard_map.105.w0_ref), channel_id=1, source_target_pairs={{0,34},{2,32},{16,50},{18,48},{32,2},{34,0},{48,18},{50,16},{1,35}... | collective-permute-start | bytes 196616 | tf_op jit(solution)/shard_map/ppermute | solution.py:311
  10.0 2.0 %shard_map.104 = (bf16[5,512,128]{2,1,0:T(8,128)(2,1)S(1)}, bf16[5,512,128]{2,1,0:T(8,128)(2,1)S(1)}, bf16[2,512,128]{2,1,0:T(8,128)(2,1)S(1)}, bf16[2,512,128]{...) custom-call(bf16[8,1024,128]{2,1,0:T(8,128)(2,1)S(1)} %get-tuple-element.35.own_ref, ...), custom_call_target="tpu_custom_call" | custom-call | tf_op jit(solution)/shard_map/pallas_call | solution.py:124
  12.0 1.8 %collective-permute-done.4.wz_ref = bf16[256,128]{1,0:T(8,128)(2,1)S(1)} collective-permute-done((bf16[256,128]{1,0:T(8,128)(2,1)S(1)}, bf16[256,128]{1,0:T(8,128)(2,1)S(1)}, u32[]{:S(2)}, u32[]{:S(2)}) %collective-permute-start.4) | collective-permute-done | bytes 65568 | tf_op jit(solution)/shard_map/ppermute | solution.py:311
  15.1 1.5 %collective-permute-start.6 = (bf16[5,512,128]{2,1,0:T(8,128)(2,1)S(1)}, bf16[5,512,128]{2,1,0:T(8,128)(2,1)S(1)}, u32[]{:S(2)}, u32[]{:S(2)}) collective-permute-start(bf16[5,512,128]{2,1,0:T(8,128)(2,1)S(1)} %get-tuple-element.41), channel_id=1, source_target_pairs={{0,12},{4,0},{8,4},{12,8},{1,13},{5,1},{9,5},{13,9},{2,14},{6,2},{... | collective-permute-start | bytes 1966088 | tf_op jit(solution)/shard_map/ppermute | solution.py:311
  16.6 3.4 %collective-permute-done.1 = f32[128,128]{1,0:T(8,128)S(1)} collective-permute-done((f32[128,128]{1,0:T(8,128)S(1)}, f32[128,128]{1,0:T(8,128)S(1)}, u32[]{:S(2)}, u32[]{:S(2)}) %collective-permute-start.1) | collective-permute-done | bytes 65568 | tf_op jit(solution)/shard_map/ppermute | solution.py:311
  21.4 2.1 %collective-permute-done.2 = f32[128,128]{1,0:T(8,128)S(1)} collective-permute-done((f32[128,128]{1,0:T(8,128)S(1)}, f32[128,128]{1,0:T(8,128)S(1)}, u32[]{:S(2)}, u32[]{:S(2)}) %collective-permute-start.2) | collective-permute-done | bytes 65568 | tf_op jit(solution)/shard_map/ppermute | solution.py:311
  23.5 2.8 %collective-permute-start.3 = (f32[128,128]{1,0:T(8,128)S(1)}, f32[128,128]{1,0:T(8,128)S(1)}, u32[]{:S(2)}, u32[]{:S(2)}) collective-permute-start(f32[128,128]{1,0:T(8,128)S(1)} %add.22), channel_id=1, source_target_pairs={{64,128},{128,64},{192,0},{0,192},{65,129},{129,65},{193,1},{1,193... | collective-permute-start | bytes 196616 | tf_op jit(solution)/shard_map/ppermute | solution.py:311
  26.4 2.0 %collective-permute-done.3 = f32[128,128]{1,0:T(8,128)S(1)} collective-permute-done((f32[128,128]{1,0:T(8,128)S(1)}, f32[128,128]{1,0:T(8,128)S(1)}, u32[]{:S(2)}, u32[]{:S(2)}) %collective-permute-start.3) | collective-permute-done | bytes 65568 | tf_op jit(solution)/shard_map/ppermute | solution.py:311
  28.3 2.5 %collective-permute-done.5.left_ref.refs_1_ = bf16[5,512,128]{2,1,0:T(8,128)(2,1)S(1)} collective-permute-done((bf16[5,512,128]{2,1,0:T(8,128)(2,1)S(1)}, bf16[5,512,128]{2,1,0:T(8,128)(2,1)S(1)}, u32[]{:S(2)}, u32[]{:S(2)}) %collective-permute-start.5) | collective-permute-done | bytes 655392 | tf_op jit(solution)/shard_map/ppermute | solution.py:311
  31.9 1.8 %collective-permute-start.9 = (bf16[1280,128]{1,0:T(8,128)(2,1)S(1)}, bf16[1280,128]{1,0:T(8,128)(2,1)S(1)}, u32[]{:S(2)}, u32[]{:S(2)}) collective-permute-start(bf16[1280,128]{1,0:T(8,128)(2,1)S(1)} %get-tuple-element.48), channel_id=1, source_target_pairs={{0,12},{4,0},{8,4},{12,8},{1,13},{5,1},{9,5},{13,9},{2,14},{6,2},{... | collective-permute-start | bytes 983048 | tf_op jit(solution)/shard_map/ppermute | solution.py:311
  33.7 4.3 %collective-permute-done.7 = f32[128,128]{1,0:T(8,128)S(1)} collective-permute-done((f32[128,128]{1,0:T(8,128)S(1)}, f32[128,128]{1,0:T(8,128)S(1)}, u32[]{:S(2)}, u32[]{:S(2)}) %collective-permute-start.7) | collective-permute-done | bytes 65568 | tf_op jit(solution)/shard_map/ppermute | solution.py:311
  38.0 1.9 %collective-permute-done.8.refs_3_.last_left_ref = bf16[1280,128]{1,0:T(8,128)(2,1)S(1)} collective-permute-done((bf16[1280,128]{1,0:T(8,128)(2,1)S(1)}, bf16[1280,128]{1,0:T(8,128)(2,1)S(1)}, u32[]{:S(2)}, u32[]{:S(2)}) %collective-permute-start.8) | collective-permute-done | bytes 327712 | tf_op jit(solution)/shard_map/ppermute | solution.py:311
  40.0 2.8 %collective-permute-start.13 = (bf16[8,256,128]{2,1,0:T(8,128)(2,1)S(1)}, bf16[8,256,128]{2,1,0:T(8,128)(2,1)S(1)}, u32[]{:S(2)}, u32[]{:S(2)}) collective-permute-start(bf16[8,256,128]{2,1,0:T(8,128)(2,1)S(1)} %shard_map.109.refs_0_), channel_id=1, source_target_pairs={{0,192},{64,0},{128,64},{192,128},{1,193},{65,1},{129,65},{193,129... | collective-permute-start | bytes 1572872 | tf_op jit(solution)/shard_map/ppermute | solution.py:311
  44.0 4.5 %collective-permute-done.10 = f32[128,128]{1,0:T(8,128)S(1)} collective-permute-done((f32[128,128]{1,0:T(8,128)S(1)}, f32[128,128]{1,0:T(8,128)S(1)}, u32[]{:S(2)}, u32[]{:S(2)}) %collective-permute-start.10) | collective-permute-done | bytes 65568 | tf_op jit(solution)/shard_map/ppermute | solution.py:311
  48.5 3.6 %collective-permute-start.17 = (bf16[1024,128]{1,0:T(8,128)(2,1)S(1)}, bf16[1024,128]{1,0:T(8,128)(2,1)S(1)}, u32[]{:S(2)}, u32[]{:S(2)}) collective-permute-start(bf16[1024,128]{1,0:T(8,128)(2,1)S(1)} %shard_map.108), channel_id=1, source_target_pairs={{0,2},{2,0},{1,3},{3,1},{4,6},{6,4},{5,7},{7,5},{8,10},{10,8},{9,1... | collective-permute-start | bytes 786440 | tf_op jit(solution)/shard_map/ppermute | solution.py:311
  52.1 3.4 %collective-permute-done.11 = f32[128,128]{1,0:T(8,128)S(1)} collective-permute-done((f32[128,128]{1,0:T(8,128)S(1)}, f32[128,128]{1,0:T(8,128)S(1)}, u32[]{:S(2)}, u32[]{:S(2)}) %collective-permute-start.11) | collective-permute-done | bytes 65568 | tf_op jit(solution)/shard_map/ppermute | solution.py:311
  55.7 5.3 %collective-permute-start.18 = (bf16[24,256,128]{2,1,0:T(8,128)(2,1)S(1)}, bf16[24,256,128]{2,1,0:T(8,128)(2,1)S(1)}, u32[]{:S(2)}, u32[]{:S(2)}) collective-permute-start(bf16[24,256,128]{2,1,0:T(8,128)(2,1)S(1)} %shard_map.112.refs_0_), channel_id=1, source_target_pairs={{0,1},{1,0},{2,3},{3,2},{4,5},{5,4},{6,7},{7,6},{8,9},{9,8},{10,11... | collective-permute-start | bytes 4718600 | tf_op jit(solution)/shard_map/ppermute | solution.py:311
  61.0 2.8 %collective-permute-start.14 = (f32[128,128]{1,0:T(8,128)S(1)}, f32[128,128]{1,0:T(8,128)S(1)}, u32[]{:S(2)}, u32[]{:S(2)}) collective-permute-start(f32[128,128]{1,0:T(8,128)S(1)} %add.26), channel_id=1, source_target_pairs={{4,8},{8,4},{12,0},{0,12},{5,9},{9,5},{13,1},{1,13},{6,10},{10,6},... | collective-permute-start | bytes 196616 | tf_op jit(solution)/shard_map/ppermute | solution.py:311
  64.2 2.6 %collective-permute-start.16 = (bf16[4,256,128]{2,1,0:T(8,128)(2,1)S(1)}, bf16[4,256,128]{2,1,0:T(8,128)(2,1)S(1)}, u32[]{:S(2)}, u32[]{:S(2)}) collective-permute-start(bf16[4,256,128]{2,1,0:T(8,128)(2,1)S(1)} %get-tuple-element.58), channel_id=1, source_target_pairs={{0,192},{64,0},{128,64},{192,128},{1,193},{65,1},{129,65},{193,129... | collective-permute-start | bytes 786440 | tf_op jit(solution)/shard_map/ppermute | solution.py:311
  66.8 2.0 %shard_map.111 = f32[1024,128]{1,0:T(8,128)} custom-call(bf16[2,1024,128]{2,1,0:T(8,128)(2,1)S(1)} %get-tuple-element.50.refs_0_, bf16[5,512,128]{2,1,0:T(8,128)(2,1)S(1)} %collective-permute-done.5.left_ref.refs_1_, bf16[5,512,128]{2,1,0:T(8,128)(2,1)S(1)} %collective-permute-done.6.right_ref.refs_2_, ...), custom_call_target="tpu_custom_call" | custom-call | flops 8000000000 | bytes 2000000 | tf_op jit(solution)/shard_map/pallas_call | solution.py:136
  68.8 4.4 %collective-permute-done.15.refs_0_ = bf16[4,256,128]{2,1,0:T(8,128)(2,1)S(1)} collective-permute-done((bf16[4,256,128]{2,1,0:T(8,128)(2,1)S(1)}, bf16[4,256,128]{2,1,0:T(8,128)(2,1)S(1)}, u32[]{:S(2)}, u32[]{:S(2)}) %collective-permute-start.15) | collective-permute-done | bytes 262176 | tf_op jit(solution)/shard_map/ppermute | solution.py:311
  74.3 1.5 %collective-permute-done.20.refs_5_ = f32[128,128]{1,0:T(8,128)S(1)} collective-permute-done((f32[128,128]{1,0:T(8,128)S(1)}, f32[128,128]{1,0:T(8,128)S(1)}, u32[]{:S(2)}, u32[]{:S(2)}) %collective-permute-start.20) | collective-permute-done | bytes 65568 | tf_op jit(solution)/shard_map/ppermute | solution.py:311
  75.9 4.3 %shard_map.114 = (f32[1024,128]{1,0:T(8,128)}, bf16[1024,2048]{1,0:T(8,128)(2,1)}) custom-call(bf16[24,256,128]{2,1,0:T(8,128)(2,1)S(1)} %shard_map.112.refs_0_, bf16[24,256,128]{2,1,0:T(8,128)(2,1)S(1)} %collective-permute-done.18.refs_1_, bf16[8,256,128]{2,1,0:T(8,128)(2,1)S(1)} %shard_map.113.refs_2_, ...), custom_call_target="tpu_custom_call" | custom-call | tf_op jit(solution)/shard_map/pallas_call | solution.py:293
  (53 shorter events, 8.6 us)
Async XLA Ops:
  4.0 6.0 %collective-permute-start = (bf16[8,1024,128]{2,1,0:T(8,128)(2,1)S(1)}, bf16[8,1024,128]{2,1,0:T(8,128)(2,1)S(1)}, u32[]{:S(2)}, u32[]{:S(2)}) collective-permute-start(bf16[8,1024,128]{2,1,0:T(8,128)(2,1)S(1)} %get-tuple-element.36), channel_id=1, source_target_pairs={{0,1},{1,0},{2,3},{3,2},{4,5},{5,4},{6,7},{7,6},{8,9},{9,8},{10,11... | collective-permute-start | bytes 6291464 | tf_op jit(solution)/shard_map/ppermute | solution.py:311
  4.8 9.0 %collective-permute-start.4 = (bf16[256,128]{1,0:T(8,128)(2,1)S(1)}, bf16[256,128]{1,0:T(8,128)(2,1)S(1)}, u32[]{:S(2)}, u32[]{:S(2)}) collective-permute-start(bf16[256,128]{1,0:T(8,128)(2,1)S(1)} %shard_map.105.w0_ref), channel_id=1, source_target_pairs={{0,34},{2,32},{16,50},{18,48},{32,2},{34,0},{48,18},{50,16},{1,35}... | collective-permute-start | bytes 196616 | tf_op jit(solution)/shard_map/ppermute | solution.py:311
  13.8 17.0 %collective-permute-start.5 = (bf16[5,512,128]{2,1,0:T(8,128)(2,1)S(1)}, bf16[5,512,128]{2,1,0:T(8,128)(2,1)S(1)}, u32[]{:S(2)}, u32[]{:S(2)}) collective-permute-start(bf16[5,512,128]{2,1,0:T(8,128)(2,1)S(1)} %get-tuple-element.40), channel_id=1, source_target_pairs={{0,4},{4,8},{8,12},{12,0},{1,5},{5,9},{9,13},{13,1},{2,6},{6,10},{... | collective-permute-start | bytes 1966088 | tf_op jit(solution)/shard_map/ppermute | solution.py:311
  15.1 15.7 %collective-permute-start.6 = (bf16[5,512,128]{2,1,0:T(8,128)(2,1)S(1)}, bf16[5,512,128]{2,1,0:T(8,128)(2,1)S(1)}, u32[]{:S(2)}, u32[]{:S(2)}) collective-permute-start(bf16[5,512,128]{2,1,0:T(8,128)(2,1)S(1)} %get-tuple-element.41), channel_id=1, source_target_pairs={{0,12},{4,0},{8,4},{12,8},{1,13},{5,1},{9,5},{13,9},{2,14},{6,2},{... | collective-permute-start | bytes 1966088 | tf_op jit(solution)/shard_map/ppermute | solution.py:311
  16.6 3.4 %collective-permute-start.1 = (f32[128,128]{1,0:T(8,128)S(1)}, f32[128,128]{1,0:T(8,128)S(1)}, u32[]{:S(2)}, u32[]{:S(2)}) collective-permute-start(f32[128,128]{1,0:T(8,128)S(1)} %get-tuple-element.37), channel_id=1, source_target_pairs={{0,16},{16,0},{32,48},{48,32},{1,17},{17,1},{33,49},{49,33},{2,18}... | collective-permute-start | bytes 196616 | tf_op jit(solution)/shard_map/ppermute | solution.py:311
  20.0 3.5 %collective-permute-start.2 = (f32[128,128]{1,0:T(8,128)S(1)}, f32[128,128]{1,0:T(8,128)S(1)}, u32[]{:S(2)}, u32[]{:S(2)}) collective-permute-start(f32[128,128]{1,0:T(8,128)S(1)} %add.21), channel_id=1, source_target_pairs={{0,64},{64,0},{128,192},{192,128},{1,65},{65,1},{129,193},{193,129... | collective-permute-start | bytes 196616 | tf_op jit(solution)/shard_map/ppermute | solution.py:311
  23.5 4.8 %collective-permute-start.3 = (f32[128,128]{1,0:T(8,128)S(1)}, f32[128,128]{1,0:T(8,128)S(1)}, u32[]{:S(2)}, u32[]{:S(2)}) collective-permute-start(f32[128,128]{1,0:T(8,128)S(1)} %add.22), channel_id=1, source_target_pairs={{64,128},{128,64},{192,0},{0,192},{65,129},{129,65},{193,1},{1,193... | collective-permute-start | bytes 196616 | tf_op jit(solution)/shard_map/ppermute | solution.py:311
  30.9 9.0 %collective-permute-start.8 = (bf16[1280,128]{1,0:T(8,128)(2,1)S(1)}, bf16[1280,128]{1,0:T(8,128)(2,1)S(1)}, u32[]{:S(2)}, u32[]{:S(2)}) collective-permute-start(bf16[1280,128]{1,0:T(8,128)(2,1)S(1)} %get-tuple-element.47), channel_id=1, source_target_pairs={{0,4},{4,8},{8,12},{12,0},{1,5},{5,9},{9,13},{13,1},{2,6},{6,10},{... | collective-permute-start | bytes 983048 | tf_op jit(solution)/shard_map/ppermute | solution.py:311
  31.9 8.1 %collective-permute-start.9 = (bf16[1280,128]{1,0:T(8,128)(2,1)S(1)}, bf16[1280,128]{1,0:T(8,128)(2,1)S(1)}, u32[]{:S(2)}, u32[]{:S(2)}) collective-permute-start(bf16[1280,128]{1,0:T(8,128)(2,1)S(1)} %get-tuple-element.48), channel_id=1, source_target_pairs={{0,12},{4,0},{8,4},{12,8},{1,13},{5,1},{9,5},{13,9},{2,14},{6,2},{... | collective-permute-start | bytes 983048 | tf_op jit(solution)/shard_map/ppermute | solution.py:311
  33.7 4.3 %collective-permute-start.7 = (f32[128,128]{1,0:T(8,128)S(1)}, f32[128,128]{1,0:T(8,128)S(1)}, u32[]{:S(2)}, u32[]{:S(2)}) collective-permute-start(f32[128,128]{1,0:T(8,128)S(1)} %add.23), channel_id=1, source_target_pairs={{0,32},{16,48},{32,0},{48,16},{1,33},{17,49},{33,1},{49,17},{2,34}... | collective-permute-start | bytes 196616 | tf_op jit(solution)/shard_map/ppermute | solution.py:311
  40.0 15.6 %collective-permute-start.13 = (bf16[8,256,128]{2,1,0:T(8,128)(2,1)S(1)}, bf16[8,256,128]{2,1,0:T(8,128)(2,1)S(1)}, u32[]{:S(2)}, u32[]{:S(2)}) collective-permute-start(bf16[8,256,128]{2,1,0:T(8,128)(2,1)S(1)} %shard_map.109.refs_0_), channel_id=1, source_target_pairs={{0,192},{64,0},{128,64},{192,128},{1,193},{65,1},{129,65},{193,129... | collective-permute-start | bytes 1572872 | tf_op jit(solution)/shard_map/ppermute | solution.py:311
  42.8 12.8 %collective-permute-start.12 = (bf16[8,256,128]{2,1,0:T(8,128)(2,1)S(1)}, bf16[8,256,128]{2,1,0:T(8,128)(2,1)S(1)}, u32[]{:S(2)}, u32[]{:S(2)}) collective-permute-start(bf16[8,256,128]{2,1,0:T(8,128)(2,1)S(1)} %shard_map.109.refs_0_), channel_id=1, source_target_pairs={{0,64},{64,128},{128,192},{192,0},{1,65},{65,129},{129,193},{193,1... | collective-permute-start | bytes 1572872 | tf_op jit(solution)/shard_map/ppermute | solution.py:311
  42.8 5.7 %collective-permute-start.10 = (f32[128,128]{1,0:T(8,128)S(1)}, f32[128,128]{1,0:T(8,128)S(1)}, u32[]{:S(2)}, u32[]{:S(2)}) collective-permute-start(f32[128,128]{1,0:T(8,128)S(1)} %add.24), channel_id=1, source_target_pairs={{0,34},{2,32},{16,50},{18,48},{32,2},{34,0},{48,18},{50,16},{1,35}... | collective-permute-start | bytes 196616 | tf_op jit(solution)/shard_map/ppermute | solution.py:311
  48.5 18.3 %collective-permute-start.17 = (bf16[1024,128]{1,0:T(8,128)(2,1)S(1)}, bf16[1024,128]{1,0:T(8,128)(2,1)S(1)}, u32[]{:S(2)}, u32[]{:S(2)}) collective-permute-start(bf16[1024,128]{1,0:T(8,128)(2,1)S(1)} %shard_map.108), channel_id=1, source_target_pairs={{0,2},{2,0},{1,3},{3,1},{4,6},{6,4},{5,7},{7,5},{8,10},{10,8},{9,1... | collective-permute-start | bytes 786440 | tf_op jit(solution)/shard_map/ppermute | solution.py:311
  52.1 3.4 %collective-permute-start.11 = (f32[128,128]{1,0:T(8,128)S(1)}, f32[128,128]{1,0:T(8,128)S(1)}, u32[]{:S(2)}, u32[]{:S(2)}) collective-permute-start(f32[128,128]{1,0:T(8,128)S(1)} %add.25), channel_id=1, source_target_pairs={{0,4},{4,0},{8,12},{12,8},{1,5},{5,1},{9,13},{13,9},{2,6},{6,2},{1... | collective-permute-start | bytes 196616 | tf_op jit(solution)/shard_map/ppermute | solution.py:311
  55.5 11.3 %copy-start.7 = (f32[128,128]{1,0:T(8,128)S(1)}, f32[128,128]{1,0:T(8,128)}, u32[]{:S(2)}) copy-start(f32[128,128]{1,0:T(8,128)} %constant.14.clone.refs_7_) | copy-start | bytes 196612
  55.7 20.2 %collective-permute-start.18 = (bf16[24,256,128]{2,1,0:T(8,128)(2,1)S(1)}, bf16[24,256,128]{2,1,0:T(8,128)(2,1)S(1)}, u32[]{:S(2)}, u32[]{:S(2)}) collective-permute-start(bf16[24,256,128]{2,1,0:T(8,128)(2,1)S(1)} %shard_map.112.refs_0_), channel_id=1, source_target_pairs={{0,1},{1,0},{2,3},{3,2},{4,5},{5,4},{6,7},{7,6},{8,9},{9,8},{10,11... | collective-permute-start | bytes 4718600 | tf_op jit(solution)/shard_map/ppermute | solution.py:311
  61.0 7.8 %collective-permute-start.14 = (f32[128,128]{1,0:T(8,128)S(1)}, f32[128,128]{1,0:T(8,128)S(1)}, u32[]{:S(2)}, u32[]{:S(2)}) collective-permute-start(f32[128,128]{1,0:T(8,128)S(1)} %add.26), channel_id=1, source_target_pairs={{4,8},{8,4},{12,0},{0,12},{5,9},{9,5},{13,1},{1,13},{6,10},{10,6},... | collective-permute-start | bytes 196616 | tf_op jit(solution)/shard_map/ppermute | solution.py:311
  63.9 9.4 %collective-permute-start.15 = (bf16[4,256,128]{2,1,0:T(8,128)(2,1)S(1)}, bf16[4,256,128]{2,1,0:T(8,128)(2,1)S(1)}, u32[]{:S(2)}, u32[]{:S(2)}) collective-permute-start(bf16[4,256,128]{2,1,0:T(8,128)(2,1)S(1)} %get-tuple-element.57), channel_id=1, source_target_pairs={{0,64},{64,128},{128,192},{192,0},{1,65},{65,129},{129,193},{193,1... | collective-permute-start | bytes 786440 | tf_op jit(solution)/shard_map/ppermute | solution.py:311
  64.2 11.7 %copy-start.3 = (bf16[1024,128]{1,0:T(8,128)(2,1)S(1)}, bf16[1024,128]{1,0:T(8,128)(2,1)}, u32[]{:S(2)}) copy-start(bf16[1024,128]{1,0:T(8,128)(2,1)} %constant.15.clone.refs_7_) | copy-start | bytes 786436
  64.2 11.7 %copy-start.4 = (f32[128,128]{1,0:T(8,128)S(1)}, f32[128,128]{1,0:T(8,128)}, u32[]{:S(2)}) copy-start(f32[128,128]{1,0:T(8,128)} %constant.16.clone.refs_8_) | copy-start | bytes 196612
  64.2 9.1 %collective-permute-start.16 = (bf16[4,256,128]{2,1,0:T(8,128)(2,1)S(1)}, bf16[4,256,128]{2,1,0:T(8,128)(2,1)S(1)}, u32[]{:S(2)}, u32[]{:S(2)}) collective-permute-start(bf16[4,256,128]{2,1,0:T(8,128)(2,1)S(1)} %get-tuple-element.58), channel_id=1, source_target_pairs={{0,192},{64,0},{128,64},{192,128},{1,193},{65,1},{129,65},{193,129... | collective-permute-start | bytes 786440 | tf_op jit(solution)/shard_map/ppermute | solution.py:311
  73.3 2.5 %collective-permute-start.19 = (bf16[8,256,128]{2,1,0:T(8,128)(2,1)S(1)}, bf16[8,256,128]{2,1,0:T(8,128)(2,1)S(1)}, u32[]{:S(2)}, u32[]{:S(2)}) collective-permute-start(bf16[8,256,128]{2,1,0:T(8,128)(2,1)S(1)} %shard_map.113.refs_2_), channel_id=1, source_target_pairs={{0,1},{1,0},{2,3},{3,2},{4,5},{5,4},{6,7},{7,6},{8,9},{9,8},{10,11... | collective-permute-start | bytes 1572872 | tf_op jit(solution)/shard_map/ppermute | solution.py:311
  74.2 1.6 %collective-permute-start.20 = (f32[128,128]{1,0:T(8,128)S(1)}, f32[128,128]{1,0:T(8,128)S(1)}, u32[]{:S(2)}, u32[]{:S(2)}) collective-permute-start(f32[128,128]{1,0:T(8,128)S(1)} %add_multiply_fusion.refs_4_), channel_id=1, source_target_pairs={{0,1},{1,0},{2,3},{3,2},{4,5},{5,4},{6,7},{7,6},{8,9},{9,8},{10,11... | collective-permute-start | bytes 196616 | tf_op jit(solution)/shard_map/ppermute | solution.py:311
  (5 other events, 25.6 us)

commit v5 on v4

--- a/solution.py
+++ b/solution.py
@@ -259,7 +259,7 @@
 
     coeffs = jnp.concatenate([band_ref[...], band_other_ref[...]], axis=1)
     spread_ref[...] = jnp.dot(
-        cols_ref[...], coeffs.astype(bf16), preferred_element_type=f32
+        cols_ref[...], coeffs, preferred_element_type=f32
     ).astype(bf16)
 
     copies = []
@@ -314,6 +314,10 @@
 together = lax.optimization_barrier
 
 
+def both(own, got):
+    return own.astype(f32) + got.astype(f32)
+
+
 def local(gradients, momentum, master_weights):
     table = cosine_rows()
     mom = momentum[0]
@@ -332,25 +336,30 @@
         jnp.asarray(table, f32),
     )
 
+    band = band.astype(bf16)
     got = send(band, "zl", EVEN4)
     up, down = enclosed(w0, wz, up, down)
     left = send(up, "x", UP4)
     right = send(down, "x", DOWN4)
 
-    band = band + got
+    band = both(band, got)
+    band = band.astype(bf16)
     got = send(band, "y", EVEN4)
 
-    band = band + got
+    band = both(band, got)
+    band = band.astype(bf16)
     got = send(band, "y", ODD4)
 
-    band, left, right = together((band + got, left, right))
+    band, left, right = together((both(band, got), left, right))
+    band = band.astype(bf16)
     got = send(band, "zl", XOR2)
     passed = jax.ShapeDtypeStruct((2 * HALF + QUARTER, GROUP), bf16)
     up, down = small_call(pass_on_kernel, [passed] * 2, keep_up, keep_down, left, right)
     last_left = send(up, "x", UP4)
     last_right = send(down, "x", DOWN4)
 
-    band, last_left, last_right = together((band + got, last_left, last_right))
+    band, last_left, last_right = together((both(band, got), last_left, last_right))
+    band = band.astype(bf16)
     got = send(band, z, CROSS8)
     parts = (mine, left, right, last_left, last_right)
     eighth = small_call(
@@ -360,11 +369,13 @@
     above = send(eighth, "y", DOWN4)
     z_send = small_call(z_send_kernel, jax.ShapeDtypeStruct(half, bf16), *parts)
 
-    band, z_send = together((band + got, z_send))
+    band, z_send = together((both(band, got), z_send))
+    band = band.astype(bf16)
     got = send(band, "x", EVEN4)
     from_z = send(z_send, "zh", SWAP2)
 
-    band, eighth, below, above = together((band + got, eighth, below, above))
+    band, eighth, below, above = together((both(band, got), eighth, below, above))
+    band = band.astype(bf16)
     got = send(band, "x", ODD4)
     four = jax.ShapeDtypeStruct((4, QUARTER, GROUP), bf16)
     up, down = small_call(half_kernel, [four] * 2, below, above)
@@ -381,8 +392,9 @@
     )
 
     band, low, high, new_momentum = together(
-        ((band + got) * (-step_size / replicas), low, high, new_momentum)
-    )
+        ((both(band, got)) * (-step_size / replicas), low, high, new_momentum)
+    )
+    band = band.astype(bf16)
     band_other = send(band, "core", SWAP2)
     early = packed(eighth, below, above)
     early_other = send(early, "core", SWAP2)

time: 80.7 us -> 77.4 us (0.959)
  waiting for transfers between devices: 31.9 us -> 27.8 us
  starting transfers between devices: 35.3 us -> 36.3 us
    ppermute x21, waiting for transfers between devices: 31.9 us -> 27.8 us  [send(): return lax.ppermute(array, axis, perm)]
    ppermute x21, starting transfers between devices: 35.3 us -> 36.3 us  [send(): return lax.ppermute(array, axis, perm)]
  transfers between devices with their start and end apart: 21 -> 21, of which waited for: 11 -> 10; matrix products, arithmetic and copies ran while one was open for 0% -> 0% of each run, Pallas kernels for 5% -> 6%
where the time goes in v5:
time: 77.4 us; the launch traced here: 77.2 us
  starting transfers between devices  36.3 us (47%)
  waiting for transfers between devices  27.8 us (36%)
  Pallas kernels  9.94 us (13%)
  local copies, waits for them, and re-layouts  2.21 us (3%)
  between operations  0.93 us (1%)
    ppermute x21, starting transfers between devices, send(): return lax.ppermute(array, axis, perm)  36.3 us
    ppermute x21, waiting for transfers between devices, send(): return lax.ppermute(array, axis, perm)  27.8 us
    pallas_call x1, Pallas kernels, weights_of(): pl.pallas_call(weights_kernel, out_shape=[jax.ShapeDtypeStruct((ROWS, GRO...  4.35 us
    pallas_call x8, Pallas kernels, small_call(): pl.pallas_call(kernel, out_shape=shapes, in_specs=[vmem] * len(args), out...  2.42 us
    unnamed x16, local copies, waits for them, and re-layouts  2.21 us
    pallas_call x1, Pallas kernels, pair_sum(): pl.pallas_call(pair_sum_kernel, out_shape=shapes, in_specs=[vmem] * 5, ou...  1.99 us
  transfers between devices with their start and end apart: 21, of which 10 were waited for; matrix products, arithmetic and copies ran while one was open for 0% of the time, Pallas kernels for 6%

profile of v5, /device:TPU:33, one launch (start us, length us, event | category | flops | bytes accessed | tf_op | source)
XLA Modules:
  0.0 77.2 jit_solution(13879148478200604241)
XLA Ops:
  0.6 2.2 %copy-done = bf16[1,1,1024,2048]{3,2,1,0:T(8,128)(2,1)S(1)} copy-done((bf16[1,1,1024,2048]{3,2,1,0:T(8,128)(2,1)S(1)}, bf16[1,1,1024,2048]{3,2,1,0:T(8,128)(2,1)}, u32[]{:S(2)}) %copy-start) | copy-done | bytes 4194328
  4.8 5.2 %collective-permute-start.4 = (bf16[256,128]{1,0:T(8,128)(2,1)S(1)}, bf16[256,128]{1,0:T(8,128)(2,1)S(1)}, u32[]{:S(2)}, u32[]{:S(2)}) collective-permute-start(bf16[256,128]{1,0:T(8,128)(2,1)S(1)} %shard_map.105.w0_ref), channel_id=1, source_target_pairs={{0,34},{2,32},{16,50},{18,48},{32,2},{34,0},{48,18},{50,16},{1,35}... | collective-permute-start | bytes 196616 | tf_op jit(solution)/shard_map/ppermute | solution.py:311
  10.0 2.0 %shard_map.104 = (bf16[5,512,128]{2,1,0:T(8,128)(2,1)S(1)}, bf16[5,512,128]{2,1,0:T(8,128)(2,1)S(1)}, bf16[2,512,128]{2,1,0:T(8,128)(2,1)S(1)}, bf16[2,512,128]{...) custom-call(bf16[8,1024,128]{2,1,0:T(8,128)(2,1)S(1)} %get-tuple-element.35.own_ref, ...), custom_call_target="tpu_custom_call" | custom-call | tf_op jit(solution)/shard_map/pallas_call | solution.py:124
  15.1 1.5 %collective-permute-start.6 = (bf16[5,512,128]{2,1,0:T(8,128)(2,1)S(1)}, bf16[5,512,128]{2,1,0:T(8,128)(2,1)S(1)}, u32[]{:S(2)}, u32[]{:S(2)}) collective-permute-start(bf16[5,512,128]{2,1,0:T(8,128)(2,1)S(1)} %get-tuple-element.41), channel_id=1, source_target_pairs={{0,12},{4,0},{8,4},{12,8},{1,13},{5,1},{9,5},{13,9},{2,14},{6,2},{... | collective-permute-start | bytes 1966088 | tf_op jit(solution)/shard_map/ppermute | solution.py:311
  16.6 1.4 %collective-permute-start.2 = (bf16[128,128]{1,0:T(8,128)(2,1)S(1)}, bf16[128,128]{1,0:T(8,128)(2,1)S(1)}, u32[]{:S(2)}, u32[]{:S(2)}) collective-permute-start(bf16[128,128]{1,0:T(8,128)(2,1)S(1)} %add_convert_fusion.1), channel_id=1, source_target_pairs={{0,64},{64,0},{128,192},{192,128},{1,65},{65,1},{129,193},{193,129... | collective-permute-start | bytes 98312 | tf_op jit(solution)/shard_map/ppermute | solution.py:311
  18.0 1.8 %collective-permute-done.2 = bf16[128,128]{1,0:T(8,128)(2,1)S(1)} collective-permute-done((bf16[128,128]{1,0:T(8,128)(2,1)S(1)}, bf16[128,128]{1,0:T(8,128)(2,1)S(1)}, u32[]{:S(2)}, u32[]{:S(2)}) %collective-permute-start.2) | collective-permute-done | bytes 32800 | tf_op jit(solution)/shard_map/ppermute | solution.py:311
  19.8 2.8 %collective-permute-start.3 = (bf16[128,128]{1,0:T(8,128)(2,1)S(1)}, bf16[128,128]{1,0:T(8,128)(2,1)S(1)}, u32[]{:S(2)}, u32[]{:S(2)}) collective-permute-start(bf16[128,128]{1,0:T(8,128)(2,1)S(1)} %add_convert_fusion), channel_id=1, source_target_pairs={{64,128},{128,64},{192,0},{0,192},{65,129},{129,65},{193,1},{1,193... | collective-permute-start | bytes 98312 | tf_op jit(solution)/shard_map/ppermute | solution.py:311
  22.6 1.6 %collective-permute-done.3 = bf16[128,128]{1,0:T(8,128)(2,1)S(1)} collective-permute-done((bf16[128,128]{1,0:T(8,128)(2,1)S(1)}, bf16[128,128]{1,0:T(8,128)(2,1)S(1)}, u32[]{:S(2)}, u32[]{:S(2)}) %collective-permute-start.3) | collective-permute-done | bytes 32800 | tf_op jit(solution)/shard_map/ppermute | solution.py:311
  24.2 6.6 %collective-permute-done.5.left_ref.refs_1_ = bf16[5,512,128]{2,1,0:T(8,128)(2,1)S(1)} collective-permute-done((bf16[5,512,128]{2,1,0:T(8,128)(2,1)S(1)}, bf16[5,512,128]{2,1,0:T(8,128)(2,1)S(1)}, u32[]{:S(2)}, u32[]{:S(2)}) %collective-permute-start.5) | collective-permute-done | bytes 655392 | tf_op jit(solution)/shard_map/ppermute | solution.py:311
  31.9 1.8 %collective-permute-start.9 = (bf16[1280,128]{1,0:T(8,128)(2,1)S(1)}, bf16[1280,128]{1,0:T(8,128)(2,1)S(1)}, u32[]{:S(2)}, u32[]{:S(2)}) collective-permute-start(bf16[1280,128]{1,0:T(8,128)(2,1)S(1)} %get-tuple-element.48), channel_id=1, source_target_pairs={{0,12},{4,0},{8,4},{12,8},{1,13},{5,1},{9,5},{13,9},{2,14},{6,2},{... | collective-permute-start | bytes 983048 | tf_op jit(solution)/shard_map/ppermute | solution.py:311
  33.7 4.0 %collective-permute-done.7 = bf16[128,128]{1,0:T(8,128)(2,1)S(1)} collective-permute-done((bf16[128,128]{1,0:T(8,128)(2,1)S(1)}, bf16[128,128]{1,0:T(8,128)(2,1)S(1)}, u32[]{:S(2)}, u32[]{:S(2)}) %collective-permute-start.7) | collective-permute-done | bytes 32800 | tf_op jit(solution)/shard_map/ppermute | solution.py:311
  37.7 2.3 %collective-permute-done.8.refs_3_.last_left_ref = bf16[1280,128]{1,0:T(8,128)(2,1)S(1)} collective-permute-done((bf16[1280,128]{1,0:T(8,128)(2,1)S(1)}, bf16[1280,128]{1,0:T(8,128)(2,1)S(1)}, u32[]{:S(2)}, u32[]{:S(2)}) %collective-permute-start.8) | collective-permute-done | bytes 327712 | tf_op jit(solution)/shard_map/ppermute | solution.py:311
  40.0 2.8 %collective-permute-start.13 = (bf16[8,256,128]{2,1,0:T(8,128)(2,1)S(1)}, bf16[8,256,128]{2,1,0:T(8,128)(2,1)S(1)}, u32[]{:S(2)}, u32[]{:S(2)}) collective-permute-start(bf16[8,256,128]{2,1,0:T(8,128)(2,1)S(1)} %shard_map.109.refs_0_), channel_id=1, source_target_pairs={{0,192},{64,0},{128,64},{192,128},{1,193},{65,1},{129,65},{193,129... | collective-permute-start | bytes 1572872 | tf_op jit(solution)/shard_map/ppermute | solution.py:311
  42.8 2.5 %collective-permute-start.10 = (bf16[128,128]{1,0:T(8,128)(2,1)S(1)}, bf16[128,128]{1,0:T(8,128)(2,1)S(1)}, u32[]{:S(2)}, u32[]{:S(2)}) collective-permute-start(bf16[128,128]{1,0:T(8,128)(2,1)S(1)} %convert_add_fusion.2), channel_id=1, source_target_pairs={{0,34},{2,32},{16,50},{18,48},{32,2},{34,0},{48,18},{50,16},{1,35}... | collective-permute-start | bytes 98312 | tf_op jit(solution)/shard_map/ppermute | solution.py:311
  45.4 2.4 %collective-permute-done.10 = bf16[128,128]{1,0:T(8,128)(2,1)S(1)} collective-permute-done((bf16[128,128]{1,0:T(8,128)(2,1)S(1)}, bf16[128,128]{1,0:T(8,128)(2,1)S(1)}, u32[]{:S(2)}, u32[]{:S(2)}) %collective-permute-start.10) | collective-permute-done | bytes 32800 | tf_op jit(solution)/shard_map/ppermute | solution.py:311
  48.1 4.1 %collective-permute-start.17 = (bf16[1024,128]{1,0:T(8,128)(2,1)S(1)}, bf16[1024,128]{1,0:T(8,128)(2,1)S(1)}, u32[]{:S(2)}, u32[]{:S(2)}) collective-permute-start(bf16[1024,128]{1,0:T(8,128)(2,1)S(1)} %shard_map.108), channel_id=1, source_target_pairs={{0,2},{2,0},{1,3},{3,1},{4,6},{6,4},{5,7},{7,5},{8,10},{10,8},{9,1... | collective-permute-start | bytes 786440 | tf_op jit(solution)/shard_map/ppermute | solution.py:311
  52.3 2.5 %collective-permute-done.12.below_ref.refs_1_ = bf16[8,256,128]{2,1,0:T(8,128)(2,1)S(1)} collective-permute-done((bf16[8,256,128]{2,1,0:T(8,128)(2,1)S(1)}, bf16[8,256,128]{2,1,0:T(8,128)(2,1)S(1)}, u32[]{:S(2)}, u32[]{:S(2)}) %collective-permute-start.12) | collective-permute-done | bytes 524320 | tf_op jit(solution)/shard_map/ppermute | solution.py:311
  54.9 3.7 %collective-permute-start.18 = (bf16[24,256,128]{2,1,0:T(8,128)(2,1)S(1)}, bf16[24,256,128]{2,1,0:T(8,128)(2,1)S(1)}, u32[]{:S(2)}, u32[]{:S(2)}) collective-permute-start(bf16[24,256,128]{2,1,0:T(8,128)(2,1)S(1)} %shard_map.112.refs_0_), channel_id=1, source_target_pairs={{0,1},{1,0},{2,3},{3,2},{4,5},{5,4},{6,7},{7,6},{8,9},{9,8},{10,11... | collective-permute-start | bytes 4718600 | tf_op jit(solution)/shard_map/ppermute | solution.py:311
  58.6 2.5 %collective-permute-start.14 = (bf16[128,128]{1,0:T(8,128)(2,1)S(1)}, bf16[128,128]{1,0:T(8,128)(2,1)S(1)}, u32[]{:S(2)}, u32[]{:S(2)}) collective-permute-start(bf16[128,128]{1,0:T(8,128)(2,1)S(1)} %convert_add_fusion), channel_id=1, source_target_pairs={{4,8},{8,4},{12,0},{0,12},{5,9},{9,5},{13,1},{1,13},{6,10},{10,6},... | collective-permute-start | bytes 98312 | tf_op jit(solution)/shard_map/ppermute | solution.py:311
  61.1 2.7 %collective-permute-start.16 = (bf16[4,256,128]{2,1,0:T(8,128)(2,1)S(1)}, bf16[4,256,128]{2,1,0:T(8,128)(2,1)S(1)}, u32[]{:S(2)}, u32[]{:S(2)}) collective-permute-start(bf16[4,256,128]{2,1,0:T(8,128)(2,1)S(1)} %get-tuple-element.58), channel_id=1, source_target_pairs={{0,192},{64,0},{128,64},{192,128},{1,193},{65,1},{129,65},{193,129... | collective-permute-start | bytes 786440 | tf_op jit(solution)/shard_map/ppermute | solution.py:311
  63.8 2.0 %shard_map.111 = f32[1024,128]{1,0:T(8,128)} custom-call(bf16[2,1024,128]{2,1,0:T(8,128)(2,1)S(1)} %get-tuple-element.50.refs_0_, bf16[5,512,128]{2,1,0:T(8,128)(2,1)S(1)} %collective-permute-done.5.left_ref.refs_1_, bf16[5,512,128]{2,1,0:T(8,128)(2,1)S(1)} %collective-permute-done.6.right_ref.refs_2_, ...), custom_call_target="tpu_custom_call" | custom-call | flops 8000000000 | bytes 2000000 | tf_op jit(solution)/shard_map/pallas_call | solution.py:136
  65.8 4.1 %collective-permute-done.15.refs_0_ = bf16[4,256,128]{2,1,0:T(8,128)(2,1)S(1)} collective-permute-done((bf16[4,256,128]{2,1,0:T(8,128)(2,1)S(1)}, bf16[4,256,128]{2,1,0:T(8,128)(2,1)S(1)}, u32[]{:S(2)}, u32[]{:S(2)}) %collective-permute-start.15) | collective-permute-done | bytes 262176 | tf_op jit(solution)/shard_map/ppermute | solution.py:311
  71.2 1.5 %collective-permute-done.20.refs_5_ = bf16[128,128]{1,0:T(8,128)(2,1)S(1)} collective-permute-done((bf16[128,128]{1,0:T(8,128)(2,1)S(1)}, bf16[128,128]{1,0:T(8,128)(2,1)S(1)}, u32[]{:S(2)}, u32[]{:S(2)}) %collective-permute-start.20) | collective-permute-done | bytes 32800 | tf_op jit(solution)/shard_map/ppermute | solution.py:311
  72.7 4.4 %shard_map.114 = (f32[1024,128]{1,0:T(8,128)}, bf16[1024,2048]{1,0:T(8,128)(2,1)}) custom-call(bf16[24,256,128]{2,1,0:T(8,128)(2,1)S(1)} %shard_map.112.refs_0_, bf16[24,256,128]{2,1,0:T(8,128)(2,1)S(1)} %collective-permute-done.18.refs_1_, bf16[8,256,128]{2,1,0:T(8,128)(2,1)S(1)} %shard_map.113.refs_2_, ...), custom_call_target="tpu_custom_call" | custom-call | tf_op jit(solution)/shard_map/pallas_call | solution.py:293
  (54 shorter events, 8.2 us)
Async XLA Ops:
  4.0 6.0 %collective-permute-start = (bf16[8,1024,128]{2,1,0:T(8,128)(2,1)S(1)}, bf16[8,1024,128]{2,1,0:T(8,128)(2,1)S(1)}, u32[]{:S(2)}, u32[]{:S(2)}) collective-permute-start(bf16[8,1024,128]{2,1,0:T(8,128)(2,1)S(1)} %get-tuple-element.36), channel_id=1, source_target_pairs={{0,1},{1,0},{2,3},{3,2},{4,5},{5,4},{6,7},{7,6},{8,9},{9,8},{10,11... | collective-permute-start | bytes 6291464 | tf_op jit(solution)/shard_map/ppermute | solution.py:311
  4.8 9.0 %collective-permute-start.4 = (bf16[256,128]{1,0:T(8,128)(2,1)S(1)}, bf16[256,128]{1,0:T(8,128)(2,1)S(1)}, u32[]{:S(2)}, u32[]{:S(2)}) collective-permute-start(bf16[256,128]{1,0:T(8,128)(2,1)S(1)} %shard_map.105.w0_ref), channel_id=1, source_target_pairs={{0,34},{2,32},{16,50},{18,48},{32,2},{34,0},{48,18},{50,16},{1,35}... | collective-permute-start | bytes 196616 | tf_op jit(solution)/shard_map/ppermute | solution.py:311
  12.0 4.6 %collective-permute-start.1 = (bf16[128,128]{1,0:T(8,128)(2,1)S(1)}, bf16[128,128]{1,0:T(8,128)(2,1)S(1)}, u32[]{:S(2)}, u32[]{:S(2)}) collective-permute-start(bf16[128,128]{1,0:T(8,128)(2,1)S(1)} %convert_element_type.66), channel_id=1, source_target_pairs={{0,16},{16,0},{32,48},{48,32},{1,17},{17,1},{33,49},{49,33},{2,18}... | collective-permute-start | bytes 98312 | tf_op jit(solution)/shard_map/ppermute | solution.py:311
  13.8 17.0 %collective-permute-start.5 = (bf16[5,512,128]{2,1,0:T(8,128)(2,1)S(1)}, bf16[5,512,128]{2,1,0:T(8,128)(2,1)S(1)}, u32[]{:S(2)}, u32[]{:S(2)}) collective-permute-start(bf16[5,512,128]{2,1,0:T(8,128)(2,1)S(1)} %get-tuple-element.40), channel_id=1, source_target_pairs={{0,4},{4,8},{8,12},{12,0},{1,5},{5,9},{9,13},{13,1},{2,6},{6,10},{... | collective-permute-start | bytes 1966088 | tf_op jit(solution)/shard_map/ppermute | solution.py:311
  15.1 15.7 %collective-permute-start.6 = (bf16[5,512,128]{2,1,0:T(8,128)(2,1)S(1)}, bf16[5,512,128]{2,1,0:T(8,128)(2,1)S(1)}, u32[]{:S(2)}, u32[]{:S(2)}) collective-permute-start(bf16[5,512,128]{2,1,0:T(8,128)(2,1)S(1)} %get-tuple-element.41), channel_id=1, source_target_pairs={{0,12},{4,0},{8,4},{12,8},{1,13},{5,1},{9,5},{13,9},{2,14},{6,2},{... | collective-permute-start | bytes 1966088 | tf_op jit(solution)/shard_map/ppermute | solution.py:311
  16.6 3.1 %collective-permute-start.2 = (bf16[128,128]{1,0:T(8,128)(2,1)S(1)}, bf16[128,128]{1,0:T(8,128)(2,1)S(1)}, u32[]{:S(2)}, u32[]{:S(2)}) collective-permute-start(bf16[128,128]{1,0:T(8,128)(2,1)S(1)} %add_convert_fusion.1), channel_id=1, source_target_pairs={{0,64},{64,0},{128,192},{192,128},{1,65},{65,1},{129,193},{193,129... | collective-permute-start | bytes 98312 | tf_op jit(solution)/shard_map/ppermute | solution.py:311
  19.8 4.4 %collective-permute-start.3 = (bf16[128,128]{1,0:T(8,128)(2,1)S(1)}, bf16[128,128]{1,0:T(8,128)(2,1)S(1)}, u32[]{:S(2)}, u32[]{:S(2)}) collective-permute-start(bf16[128,128]{1,0:T(8,128)(2,1)S(1)} %add_convert_fusion), channel_id=1, source_target_pairs={{64,128},{128,64},{192,0},{0,192},{65,129},{129,65},{193,1},{1,193... | collective-permute-start | bytes 98312 | tf_op jit(solution)/shard_map/ppermute | solution.py:311
  30.9 9.0 %collective-permute-start.8 = (bf16[1280,128]{1,0:T(8,128)(2,1)S(1)}, bf16[1280,128]{1,0:T(8,128)(2,1)S(1)}, u32[]{:S(2)}, u32[]{:S(2)}) collective-permute-start(bf16[1280,128]{1,0:T(8,128)(2,1)S(1)} %get-tuple-element.47), channel_id=1, source_target_pairs={{0,4},{4,8},{8,12},{12,0},{1,5},{5,9},{9,13},{13,1},{2,6},{6,10},{... | collective-permute-start | bytes 983048 | tf_op jit(solution)/shard_map/ppermute | solution.py:311
  31.9 8.1 %collective-permute-start.9 = (bf16[1280,128]{1,0:T(8,128)(2,1)S(1)}, bf16[1280,128]{1,0:T(8,128)(2,1)S(1)}, u32[]{:S(2)}, u32[]{:S(2)}) collective-permute-start(bf16[1280,128]{1,0:T(8,128)(2,1)S(1)} %get-tuple-element.48), channel_id=1, source_target_pairs={{0,12},{4,0},{8,4},{12,8},{1,13},{5,1},{9,5},{13,9},{2,14},{6,2},{... | collective-permute-start | bytes 983048 | tf_op jit(solution)/shard_map/ppermute | solution.py:311
  33.7 4.0 %collective-permute-start.7 = (bf16[128,128]{1,0:T(8,128)(2,1)S(1)}, bf16[128,128]{1,0:T(8,128)(2,1)S(1)}, u32[]{:S(2)}, u32[]{:S(2)}) collective-permute-start(bf16[128,128]{1,0:T(8,128)(2,1)S(1)} %convert_add_fusion.3), channel_id=1, source_target_pairs={{0,32},{16,48},{32,0},{48,16},{1,33},{17,49},{33,1},{49,17},{2,34}... | collective-permute-start | bytes 98312 | tf_op jit(solution)/shard_map/ppermute | solution.py:311
  40.0 12.3 %collective-permute-start.13 = (bf16[8,256,128]{2,1,0:T(8,128)(2,1)S(1)}, bf16[8,256,128]{2,1,0:T(8,128)(2,1)S(1)}, u32[]{:S(2)}, u32[]{:S(2)}) collective-permute-start(bf16[8,256,128]{2,1,0:T(8,128)(2,1)S(1)} %shard_map.109.refs_0_), channel_id=1, source_target_pairs={{0,192},{64,0},{128,64},{192,128},{1,193},{65,1},{129,65},{193,129... | collective-permute-start | bytes 1572872 | tf_op jit(solution)/shard_map/ppermute | solution.py:311
  42.8 12.0 %collective-permute-start.12 = (bf16[8,256,128]{2,1,0:T(8,128)(2,1)S(1)}, bf16[8,256,128]{2,1,0:T(8,128)(2,1)S(1)}, u32[]{:S(2)}, u32[]{:S(2)}) collective-permute-start(bf16[8,256,128]{2,1,0:T(8,128)(2,1)S(1)} %shard_map.109.refs_0_), channel_id=1, source_target_pairs={{0,64},{64,128},{128,192},{192,0},{1,65},{65,129},{129,193},{193,1... | collective-permute-start | bytes 1572872 | tf_op jit(solution)/shard_map/ppermute | solution.py:311
  42.8 5.0 %collective-permute-start.10 = (bf16[128,128]{1,0:T(8,128)(2,1)S(1)}, bf16[128,128]{1,0:T(8,128)(2,1)S(1)}, u32[]{:S(2)}, u32[]{:S(2)}) collective-permute-start(bf16[128,128]{1,0:T(8,128)(2,1)S(1)} %convert_add_fusion.2), channel_id=1, source_target_pairs={{0,34},{2,32},{16,50},{18,48},{32,2},{34,0},{48,18},{50,16},{1,35}... | collective-permute-start | bytes 98312 | tf_op jit(solution)/shard_map/ppermute | solution.py:311
  47.8 4.4 %collective-permute-start.11 = (bf16[128,128]{1,0:T(8,128)(2,1)S(1)}, bf16[128,128]{1,0:T(8,128)(2,1)S(1)}, u32[]{:S(2)}, u32[]{:S(2)}) collective-permute-start(bf16[128,128]{1,0:T(8,128)(2,1)S(1)} %convert_add_fusion.1), channel_id=1, source_target_pairs={{0,4},{4,0},{8,12},{12,8},{1,5},{5,1},{9,13},{13,9},{2,6},{6,2},{1... | collective-permute-start | bytes 98312 | tf_op jit(solution)/shard_map/ppermute | solution.py:311
  48.1 15.6 %collective-permute-start.17 = (bf16[1024,128]{1,0:T(8,128)(2,1)S(1)}, bf16[1024,128]{1,0:T(8,128)(2,1)S(1)}, u32[]{:S(2)}, u32[]{:S(2)}) collective-permute-start(bf16[1024,128]{1,0:T(8,128)(2,1)S(1)} %shard_map.108), channel_id=1, source_target_pairs={{0,2},{2,0},{1,3},{3,1},{4,6},{6,4},{5,7},{7,5},{8,10},{10,8},{9,1... | collective-permute-start | bytes 786440 | tf_op jit(solution)/shard_map/ppermute | solution.py:311
  52.2 11.5 %copy-start.7 = (f32[128,128]{1,0:T(8,128)S(1)}, f32[128,128]{1,0:T(8,128)}, u32[]{:S(2)}) copy-start(f32[128,128]{1,0:T(8,128)} %constant.14.clone.refs_7_) | copy-start | bytes 196612
  54.9 17.9 %collective-permute-start.18 = (bf16[24,256,128]{2,1,0:T(8,128)(2,1)S(1)}, bf16[24,256,128]{2,1,0:T(8,128)(2,1)S(1)}, u32[]{:S(2)}, u32[]{:S(2)}) collective-permute-start(bf16[24,256,128]{2,1,0:T(8,128)(2,1)S(1)} %shard_map.112.refs_0_), channel_id=1, source_target_pairs={{0,1},{1,0},{2,3},{3,2},{4,5},{5,4},{6,7},{7,6},{8,9},{9,8},{10,11... | collective-permute-start | bytes 4718600 | tf_op jit(solution)/shard_map/ppermute | solution.py:311
  58.6 7.2 %collective-permute-start.14 = (bf16[128,128]{1,0:T(8,128)(2,1)S(1)}, bf16[128,128]{1,0:T(8,128)(2,1)S(1)}, u32[]{:S(2)}, u32[]{:S(2)}) collective-permute-start(bf16[128,128]{1,0:T(8,128)(2,1)S(1)} %convert_add_fusion), channel_id=1, source_target_pairs={{4,8},{8,4},{12,0},{0,12},{5,9},{9,5},{13,1},{1,13},{6,10},{10,6},... | collective-permute-start | bytes 98312 | tf_op jit(solution)/shard_map/ppermute | solution.py:311
  61.1 8.8 %collective-permute-start.15 = (bf16[4,256,128]{2,1,0:T(8,128)(2,1)S(1)}, bf16[4,256,128]{2,1,0:T(8,128)(2,1)S(1)}, u32[]{:S(2)}, u32[]{:S(2)}) collective-permute-start(bf16[4,256,128]{2,1,0:T(8,128)(2,1)S(1)} %get-tuple-element.57), channel_id=1, source_target_pairs={{0,64},{64,128},{128,192},{192,0},{1,65},{65,129},{129,193},{193,1... | collective-permute-start | bytes 786440 | tf_op jit(solution)/shard_map/ppermute | solution.py:311
  61.1 11.7 %copy-start.3 = (bf16[1024,128]{1,0:T(8,128)(2,1)S(1)}, bf16[1024,128]{1,0:T(8,128)(2,1)}, u32[]{:S(2)}) copy-start(bf16[1024,128]{1,0:T(8,128)(2,1)} %constant.15.clone.refs_7_) | copy-start | bytes 786436
  61.1 11.7 %copy-start.4 = (f32[128,128]{1,0:T(8,128)S(1)}, f32[128,128]{1,0:T(8,128)}, u32[]{:S(2)}) copy-start(f32[128,128]{1,0:T(8,128)} %constant.16.clone.refs_8_) | copy-start | bytes 196612
  61.1 8.8 %collective-permute-start.16 = (bf16[4,256,128]{2,1,0:T(8,128)(2,1)S(1)}, bf16[4,256,128]{2,1,0:T(8,128)(2,1)S(1)}, u32[]{:S(2)}, u32[]{:S(2)}) collective-permute-start(bf16[4,256,128]{2,1,0:T(8,128)(2,1)S(1)} %get-tuple-element.58), channel_id=1, source_target_pairs={{0,192},{64,0},{128,64},{192,128},{1,193},{65,1},{129,65},{193,129... | collective-permute-start | bytes 786440 | tf_op jit(solution)/shard_map/ppermute | solution.py:311
  69.9 2.8 %collective-permute-start.19 = (bf16[8,256,128]{2,1,0:T(8,128)(2,1)S(1)}, bf16[8,256,128]{2,1,0:T(8,128)(2,1)S(1)}, u32[]{:S(2)}, u32[]{:S(2)}) collective-permute-start(bf16[8,256,128]{2,1,0:T(8,128)(2,1)S(1)} %shard_map.113.refs_2_), channel_id=1, source_target_pairs={{0,1},{1,0},{2,3},{3,2},{4,5},{5,4},{6,7},{7,6},{8,9},{9,8},{10,11... | collective-permute-start | bytes 1572872 | tf_op jit(solution)/shard_map/ppermute | solution.py:311
  71.1 1.6 %collective-permute-start.20 = (bf16[128,128]{1,0:T(8,128)(2,1)S(1)}, bf16[128,128]{1,0:T(8,128)(2,1)S(1)}, u32[]{:S(2)}, u32[]{:S(2)}) collective-permute-start(bf16[128,128]{1,0:T(8,128)(2,1)S(1)} %add_multiply_fusion.refs_4_), channel_id=1, source_target_pairs={{0,1},{1,0},{2,3},{3,2},{4,5},{5,4},{6,7},{7,6},{8,9},{9,8},{10,11... | collective-permute-start | bytes 98312 | tf_op jit(solution)/shard_map/ppermute | solution.py:311
  (5 other events, 25.6 us)

commit v6 on v5

--- a/solution.py
+++ b/solution.py
@@ -241,46 +241,54 @@
         out_ref[r] = moment - low
 
 
-def weights_kernel(*refs):
-    packs, (band_ref, band_other_ref, master_ref, cols_ref, table_ref) = refs[:4], refs[4:9]
-    master_out, full_out, spread_ref, page_ref, sem = refs[9:]
-    x, y, zh, core = (lax.axis_index(name) for name in ("x", "y", "zh", "core"))
-
+def columns_side(table_ref):
+    x, zh = lax.axis_index("x"), lax.axis_index("zh")
     row_slot = lax.broadcasted_iota(jnp.int32, (GROUP, GROUP), 0) // BAND
     table = table_ref[...]
     zero = jnp.zeros_like(table)
     columns = []
     wide = []
-    for gz, dx in [(gz, dx) for gz in range(2) for dx in (0, 3, 1, 2)]:
-        bx, bz = lax.rem(x + dx, 4), (zh if gz == 0 else 1 - zh)
-        columns.append(bx * 4 + bz * 2)
-        wide.append(jnp.where(row_slot == bx * 2 + bz, table, zero).astype(bf16))
-    wide = jnp.concatenate(wide, axis=1)
-
+    for gz in range(2):
+        for dx in (0, 3, 1, 2):
+            bx, bz = lax.rem(x + dx, 4), (zh if gz == 0 else 1 - zh)
+            columns.append(bx * 4 + bz * 2)
+            wide.append(jnp.where(row_slot == bx * 2 + bz, table, zero).astype(bf16))
+    return jnp.concatenate(wide, axis=1), columns
+
+
+def update_quarter(dy, packs, at, spread_ref, wide, columns, page_ref, full_out, sem):
+    core = lax.axis_index("core")
+    quarter = lax.rem(lax.axis_index("y") + dy, 4)
+    rows = pl.ds(pl.multiple_of(quarter * QUARTER, QUARTER), QUARTER)
+    for who in range(2):
+        side = core if who == 0 else 1 - core
+        update = jnp.dot(
+            spread_ref[rows, who * GROUP : (who + 1) * GROUP], wide, preferred_element_type=f32
+        )
+        for k, column in enumerate(columns):
+            new = packs[who][at + k].astype(f32) + update[:, k * GROUP : (k + 1) * GROUP]
+            page_ref[:, lanes(column + side)] = new.astype(bf16)
+    copy = pltpu.make_async_copy(page_ref, full_out.at[rows, :], sem)
+    copy.start()
+    return copy
+
+
+def first_weights_kernel(
+    early_ref, early_other_ref, band_ref, band_other_ref, master_ref, cols_ref, table_ref,
+    master_out, full_out, spread_ref, page_ref, sem,
+):
+    wide, columns = columns_side(table_ref)
     coeffs = jnp.concatenate([band_ref[...], band_other_ref[...]], axis=1)
     spread_ref[...] = jnp.dot(
         cols_ref[...], coeffs, preferred_element_type=f32
     ).astype(bf16)
-
-    copies = []
-    for step, dy in enumerate((0, 3, 1, 2)):
-        quarter = lax.rem(y + dy, 4)
-        rows = pl.ds(pl.multiple_of(quarter * QUARTER, QUARTER), QUARTER)
-        for who in range(2):
-            side = core if who == 0 else 1 - core
-            update = jnp.dot(
-                spread_ref[rows, who * GROUP : (who + 1) * GROUP],
-                wide,
-                preferred_element_type=f32,
-            )
-            for k in range(8):
-                part = update[:, k * GROUP : (k + 1) * GROUP]
-                prior = packs[2 + who][k] if step == 3 else packs[who][step * 8 + k]
-                new = prior.astype(f32) + part
-                page_ref[step, :, lanes(columns[k] + side)] = new.astype(bf16)
-        copy = pltpu.make_async_copy(page_ref.at[step], full_out.at[rows, :], sem.at[step])
-        copy.start()
-        copies.append(copy)
+    packs = (early_ref, early_other_ref)
+    copies = [
+        update_quarter(
+            dy, packs, 8 * step, spread_ref, wide, columns, page_ref.at[step], full_out, sem.at[step]
+        )
+        for step, dy in enumerate((0, 3, 1))
+    ]
     master_out[...] = master_ref[...] + jnp.dot(
         spread_ref[:, :GROUP], wide[:, :GROUP], preferred_element_type=f32
     )
@@ -288,23 +296,48 @@
         copy.wait()
 
 
-def weights_of(packs, bands, master, cols, table):
-    vmem = pl.BlockSpec(memory_space=pltpu.VMEM)
-    return pl.pallas_call(
-        weights_kernel,
+def last_weights_kernel(
+    late_ref, late_other_ref, spread_ref, table_ref, started_ref, full_out, page_ref, sem
+):
+    del started_ref
+    wide, columns = columns_side(table_ref)
+    packs = (late_ref, late_other_ref)
+    update_quarter(2, packs, 0, spread_ref, wide, columns, page_ref, full_out, sem).wait()
+
+
+VMEM = pl.BlockSpec(memory_space=pltpu.VMEM)
+ANYWHERE = pl.BlockSpec(memory_space=pl.ANY)
+FULL = jax.ShapeDtypeStruct((ROWS, 16 * GROUP), bf16)
+
+
+def first_weights(early, early_other, band, band_other, master, cols, table):
+    return pl.pallas_call(
+        first_weights_kernel,
         out_shape=[
             jax.ShapeDtypeStruct((ROWS, GROUP), f32),
-            jax.ShapeDtypeStruct((ROWS, 16 * GROUP), bf16),
+            FULL,
+            jax.ShapeDtypeStruct((ROWS, 2 * GROUP), bf16),
         ],
-        in_specs=[vmem] * 9,
-        out_specs=[vmem, pl.BlockSpec(memory_space=pl.ANY)],
+        in_specs=[VMEM] * 7,
+        out_specs=[VMEM, ANYWHERE, VMEM],
         scratch_shapes=[
-            pltpu.VMEM((ROWS, 2 * GROUP), bf16),
-            pltpu.VMEM((4, QUARTER, 16 * GROUP), bf16),
-            pltpu.SemaphoreType.DMA((4,)),
+            pltpu.VMEM((3, QUARTER, 16 * GROUP), bf16),
+            pltpu.SemaphoreType.DMA((3,)),
         ],
         compiler_params=pltpu.CompilerParams(vmem_limit_bytes=20 * 2**20),
-    )(*packs, *bands, master, cols, table)
+    )(early, early_other, band, band_other, master, cols, table)
+
+
+def last_weights(late, late_other, spread, table, started):
+    return pl.pallas_call(
+        last_weights_kernel,
+        out_shape=FULL,
+        in_specs=[VMEM] * 4 + [ANYWHERE],
+        out_specs=ANYWHERE,
+        input_output_aliases={4: 0},
+        scratch_shapes=[pltpu.VMEM((QUARTER, 16 * GROUP), bf16), pltpu.SemaphoreType.DMA],
+        compiler_params=pltpu.CompilerParams(vmem_limit_bytes=12 * 2**20),
+    )(late, late_other, spread, table, started)
 
 
 def send(array, axis, perm):
@@ -316,6 +349,11 @@
 
 def both(own, got):
     return own.astype(f32) + got.astype(f32)
+
+
+def all_four(own, axis):
+    across, below, above = (send(own, axis, perm) for perm in (ACROSS4, UP4, DOWN4))
+    return lambda: both(own, across) + both(below, above)
 
 
 def local(gradients, momentum, master_weights):
@@ -342,25 +380,21 @@
     left = send(up, "x", UP4)
     right = send(down, "x", DOWN4)
 
-    band = both(band, got)
-    band = band.astype(bf16)
-    got = send(band, "y", EVEN4)
-
-    band = both(band, got)
-    band = band.astype(bf16)
-    got = send(band, "y", ODD4)
+    total = all_four(both(band, got).astype(bf16), "y")
+
+    band = total().astype(bf16)
+    got = send(band, "zl", XOR2)
 
     band, left, right = together((both(band, got), left, right))
     band = band.astype(bf16)
-    got = send(band, "zl", XOR2)
+    got = send(band, z, CROSS8)
     passed = jax.ShapeDtypeStruct((2 * HALF + QUARTER, GROUP), bf16)
     up, down = small_call(pass_on_kernel, [passed] * 2, keep_up, keep_down, left, right)
     last_left = send(up, "x", UP4)
     last_right = send(down, "x", DOWN4)
 
     band, last_left, last_right = together((both(band, got), last_left, last_right))
-    band = band.astype(bf16)
-    got = send(band, z, CROSS8)
+    total = all_four(band.astype(bf16), "x")
     parts = (mine, left, right, last_left, last_right)
     eighth = small_call(
         collect_kernel, jax.ShapeDtypeStruct((8, QUARTER, GROUP), bf16), w0, wz, *parts[1:]
@@ -368,19 +402,27 @@
     below = send(eighth, "y", UP4)
     above = send(eighth, "y", DOWN4)
     z_send = small_call(z_send_kernel, jax.ShapeDtypeStruct(half, bf16), *parts)
-
-    band, z_send = together((both(band, got), z_send))
-    band = band.astype(bf16)
-    got = send(band, "x", EVEN4)
     from_z = send(z_send, "zh", SWAP2)
 
-    band, eighth, below, above = together((both(band, got), eighth, below, above))
-    band = band.astype(bf16)
-    got = send(band, "x", ODD4)
+    band, eighth, below, above, from_z = together((total(), eighth, below, above, from_z))
+    band = (band * (-step_size / replicas)).astype(bf16)
+    band_other = send(band, "core", SWAP2)
+    early = packed(eighth, below, above)
+    early_other = send(early, "core", SWAP2)
     four = jax.ShapeDtypeStruct((4, QUARTER, GROUP), bf16)
     up, down = small_call(half_kernel, [four] * 2, below, above)
     low = send(up, "y", UP4)
     high = send(down, "y", DOWN4)
+    columns_table = jnp.asarray(np.tile(table, (8, 1)), f32)
+    new_master, started, spread = first_weights(
+        early,
+        early_other,
+        band,
+        band_other,
+        master_weights,
+        jnp.asarray(np.kron(np.eye(8), table.T), bf16),
+        columns_table,
+    )
     new_momentum = small_call(
         remaining_kernel,
         jax.ShapeDtypeStruct(half, f32),
@@ -388,25 +430,12 @@
         from_z,
         mom,
         jnp.asarray(table.T @ table, f32),
-        cost=pl.CostEstimate(flops=8000000000, bytes_accessed=2000000, transcendentals=0),
-    )
-
-    band, low, high, new_momentum = together(
-        ((both(band, got)) * (-step_size / replicas), low, high, new_momentum)
-    )
-    band = band.astype(bf16)
-    band_other = send(band, "core", SWAP2)
-    early = packed(eighth, below, above)
-    early_other = send(early, "core", SWAP2)
+    )
+
+    spread, new_momentum, low, high = together((spread, new_momentum, low, high))
     late = packed(low, high)
     late_other = send(late, "core", SWAP2)
-    new_master, weights_full = weights_of(
-        (early, early_other, late, late_other),
-        (band, band_other),
-        master_weights,
-        jnp.asarray(np.kron(np.eye(8), table.T), bf16),
-        jnp.asarray(np.tile(table, (8, 1)), f32),
-    )
+    weights_full = last_weights(late, late_other, spread, columns_table, started)
     return (new_momentum[None], new_master, weights_full)
 
 

time: 77.4 us -> 75.1 us (0.970)
  waiting for transfers between devices: 27.8 us -> 23.4 us
  Pallas kernels: 9.94 us -> 11 us
    ppermute x21 -> x23, waiting for transfers between devices: 27.8 us -> 23.4 us  [send(): return lax.ppermute(array, axis, perm)]
    pallas_call x1 -> x2, Pallas kernels: 4.35 us -> 5.42 us  [the longest x1 3.8 us: first_weights(): pl.pallas_call(first_weights_kernel, out_shape=[jax.ShapeDtypeStruct((ROW...]
    ppermute x21 -> x23, starting transfers between devices: 36.3 us -> 36.5 us  [send(): return lax.ppermute(array, axis, perm)]
  transfers between devices with their start and end apart: 21 -> 23, of which waited for: 10 -> 11; matrix products, arithmetic and copies ran while one was open for 0% -> 0% of each run, Pallas kernels for 6% -> 11%
where the time goes in v6:
time: 75.1 us; the launch traced here: 74.2 us
  starting transfers between devices  36.5 us (49%)
  waiting for transfers between devices  23.4 us (31%)
  Pallas kernels  11 us (15%)
  local copies, waits for them, and re-layouts  2.22 us (3%)
  between operations  0.94 us (1%)
    ppermute x23, starting transfers between devices, send(): return lax.ppermute(array, axis, perm)  36.5 us
    ppermute x23, waiting for transfers between devices, send(): return lax.ppermute(array, axis, perm)  23.4 us
    pallas_call x1, Pallas kernels, first_weights(): pl.pallas_call(first_weights_kernel, out_shape=[jax.ShapeDtypeStruct((ROW...  3.8 us
    pallas_call x8, Pallas kernels, small_call(): pl.pallas_call(kernel, out_shape=shapes, in_specs=[vmem] * len(args), out...  2.42 us
    unnamed x16, local copies, waits for them, and re-layouts  2.22 us
    pallas_call x1, Pallas kernels, pair_sum(): pl.pallas_call(pair_sum_kernel, out_shape=shapes, in_specs=[vmem] * 5, ou...  2 us
    pallas_call x1, Pallas kernels, last_weights(): pl.pallas_call(last_weights_kernel, out_shape=FULL, in_specs=[VMEM] * 4 +...  1.62 us
  transfers between devices with their start and end apart: 23, of which 11 were waited for; matrix products, arithmetic and copies ran while one was open for 0% of the time, Pallas kernels for 11%

profile of v6, /device:TPU:33, one launch (start us, length us, event | category | flops | bytes accessed | tf_op | source)
XLA Modules:
  0.0 74.2 jit_solution(14514824432331999597)
XLA Ops:
  0.6 2.2 %copy-done = bf16[1,1,1024,2048]{3,2,1,0:T(8,128)(2,1)S(1)} copy-done((bf16[1,1,1024,2048]{3,2,1,0:T(8,128)(2,1)S(1)}, bf16[1,1,1024,2048]{3,2,1,0:T(8,128)(2,1)}, u32[]{:S(2)}) %copy-start) | copy-done | bytes 4194328
  4.8 5.2 %collective-permute-start.6 = (bf16[256,128]{1,0:T(8,128)(2,1)S(1)}, bf16[256,128]{1,0:T(8,128)(2,1)S(1)}, u32[]{:S(2)}, u32[]{:S(2)}) collective-permute-start(bf16[256,128]{1,0:T(8,128)(2,1)S(1)} %shard_map.105.w0_ref), channel_id=1, source_target_pairs={{0,34},{2,32},{16,50},{18,48},{32,2},{34,0},{48,18},{50,16},{1,35}... | collective-permute-start | bytes 196616 | tf_op jit(solution)/shard_map/ppermute | solution.py:344
  10.0 2.0 %shard_map.104 = (bf16[5,512,128]{2,1,0:T(8,128)(2,1)S(1)}, bf16[5,512,128]{2,1,0:T(8,128)(2,1)S(1)}, bf16[2,512,128]{2,1,0:T(8,128)(2,1)S(1)}, bf16[2,512,128]{...) custom-call(bf16[8,1024,128]{2,1,0:T(8,128)(2,1)S(1)} %get-tuple-element.35.own_ref, ...), custom_call_target="tpu_custom_call" | custom-call | tf_op jit(solution)/shard_map/pallas_call | solution.py:124
  13.8 1.3 %collective-permute-start.7 = (bf16[5,512,128]{2,1,0:T(8,128)(2,1)S(1)}, bf16[5,512,128]{2,1,0:T(8,128)(2,1)S(1)}, u32[]{:S(2)}, u32[]{:S(2)}) collective-permute-start(bf16[5,512,128]{2,1,0:T(8,128)(2,1)S(1)} %get-tuple-element.40), channel_id=1, source_target_pairs={{0,4},{4,8},{8,12},{12,0},{1,5},{5,9},{9,13},{13,1},{2,6},{6,10},{... | collective-permute-start | bytes 1966088 | tf_op jit(solution)/shard_map/ppermute | solution.py:344
  15.1 1.5 %collective-permute-start.8 = (bf16[5,512,128]{2,1,0:T(8,128)(2,1)S(1)}, bf16[5,512,128]{2,1,0:T(8,128)(2,1)S(1)}, u32[]{:S(2)}, u32[]{:S(2)}) collective-permute-start(bf16[5,512,128]{2,1,0:T(8,128)(2,1)S(1)} %get-tuple-element.41), channel_id=1, source_target_pairs={{0,12},{4,0},{8,4},{12,8},{1,13},{5,1},{9,5},{13,9},{2,14},{6,2},{... | collective-permute-start | bytes 1966088 | tf_op jit(solution)/shard_map/ppermute | solution.py:344
  16.6 2.8 %collective-permute-start.4 = (bf16[128,128]{1,0:T(8,128)(2,1)S(1)}, bf16[128,128]{1,0:T(8,128)(2,1)S(1)}, u32[]{:S(2)}, u32[]{:S(2)}) collective-permute-start(bf16[128,128]{1,0:T(8,128)(2,1)S(1)} %add_convert_fusion.1), channel_id=1, source_target_pairs={{0,192},{64,0},{128,64},{192,128},{1,193},{65,1},{129,65},{193,129... | collective-permute-start | bytes 98312 | tf_op jit(solution)/shard_map/ppermute | solution.py:344
  19.4 1.6 %collective-permute-start.2 = (bf16[128,128]{1,0:T(8,128)(2,1)S(1)}, bf16[128,128]{1,0:T(8,128)(2,1)S(1)}, u32[]{:S(2)}, u32[]{:S(2)}) collective-permute-start(bf16[128,128]{1,0:T(8,128)(2,1)S(1)} %add_convert_fusion.1), channel_id=1, source_target_pairs={{0,128},{64,192},{128,0},{192,64},{1,129},{65,193},{129,1},{193,65... | collective-permute-start | bytes 98312 | tf_op jit(solution)/shard_map/ppermute | solution.py:344
  21.1 2.6 %collective-permute-done.3 = bf16[128,128]{1,0:T(8,128)(2,1)S(1)} collective-permute-done((bf16[128,128]{1,0:T(8,128)(2,1)S(1)}, bf16[128,128]{1,0:T(8,128)(2,1)S(1)}, u32[]{:S(2)}, u32[]{:S(2)}) %collective-permute-start.3) | collective-permute-done | bytes 32800 | tf_op jit(solution)/shard_map/ppermute | solution.py:344
  24.0 3.9 %collective-permute-done.5 = bf16[128,128]{1,0:T(8,128)(2,1)S(1)} collective-permute-done((bf16[128,128]{1,0:T(8,128)(2,1)S(1)}, bf16[128,128]{1,0:T(8,128)(2,1)S(1)}, u32[]{:S(2)}, u32[]{:S(2)}) %collective-permute-start.5) | collective-permute-done | bytes 32800 | tf_op jit(solution)/shard_map/ppermute | solution.py:344
  27.8 3.0 %collective-permute-done.7.left_ref.refs_1_ = bf16[5,512,128]{2,1,0:T(8,128)(2,1)S(1)} collective-permute-done((bf16[5,512,128]{2,1,0:T(8,128)(2,1)S(1)}, bf16[5,512,128]{2,1,0:T(8,128)(2,1)S(1)}, u32[]{:S(2)}, u32[]{:S(2)}) %collective-permute-start.7) | collective-permute-done | bytes 655392 | tf_op jit(solution)/shard_map/ppermute | solution.py:344
  31.9 1.8 %collective-permute-start.11 = (bf16[1280,128]{1,0:T(8,128)(2,1)S(1)}, bf16[1280,128]{1,0:T(8,128)(2,1)S(1)}, u32[]{:S(2)}, u32[]{:S(2)}) collective-permute-start(bf16[1280,128]{1,0:T(8,128)(2,1)S(1)} %get-tuple-element.48), channel_id=1, source_target_pairs={{0,12},{4,0},{8,4},{12,8},{1,13},{5,1},{9,5},{13,9},{2,14},{6,2},{... | collective-permute-start | bytes 983048 | tf_op jit(solution)/shard_map/ppermute | solution.py:344
  33.7 2.5 %collective-permute-start.9 = (bf16[128,128]{1,0:T(8,128)(2,1)S(1)}, bf16[128,128]{1,0:T(8,128)(2,1)S(1)}, u32[]{:S(2)}, u32[]{:S(2)}) collective-permute-start(bf16[128,128]{1,0:T(8,128)(2,1)S(1)} %convert_add_fusion.1), channel_id=1, source_target_pairs={{0,34},{2,32},{16,50},{18,48},{32,2},{34,0},{48,18},{50,16},{1,35}... | collective-permute-start | bytes 98312 | tf_op jit(solution)/shard_map/ppermute | solution.py:344
  36.2 2.7 %collective-permute-done.9 = bf16[128,128]{1,0:T(8,128)(2,1)S(1)} collective-permute-done((bf16[128,128]{1,0:T(8,128)(2,1)S(1)}, bf16[128,128]{1,0:T(8,128)(2,1)S(1)}, u32[]{:S(2)}, u32[]{:S(2)}) %collective-permute-start.9) | collective-permute-done | bytes 32800 | tf_op jit(solution)/shard_map/ppermute | solution.py:344
  40.0 2.8 %collective-permute-start.16 = (bf16[8,256,128]{2,1,0:T(8,128)(2,1)S(1)}, bf16[8,256,128]{2,1,0:T(8,128)(2,1)S(1)}, u32[]{:S(2)}, u32[]{:S(2)}) collective-permute-start(bf16[8,256,128]{2,1,0:T(8,128)(2,1)S(1)} %shard_map.108.refs_0_), channel_id=1, source_target_pairs={{0,192},{64,0},{128,64},{192,128},{1,193},{65,1},{129,65},{193,129... | collective-permute-start | bytes 1572872 | tf_op jit(solution)/shard_map/ppermute | solution.py:344
  42.9 3.9 %collective-permute-start.17 = (bf16[1024,128]{1,0:T(8,128)(2,1)S(1)}, bf16[1024,128]{1,0:T(8,128)(2,1)S(1)}, u32[]{:S(2)}, u32[]{:S(2)}) collective-permute-start(bf16[1024,128]{1,0:T(8,128)(2,1)S(1)} %shard_map.109), channel_id=1, source_target_pairs={{0,2},{2,0},{1,3},{3,1},{4,6},{6,4},{5,7},{7,5},{8,10},{10,8},{9,1... | collective-permute-start | bytes 786440 | tf_op jit(solution)/shard_map/ppermute | solution.py:344
  46.8 3.6 %collective-permute-start.12 = (bf16[128,128]{1,0:T(8,128)(2,1)S(1)}, bf16[128,128]{1,0:T(8,128)(2,1)S(1)}, u32[]{:S(2)}, u32[]{:S(2)}) collective-permute-start(bf16[128,128]{1,0:T(8,128)(2,1)S(1)} %convert_add_fusion), channel_id=1, source_target_pairs={{0,8},{4,12},{8,0},{12,4},{1,9},{5,13},{9,1},{13,5},{2,10},{6,14},... | collective-permute-start | bytes 98312 | tf_op jit(solution)/shard_map/ppermute | solution.py:344
  51.7 1.8 %collective-permute-done.14 = bf16[128,128]{1,0:T(8,128)(2,1)S(1)} collective-permute-done((bf16[128,128]{1,0:T(8,128)(2,1)S(1)}, bf16[128,128]{1,0:T(8,128)(2,1)S(1)}, u32[]{:S(2)}, u32[]{:S(2)}) %collective-permute-start.14) | collective-permute-done | bytes 32800 | tf_op jit(solution)/shard_map/ppermute | solution.py:344
  53.5 4.7 %collective-permute-done.17.refs_5_ = bf16[1024,128]{1,0:T(8,128)(2,1)S(1)} collective-permute-done((bf16[1024,128]{1,0:T(8,128)(2,1)S(1)}, bf16[1024,128]{1,0:T(8,128)(2,1)S(1)}, u32[]{:S(2)}, u32[]{:S(2)}) %collective-permute-start.17) | collective-permute-done | bytes 262176 | tf_op jit(solution)/shard_map/ppermute | solution.py:344
  58.3 2.3 %collective-permute-start.18 = (bf16[24,256,128]{2,1,0:T(8,128)(2,1)S(1)}, bf16[24,256,128]{2,1,0:T(8,128)(2,1)S(1)}, u32[]{:S(2)}, u32[]{:S(2)}) collective-permute-start(bf16[24,256,128]{2,1,0:T(8,128)(2,1)S(1)} %shard_map.110.early_ref), channel_id=1, source_target_pairs={{0,1},{1,0},{2,3},{3,2},{4,5},{5,4},{6,7},{7,6},{8,9},{9,8},{10,11... | collective-permute-start | bytes 4718600 | tf_op jit(solution)/shard_map/ppermute | solution.py:344
  61.0 2.6 %collective-permute-start.21 = (bf16[4,256,128]{2,1,0:T(8,128)(2,1)S(1)}, bf16[4,256,128]{2,1,0:T(8,128)(2,1)S(1)}, u32[]{:S(2)}, u32[]{:S(2)}) collective-permute-start(bf16[4,256,128]{2,1,0:T(8,128)(2,1)S(1)} %get-tuple-element.60), channel_id=1, source_target_pairs={{0,192},{64,0},{128,64},{192,128},{1,193},{65,1},{129,65},{193,129... | collective-permute-start | bytes 786440 | tf_op jit(solution)/shard_map/ppermute | solution.py:344
  64.2 2.0 %shard_map.112 = f32[1024,128]{1,0:T(8,128)} custom-call(bf16[2,1024,128]{2,1,0:T(8,128)(2,1)S(1)} %get-tuple-element.52.refs_0_, bf16[5,512,128]{2,1,0:T(8,128)(2,1)S(1)} %collective-permute-done.7.left_ref.refs_1_, bf16[5,512,128]{2,1,0:T(8,128)(2,1)S(1)} %collective-permute-done.8.right_ref.refs_2_, ...), custom_call_target="tpu_custom_call" | custom-call | tf_op jit(solution)/shard_map/pallas_call | solution.py:136
  66.2 3.8 %shard_map.111 = (f32[1024,128]{1,0:T(8,128)}, bf16[1024,2048]{1,0:T(8,128)(2,1)}, bf16[1024,256]{1,0:T(8,128)(2,1)S(1)}) custom-call(bf16[24,256,128]{2,1,0:T(8,128)(2,1)S(1)} %shard_map.110.early_ref, bf16[24,256,128]{2,1,0:T(8,128)(2,1)S(1)} %collective-permute-done.18.early_other_ref, bf16[128,128]{1,0:T(8,128)(2,1)S(1)} %multiply_convert_fusion.band_ref, ...), custom_call_target="tpu_custom_call" | custom-call | tf_op jit(solution)/shard_map/pallas_call | solution.py:314
  70.9 1.5 %collective-permute-done.22.late_other_ref = bf16[8,256,128]{2,1,0:T(8,128)(2,1)S(1)} collective-permute-done((bf16[8,256,128]{2,1,0:T(8,128)(2,1)S(1)}, bf16[8,256,128]{2,1,0:T(8,128)(2,1)S(1)}, u32[]{:S(2)}, u32[]{:S(2)}) %collective-permute-start.22) | collective-permute-done | bytes 524320 | tf_op jit(solution)/shard_map/ppermute | solution.py:344
  72.5 1.6 %shard_map.115 = bf16[1024,2048]{1,0:T(8,128)(2,1)} custom-call(bf16[8,256,128]{2,1,0:T(8,128)(2,1)S(1)} %shard_map.114.late_ref, bf16[8,256,128]{2,1,0:T(8,128)(2,1)S(1)} %collective-permute-done.22.late_other_ref, bf16[1024,256]{1,0:T(8,128)(2,1)S(1)} %get-tuple-element.65.spread_ref, f32[128,128]{1,0:T(8,128)S(1)} %copy-done.3, ...), custom_call_target="tpu_custom_call", output_to_operand_aliasing={{}: (4, {})} | custom-call | tf_op jit(solution)/shard_map/pallas_call | solution.py:332
  (58 shorter events, 9.5 us)
Async XLA Ops:
  4.0 6.0 %collective-permute-start = (bf16[8,1024,128]{2,1,0:T(8,128)(2,1)S(1)}, bf16[8,1024,128]{2,1,0:T(8,128)(2,1)S(1)}, u32[]{:S(2)}, u32[]{:S(2)}) collective-permute-start(bf16[8,1024,128]{2,1,0:T(8,128)(2,1)S(1)} %get-tuple-element.36), channel_id=1, source_target_pairs={{0,1},{1,0},{2,3},{3,2},{4,5},{5,4},{6,7},{7,6},{8,9},{9,8},{10,11... | collective-permute-start | bytes 6291464 | tf_op jit(solution)/shard_map/ppermute | solution.py:344
  4.8 9.0 %collective-permute-start.6 = (bf16[256,128]{1,0:T(8,128)(2,1)S(1)}, bf16[256,128]{1,0:T(8,128)(2,1)S(1)}, u32[]{:S(2)}, u32[]{:S(2)}) collective-permute-start(bf16[256,128]{1,0:T(8,128)(2,1)S(1)} %shard_map.105.w0_ref), channel_id=1, source_target_pairs={{0,34},{2,32},{16,50},{18,48},{32,2},{34,0},{48,18},{50,16},{1,35}... | collective-permute-start | bytes 196616 | tf_op jit(solution)/shard_map/ppermute | solution.py:344
  12.0 4.6 %collective-permute-start.1 = (bf16[128,128]{1,0:T(8,128)(2,1)S(1)}, bf16[128,128]{1,0:T(8,128)(2,1)S(1)}, u32[]{:S(2)}, u32[]{:S(2)}) collective-permute-start(bf16[128,128]{1,0:T(8,128)(2,1)S(1)} %convert_element_type.60), channel_id=1, source_target_pairs={{0,16},{16,0},{32,48},{48,32},{1,17},{17,1},{33,49},{49,33},{2,18}... | collective-permute-start | bytes 98312 | tf_op jit(solution)/shard_map/ppermute | solution.py:344
  13.8 17.0 %collective-permute-start.7 = (bf16[5,512,128]{2,1,0:T(8,128)(2,1)S(1)}, bf16[5,512,128]{2,1,0:T(8,128)(2,1)S(1)}, u32[]{:S(2)}, u32[]{:S(2)}) collective-permute-start(bf16[5,512,128]{2,1,0:T(8,128)(2,1)S(1)} %get-tuple-element.40), channel_id=1, source_target_pairs={{0,4},{4,8},{8,12},{12,0},{1,5},{5,9},{9,13},{13,1},{2,6},{6,10},{... | collective-permute-start | bytes 1966088 | tf_op jit(solution)/shard_map/ppermute | solution.py:344
  15.1 15.7 %collective-permute-start.8 = (bf16[5,512,128]{2,1,0:T(8,128)(2,1)S(1)}, bf16[5,512,128]{2,1,0:T(8,128)(2,1)S(1)}, u32[]{:S(2)}, u32[]{:S(2)}) collective-permute-start(bf16[5,512,128]{2,1,0:T(8,128)(2,1)S(1)} %get-tuple-element.41), channel_id=1, source_target_pairs={{0,12},{4,0},{8,4},{12,8},{1,13},{5,1},{9,5},{13,9},{2,14},{6,2},{... | collective-permute-start | bytes 1966088 | tf_op jit(solution)/shard_map/ppermute | solution.py:344
  16.6 4.5 %collective-permute-start.4 = (bf16[128,128]{1,0:T(8,128)(2,1)S(1)}, bf16[128,128]{1,0:T(8,128)(2,1)S(1)}, u32[]{:S(2)}, u32[]{:S(2)}) collective-permute-start(bf16[128,128]{1,0:T(8,128)(2,1)S(1)} %add_convert_fusion.1), channel_id=1, source_target_pairs={{0,192},{64,0},{128,64},{192,128},{1,193},{65,1},{129,65},{193,129... | collective-permute-start | bytes 98312 | tf_op jit(solution)/shard_map/ppermute | solution.py:344
  19.4 4.3 %collective-permute-start.3 = (bf16[128,128]{1,0:T(8,128)(2,1)S(1)}, bf16[128,128]{1,0:T(8,128)(2,1)S(1)}, u32[]{:S(2)}, u32[]{:S(2)}) collective-permute-start(bf16[128,128]{1,0:T(8,128)(2,1)S(1)} %add_convert_fusion.1), channel_id=1, source_target_pairs={{0,64},{64,128},{128,192},{192,0},{1,65},{65,129},{129,193},{193,1... | collective-permute-start | bytes 98312 | tf_op jit(solution)/shard_map/ppermute | solution.py:344
  19.4 4.3 %collective-permute-start.2 = (bf16[128,128]{1,0:T(8,128)(2,1)S(1)}, bf16[128,128]{1,0:T(8,128)(2,1)S(1)}, u32[]{:S(2)}, u32[]{:S(2)}) collective-permute-start(bf16[128,128]{1,0:T(8,128)(2,1)S(1)} %add_convert_fusion.1), channel_id=1, source_target_pairs={{0,128},{64,192},{128,0},{192,64},{1,129},{65,193},{129,1},{193,65... | collective-permute-start | bytes 98312 | tf_op jit(solution)/shard_map/ppermute | solution.py:344
  23.8 4.0 %collective-permute-start.5 = (bf16[128,128]{1,0:T(8,128)(2,1)S(1)}, bf16[128,128]{1,0:T(8,128)(2,1)S(1)}, u32[]{:S(2)}, u32[]{:S(2)}) collective-permute-start(bf16[128,128]{1,0:T(8,128)(2,1)S(1)} %add_convert_fusion), channel_id=1, source_target_pairs={{0,32},{16,48},{32,0},{48,16},{1,33},{17,49},{33,1},{49,17},{2,34}... | collective-permute-start | bytes 98312 | tf_op jit(solution)/shard_map/ppermute | solution.py:344
  30.9 9.0 %collective-permute-start.10 = (bf16[1280,128]{1,0:T(8,128)(2,1)S(1)}, bf16[1280,128]{1,0:T(8,128)(2,1)S(1)}, u32[]{:S(2)}, u32[]{:S(2)}) collective-permute-start(bf16[1280,128]{1,0:T(8,128)(2,1)S(1)} %get-tuple-element.47), channel_id=1, source_target_pairs={{0,4},{4,8},{8,12},{12,0},{1,5},{5,9},{9,13},{13,1},{2,6},{6,10},{... | collective-permute-start | bytes 983048 | tf_op jit(solution)/shard_map/ppermute | solution.py:344
  31.9 8.1 %collective-permute-start.11 = (bf16[1280,128]{1,0:T(8,128)(2,1)S(1)}, bf16[1280,128]{1,0:T(8,128)(2,1)S(1)}, u32[]{:S(2)}, u32[]{:S(2)}) collective-permute-start(bf16[1280,128]{1,0:T(8,128)(2,1)S(1)} %get-tuple-element.48), channel_id=1, source_target_pairs={{0,12},{4,0},{8,4},{12,8},{1,13},{5,1},{9,5},{13,9},{2,14},{6,2},{... | collective-permute-start | bytes 983048 | tf_op jit(solution)/shard_map/ppermute | solution.py:344
  33.7 5.2 %collective-permute-start.9 = (bf16[128,128]{1,0:T(8,128)(2,1)S(1)}, bf16[128,128]{1,0:T(8,128)(2,1)S(1)}, u32[]{:S(2)}, u32[]{:S(2)}) collective-permute-start(bf16[128,128]{1,0:T(8,128)(2,1)S(1)} %convert_add_fusion.1), channel_id=1, source_target_pairs={{0,34},{2,32},{16,50},{18,48},{32,2},{34,0},{48,18},{50,16},{1,35}... | collective-permute-start | bytes 98312 | tf_op jit(solution)/shard_map/ppermute | solution.py:344
  40.0 18.2 %collective-permute-start.16 = (bf16[8,256,128]{2,1,0:T(8,128)(2,1)S(1)}, bf16[8,256,128]{2,1,0:T(8,128)(2,1)S(1)}, u32[]{:S(2)}, u32[]{:S(2)}) collective-permute-start(bf16[8,256,128]{2,1,0:T(8,128)(2,1)S(1)} %shard_map.108.refs_0_), channel_id=1, source_target_pairs={{0,192},{64,0},{128,64},{192,128},{1,193},{65,1},{129,65},{193,129... | collective-permute-start | bytes 1572872 | tf_op jit(solution)/shard_map/ppermute | solution.py:344
  42.8 15.4 %collective-permute-start.15 = (bf16[8,256,128]{2,1,0:T(8,128)(2,1)S(1)}, bf16[8,256,128]{2,1,0:T(8,128)(2,1)S(1)}, u32[]{:S(2)}, u32[]{:S(2)}) collective-permute-start(bf16[8,256,128]{2,1,0:T(8,128)(2,1)S(1)} %shard_map.108.refs_0_), channel_id=1, source_target_pairs={{0,64},{64,128},{128,192},{192,0},{1,65},{65,129},{129,193},{193,1... | collective-permute-start | bytes 1572872 | tf_op jit(solution)/shard_map/ppermute | solution.py:344
  42.8 7.6 %collective-permute-start.13 = (bf16[128,128]{1,0:T(8,128)(2,1)S(1)}, bf16[128,128]{1,0:T(8,128)(2,1)S(1)}, u32[]{:S(2)}, u32[]{:S(2)}) collective-permute-start(bf16[128,128]{1,0:T(8,128)(2,1)S(1)} %convert_add_fusion), channel_id=1, source_target_pairs={{0,4},{4,8},{8,12},{12,0},{1,5},{5,9},{9,13},{13,1},{2,6},{6,10},{... | collective-permute-start | bytes 98312 | tf_op jit(solution)/shard_map/ppermute | solution.py:344
  42.9 15.3 %collective-permute-start.17 = (bf16[1024,128]{1,0:T(8,128)(2,1)S(1)}, bf16[1024,128]{1,0:T(8,128)(2,1)S(1)}, u32[]{:S(2)}, u32[]{:S(2)}) collective-permute-start(bf16[1024,128]{1,0:T(8,128)(2,1)S(1)} %shard_map.109), channel_id=1, source_target_pairs={{0,2},{2,0},{1,3},{3,1},{4,6},{6,4},{5,7},{7,5},{8,10},{10,8},{9,1... | collective-permute-start | bytes 786440 | tf_op jit(solution)/shard_map/ppermute | solution.py:344
  46.8 4.9 %collective-permute-start.12 = (bf16[128,128]{1,0:T(8,128)(2,1)S(1)}, bf16[128,128]{1,0:T(8,128)(2,1)S(1)}, u32[]{:S(2)}, u32[]{:S(2)}) collective-permute-start(bf16[128,128]{1,0:T(8,128)(2,1)S(1)} %convert_add_fusion), channel_id=1, source_target_pairs={{0,8},{4,12},{8,0},{12,4},{1,9},{5,13},{9,1},{13,5},{2,10},{6,14},... | collective-permute-start | bytes 98312 | tf_op jit(solution)/shard_map/ppermute | solution.py:344
  50.4 3.1 %collective-permute-start.14 = (bf16[128,128]{1,0:T(8,128)(2,1)S(1)}, bf16[128,128]{1,0:T(8,128)(2,1)S(1)}, u32[]{:S(2)}, u32[]{:S(2)}) collective-permute-start(bf16[128,128]{1,0:T(8,128)(2,1)S(1)} %convert_add_fusion), channel_id=1, source_target_pairs={{0,12},{4,0},{8,4},{12,8},{1,13},{5,1},{9,5},{13,9},{2,14},{6,2},{... | collective-permute-start | bytes 98312 | tf_op jit(solution)/shard_map/ppermute | solution.py:344
  53.5 10.7 %copy-start.5 = (f32[128,128]{1,0:T(8,128)S(1)}, f32[128,128]{1,0:T(8,128)}, u32[]{:S(2)}) copy-start(f32[128,128]{1,0:T(8,128)} %constant.16.clone.refs_7_) | copy-start | bytes 196612
  58.3 7.8 %collective-permute-start.18 = (bf16[24,256,128]{2,1,0:T(8,128)(2,1)S(1)}, bf16[24,256,128]{2,1,0:T(8,128)(2,1)S(1)}, u32[]{:S(2)}, u32[]{:S(2)}) collective-permute-start(bf16[24,256,128]{2,1,0:T(8,128)(2,1)S(1)} %shard_map.110.early_ref), channel_id=1, source_target_pairs={{0,1},{1,0},{2,3},{3,2},{4,5},{5,4},{6,7},{7,6},{8,9},{9,8},{10,11... | collective-permute-start | bytes 4718600 | tf_op jit(solution)/shard_map/ppermute | solution.py:344
  60.7 9.3 %collective-permute-start.20 = (bf16[4,256,128]{2,1,0:T(8,128)(2,1)S(1)}, bf16[4,256,128]{2,1,0:T(8,128)(2,1)S(1)}, u32[]{:S(2)}, u32[]{:S(2)}) collective-permute-start(bf16[4,256,128]{2,1,0:T(8,128)(2,1)S(1)} %get-tuple-element.59), channel_id=1, source_target_pairs={{0,64},{64,128},{128,192},{192,0},{1,65},{65,129},{129,193},{193,1... | collective-permute-start | bytes 786440 | tf_op jit(solution)/shard_map/ppermute | solution.py:344
  61.0 9.1 %collective-permute-start.21 = (bf16[4,256,128]{2,1,0:T(8,128)(2,1)S(1)}, bf16[4,256,128]{2,1,0:T(8,128)(2,1)S(1)}, u32[]{:S(2)}, u32[]{:S(2)}) collective-permute-start(bf16[4,256,128]{2,1,0:T(8,128)(2,1)S(1)} %get-tuple-element.60), channel_id=1, source_target_pairs={{0,192},{64,0},{128,64},{192,128},{1,193},{65,1},{129,65},{193,129... | collective-permute-start | bytes 786440 | tf_op jit(solution)/shard_map/ppermute | solution.py:344
  63.6 2.5 %collective-permute-start.19 = (bf16[128,128]{1,0:T(8,128)(2,1)S(1)}, bf16[128,128]{1,0:T(8,128)(2,1)S(1)}, u32[]{:S(2)}, u32[]{:S(2)}) collective-permute-start(bf16[128,128]{1,0:T(8,128)(2,1)S(1)} %multiply_convert_fusion.band_ref), channel_id=1, source_target_pairs={{0,1},{1,0},{2,3},{3,2},{4,5},{5,4},{6,7},{7,6},{8,9},{9,8},{10,11... | collective-permute-start | bytes 98312 | tf_op jit(solution)/shard_map/ppermute | solution.py:344
  70.1 2.4 %collective-permute-start.22 = (bf16[8,256,128]{2,1,0:T(8,128)(2,1)S(1)}, bf16[8,256,128]{2,1,0:T(8,128)(2,1)S(1)}, u32[]{:S(2)}, u32[]{:S(2)}) collective-permute-start(bf16[8,256,128]{2,1,0:T(8,128)(2,1)S(1)} %shard_map.114.late_ref), channel_id=1, source_target_pairs={{0,1},{1,0},{2,3},{3,2},{4,5},{5,4},{6,7},{7,6},{8,9},{9,8},{10,11... | collective-permute-start | bytes 1572872 | tf_op jit(solution)/shard_map/ppermute | solution.py:344
  (7 other events, 36.5 us)

commit v7 on v6

--- a/solution.py
+++ b/solution.py
@@ -236,8 +236,8 @@
         r = slice(a * GROUP, (a + 1) * GROUP)
         summed = x_total(*refs[:5], 0, a) + z_ref[r].astype(f32)
         moment = momentum_decay * mom_ref[r] + summed
-        low = jnp.dot(moment, q, precision=HIGHEST, preferred_element_type=f32)
-        low = jnp.dot(q, low, precision=HIGHEST, preferred_element_type=f32)
+        low = jnp.dot(moment, q, preferred_element_type=f32)
+        low = jnp.dot(q, low, preferred_element_type=f32)
         out_ref[r] = moment - low
 
 

time: 75.1 us -> 75.1 us (level)
  Pallas kernels: 11 us -> 10.2 us
  waiting for transfers between devices: 23.4 us -> 24.2 us
    ppermute x23, waiting for transfers between devices: 23.4 us -> 24.2 us  [send(): return lax.ppermute(array, axis, perm)]
    pallas_call x8, Pallas kernels: 2.42 us -> 1.64 us  [small_call(): pl.pallas_call(kernel, out_shape=shapes, in_specs=[vmem] * len(args), out...]
  transfers between devices with their start and end apart: 23 -> 23, of which waited for: 11 -> 11; matrix products, arithmetic and copies ran while one was open for 0% -> 0% of each run, Pallas kernels for 11% -> 10%
where the time goes in v7:
time: 75.1 us; the launch traced here: 74.2 us
  starting transfers between devices  36.5 us (49%)
  waiting for transfers between devices  24.2 us (32%)
  Pallas kernels  10.2 us (14%)
  local copies, waits for them, and re-layouts  2.22 us (3%)
  between operations  0.94 us (1%)
    ppermute x23, starting transfers between devices, send(): return lax.ppermute(array, axis, perm)  36.5 us
    ppermute x23, waiting for transfers between devices, send(): return lax.ppermute(array, axis, perm)  24.2 us
    pallas_call x1, Pallas kernels, first_weights(): pl.pallas_call(first_weights_kernel, out_shape=[jax.ShapeDtypeStruct((ROW...  3.79 us
    unnamed x16, local copies, waits for them, and re-layouts  2.22 us
    pallas_call x1, Pallas kernels, pair_sum(): pl.pallas_call(pair_sum_kernel, out_shape=shapes, in_specs=[vmem] * 5, ou...  2 us
    pallas_call x8, Pallas kernels, small_call(): pl.pallas_call(kernel, out_shape=shapes, in_specs=[vmem] * len(args), out...  1.64 us
    pallas_call x1, Pallas kernels, last_weights(): pl.pallas_call(last_weights_kernel, out_shape=FULL, in_specs=[VMEM] * 4 +...  1.62 us
  transfers between devices with their start and end apart: 23, of which 11 were waited for; matrix products, arithmetic and copies ran while one was open for 0% of the time, Pallas kernels for 10%

profile of v7, /device:TPU:33, one launch (start us, length us, event | category | flops | bytes accessed | tf_op | source)
XLA Modules:
  0.0 74.2 jit_solution(2548253186619295511)
XLA Ops:
  0.6 2.2 %copy-done = bf16[1,1,1024,2048]{3,2,1,0:T(8,128)(2,1)S(1)} copy-done((bf16[1,1,1024,2048]{3,2,1,0:T(8,128)(2,1)S(1)}, bf16[1,1,1024,2048]{3,2,1,0:T(8,128)(2,1)}, u32[]{:S(2)}) %copy-start) | copy-done | bytes 4194328
  4.8 5.2 %collective-permute-start.6 = (bf16[256,128]{1,0:T(8,128)(2,1)S(1)}, bf16[256,128]{1,0:T(8,128)(2,1)S(1)}, u32[]{:S(2)}, u32[]{:S(2)}) collective-permute-start(bf16[256,128]{1,0:T(8,128)(2,1)S(1)} %shard_map.105.w0_ref), channel_id=1, source_target_pairs={{0,34},{2,32},{16,50},{18,48},{32,2},{34,0},{48,18},{50,16},{1,35}... | collective-permute-start | bytes 196616 | tf_op jit(solution)/shard_map/ppermute | solution.py:344
  10.0 2.0 %shard_map.104 = (bf16[5,512,128]{2,1,0:T(8,128)(2,1)S(1)}, bf16[5,512,128]{2,1,0:T(8,128)(2,1)S(1)}, bf16[2,512,128]{2,1,0:T(8,128)(2,1)S(1)}, bf16[2,512,128]{...) custom-call(bf16[8,1024,128]{2,1,0:T(8,128)(2,1)S(1)} %get-tuple-element.35.own_ref, ...), custom_call_target="tpu_custom_call" | custom-call | tf_op jit(solution)/shard_map/pallas_call | solution.py:124
  13.8 1.3 %collective-permute-start.7 = (bf16[5,512,128]{2,1,0:T(8,128)(2,1)S(1)}, bf16[5,512,128]{2,1,0:T(8,128)(2,1)S(1)}, u32[]{:S(2)}, u32[]{:S(2)}) collective-permute-start(bf16[5,512,128]{2,1,0:T(8,128)(2,1)S(1)} %get-tuple-element.40), channel_id=1, source_target_pairs={{0,4},{4,8},{8,12},{12,0},{1,5},{5,9},{9,13},{13,1},{2,6},{6,10},{... | collective-permute-start | bytes 1966088 | tf_op jit(solution)/shard_map/ppermute | solution.py:344
  15.1 1.5 %collective-permute-start.8 = (bf16[5,512,128]{2,1,0:T(8,128)(2,1)S(1)}, bf16[5,512,128]{2,1,0:T(8,128)(2,1)S(1)}, u32[]{:S(2)}, u32[]{:S(2)}) collective-permute-start(bf16[5,512,128]{2,1,0:T(8,128)(2,1)S(1)} %get-tuple-element.41), channel_id=1, source_target_pairs={{0,12},{4,0},{8,4},{12,8},{1,13},{5,1},{9,5},{13,9},{2,14},{6,2},{... | collective-permute-start | bytes 1966088 | tf_op jit(solution)/shard_map/ppermute | solution.py:344
  16.6 2.8 %collective-permute-start.4 = (bf16[128,128]{1,0:T(8,128)(2,1)S(1)}, bf16[128,128]{1,0:T(8,128)(2,1)S(1)}, u32[]{:S(2)}, u32[]{:S(2)}) collective-permute-start(bf16[128,128]{1,0:T(8,128)(2,1)S(1)} %add_convert_fusion.1), channel_id=1, source_target_pairs={{0,192},{64,0},{128,64},{192,128},{1,193},{65,1},{129,65},{193,129... | collective-permute-start | bytes 98312 | tf_op jit(solution)/shard_map/ppermute | solution.py:344
  19.4 1.6 %collective-permute-start.2 = (bf16[128,128]{1,0:T(8,128)(2,1)S(1)}, bf16[128,128]{1,0:T(8,128)(2,1)S(1)}, u32[]{:S(2)}, u32[]{:S(2)}) collective-permute-start(bf16[128,128]{1,0:T(8,128)(2,1)S(1)} %add_convert_fusion.1), channel_id=1, source_target_pairs={{0,128},{64,192},{128,0},{192,64},{1,129},{65,193},{129,1},{193,65... | collective-permute-start | bytes 98312 | tf_op jit(solution)/shard_map/ppermute | solution.py:344
  21.1 2.6 %collective-permute-done.3 = bf16[128,128]{1,0:T(8,128)(2,1)S(1)} collective-permute-done((bf16[128,128]{1,0:T(8,128)(2,1)S(1)}, bf16[128,128]{1,0:T(8,128)(2,1)S(1)}, u32[]{:S(2)}, u32[]{:S(2)}) %collective-permute-start.3) | collective-permute-done | bytes 32800 | tf_op jit(solution)/shard_map/ppermute | solution.py:344
  24.0 3.9 %collective-permute-done.5 = bf16[128,128]{1,0:T(8,128)(2,1)S(1)} collective-permute-done((bf16[128,128]{1,0:T(8,128)(2,1)S(1)}, bf16[128,128]{1,0:T(8,128)(2,1)S(1)}, u32[]{:S(2)}, u32[]{:S(2)}) %collective-permute-start.5) | collective-permute-done | bytes 32800 | tf_op jit(solution)/shard_map/ppermute | solution.py:344
  27.8 3.0 %collective-permute-done.7.left_ref.refs_1_ = bf16[5,512,128]{2,1,0:T(8,128)(2,1)S(1)} collective-permute-done((bf16[5,512,128]{2,1,0:T(8,128)(2,1)S(1)}, bf16[5,512,128]{2,1,0:T(8,128)(2,1)S(1)}, u32[]{:S(2)}, u32[]{:S(2)}) %collective-permute-start.7) | collective-permute-done | bytes 655392 | tf_op jit(solution)/shard_map/ppermute | solution.py:344
  31.9 1.8 %collective-permute-start.11 = (bf16[1280,128]{1,0:T(8,128)(2,1)S(1)}, bf16[1280,128]{1,0:T(8,128)(2,1)S(1)}, u32[]{:S(2)}, u32[]{:S(2)}) collective-permute-start(bf16[1280,128]{1,0:T(8,128)(2,1)S(1)} %get-tuple-element.48), channel_id=1, source_target_pairs={{0,12},{4,0},{8,4},{12,8},{1,13},{5,1},{9,5},{13,9},{2,14},{6,2},{... | collective-permute-start | bytes 983048 | tf_op jit(solution)/shard_map/ppermute | solution.py:344
  33.7 2.5 %collective-permute-start.9 = (bf16[128,128]{1,0:T(8,128)(2,1)S(1)}, bf16[128,128]{1,0:T(8,128)(2,1)S(1)}, u32[]{:S(2)}, u32[]{:S(2)}) collective-permute-start(bf16[128,128]{1,0:T(8,128)(2,1)S(1)} %convert_add_fusion.1), channel_id=1, source_target_pairs={{0,34},{2,32},{16,50},{18,48},{32,2},{34,0},{48,18},{50,16},{1,35}... | collective-permute-start | bytes 98312 | tf_op jit(solution)/shard_map/ppermute | solution.py:344
  36.2 2.7 %collective-permute-done.9 = bf16[128,128]{1,0:T(8,128)(2,1)S(1)} collective-permute-done((bf16[128,128]{1,0:T(8,128)(2,1)S(1)}, bf16[128,128]{1,0:T(8,128)(2,1)S(1)}, u32[]{:S(2)}, u32[]{:S(2)}) %collective-permute-start.9) | collective-permute-done | bytes 32800 | tf_op jit(solution)/shard_map/ppermute | solution.py:344
  40.0 2.8 %collective-permute-start.16 = (bf16[8,256,128]{2,1,0:T(8,128)(2,1)S(1)}, bf16[8,256,128]{2,1,0:T(8,128)(2,1)S(1)}, u32[]{:S(2)}, u32[]{:S(2)}) collective-permute-start(bf16[8,256,128]{2,1,0:T(8,128)(2,1)S(1)} %shard_map.108.refs_0_), channel_id=1, source_target_pairs={{0,192},{64,0},{128,64},{192,128},{1,193},{65,1},{129,65},{193,129... | collective-permute-start | bytes 1572872 | tf_op jit(solution)/shard_map/ppermute | solution.py:344
  42.9 3.9 %collective-permute-start.17 = (bf16[1024,128]{1,0:T(8,128)(2,1)S(1)}, bf16[1024,128]{1,0:T(8,128)(2,1)S(1)}, u32[]{:S(2)}, u32[]{:S(2)}) collective-permute-start(bf16[1024,128]{1,0:T(8,128)(2,1)S(1)} %shard_map.109), channel_id=1, source_target_pairs={{0,2},{2,0},{1,3},{3,1},{4,6},{6,4},{5,7},{7,5},{8,10},{10,8},{9,1... | collective-permute-start | bytes 786440 | tf_op jit(solution)/shard_map/ppermute | solution.py:344
  46.8 3.6 %collective-permute-start.12 = (bf16[128,128]{1,0:T(8,128)(2,1)S(1)}, bf16[128,128]{1,0:T(8,128)(2,1)S(1)}, u32[]{:S(2)}, u32[]{:S(2)}) collective-permute-start(bf16[128,128]{1,0:T(8,128)(2,1)S(1)} %convert_add_fusion), channel_id=1, source_target_pairs={{0,8},{4,12},{8,0},{12,4},{1,9},{5,13},{9,1},{13,5},{2,10},{6,14},... | collective-permute-start | bytes 98312 | tf_op jit(solution)/shard_map/ppermute | solution.py:344
  51.7 1.8 %collective-permute-done.14 = bf16[128,128]{1,0:T(8,128)(2,1)S(1)} collective-permute-done((bf16[128,128]{1,0:T(8,128)(2,1)S(1)}, bf16[128,128]{1,0:T(8,128)(2,1)S(1)}, u32[]{:S(2)}, u32[]{:S(2)}) %collective-permute-start.14) | collective-permute-done | bytes 32800 | tf_op jit(solution)/shard_map/ppermute | solution.py:344
  53.5 4.7 %collective-permute-done.17.refs_5_ = bf16[1024,128]{1,0:T(8,128)(2,1)S(1)} collective-permute-done((bf16[1024,128]{1,0:T(8,128)(2,1)S(1)}, bf16[1024,128]{1,0:T(8,128)(2,1)S(1)}, u32[]{:S(2)}, u32[]{:S(2)}) %collective-permute-start.17) | collective-permute-done | bytes 262176 | tf_op jit(solution)/shard_map/ppermute | solution.py:344
  58.3 2.3 %collective-permute-start.18 = (bf16[24,256,128]{2,1,0:T(8,128)(2,1)S(1)}, bf16[24,256,128]{2,1,0:T(8,128)(2,1)S(1)}, u32[]{:S(2)}, u32[]{:S(2)}) collective-permute-start(bf16[24,256,128]{2,1,0:T(8,128)(2,1)S(1)} %shard_map.110.early_ref), channel_id=1, source_target_pairs={{0,1},{1,0},{2,3},{3,2},{4,5},{5,4},{6,7},{7,6},{8,9},{9,8},{10,11... | collective-permute-start | bytes 4718600 | tf_op jit(solution)/shard_map/ppermute | solution.py:344
  61.0 2.6 %collective-permute-start.21 = (bf16[4,256,128]{2,1,0:T(8,128)(2,1)S(1)}, bf16[4,256,128]{2,1,0:T(8,128)(2,1)S(1)}, u32[]{:S(2)}, u32[]{:S(2)}) collective-permute-start(bf16[4,256,128]{2,1,0:T(8,128)(2,1)S(1)} %get-tuple-element.60), channel_id=1, source_target_pairs={{0,192},{64,0},{128,64},{192,128},{1,193},{65,1},{129,65},{193,129... | collective-permute-start | bytes 786440 | tf_op jit(solution)/shard_map/ppermute | solution.py:344
  64.2 1.2 %shard_map.112 = f32[1024,128]{1,0:T(8,128)} custom-call(bf16[2,1024,128]{2,1,0:T(8,128)(2,1)S(1)} %get-tuple-element.52.refs_0_, bf16[5,512,128]{2,1,0:T(8,128)(2,1)S(1)} %collective-permute-done.7.left_ref.refs_1_, bf16[5,512,128]{2,1,0:T(8,128)(2,1)S(1)} %collective-permute-done.8.right_ref.refs_2_, ...), custom_call_target="tpu_custom_call" | custom-call | tf_op jit(solution)/shard_map/pallas_call | solution.py:136
  65.4 3.8 %shard_map.111 = (f32[1024,128]{1,0:T(8,128)}, bf16[1024,2048]{1,0:T(8,128)(2,1)}, bf16[1024,256]{1,0:T(8,128)(2,1)S(1)}) custom-call(bf16[24,256,128]{2,1,0:T(8,128)(2,1)S(1)} %shard_map.110.early_ref, bf16[24,256,128]{2,1,0:T(8,128)(2,1)S(1)} %collective-permute-done.18.early_other_ref, bf16[128,128]{1,0:T(8,128)(2,1)S(1)} %multiply_convert_fusion.band_ref, ...), custom_call_target="tpu_custom_call" | custom-call | tf_op jit(solution)/shard_map/pallas_call | solution.py:314
  70.9 1.5 %collective-permute-done.22.late_other_ref = bf16[8,256,128]{2,1,0:T(8,128)(2,1)S(1)} collective-permute-done((bf16[8,256,128]{2,1,0:T(8,128)(2,1)S(1)}, bf16[8,256,128]{2,1,0:T(8,128)(2,1)S(1)}, u32[]{:S(2)}, u32[]{:S(2)}) %collective-permute-start.22) | collective-permute-done | bytes 524320 | tf_op jit(solution)/shard_map/ppermute | solution.py:344
  72.5 1.6 %shard_map.115 = bf16[1024,2048]{1,0:T(8,128)(2,1)} custom-call(bf16[8,256,128]{2,1,0:T(8,128)(2,1)S(1)} %shard_map.114.late_ref, bf16[8,256,128]{2,1,0:T(8,128)(2,1)S(1)} %collective-permute-done.22.late_other_ref, bf16[1024,256]{1,0:T(8,128)(2,1)S(1)} %get-tuple-element.65.spread_ref, f32[128,128]{1,0:T(8,128)S(1)} %copy-done.3, ...), custom_call_target="tpu_custom_call", output_to_operand_aliasing={{}: (4, {})} | custom-call | tf_op jit(solution)/shard_map/pallas_call | solution.py:332
  (58 shorter events, 10.3 us)
Async XLA Ops:
  4.0 6.0 %collective-permute-start = (bf16[8,1024,128]{2,1,0:T(8,128)(2,1)S(1)}, bf16[8,1024,128]{2,1,0:T(8,128)(2,1)S(1)}, u32[]{:S(2)}, u32[]{:S(2)}) collective-permute-start(bf16[8,1024,128]{2,1,0:T(8,128)(2,1)S(1)} %get-tuple-element.36), channel_id=1, source_target_pairs={{0,1},{1,0},{2,3},{3,2},{4,5},{5,4},{6,7},{7,6},{8,9},{9,8},{10,11... | collective-permute-start | bytes 6291464 | tf_op jit(solution)/shard_map/ppermute | solution.py:344
  4.8 9.0 %collective-permute-start.6 = (bf16[256,128]{1,0:T(8,128)(2,1)S(1)}, bf16[256,128]{1,0:T(8,128)(2,1)S(1)}, u32[]{:S(2)}, u32[]{:S(2)}) collective-permute-start(bf16[256,128]{1,0:T(8,128)(2,1)S(1)} %shard_map.105.w0_ref), channel_id=1, source_target_pairs={{0,34},{2,32},{16,50},{18,48},{32,2},{34,0},{48,18},{50,16},{1,35}... | collective-permute-start | bytes 196616 | tf_op jit(solution)/shard_map/ppermute | solution.py:344
  12.0 4.6 %collective-permute-start.1 = (bf16[128,128]{1,0:T(8,128)(2,1)S(1)}, bf16[128,128]{1,0:T(8,128)(2,1)S(1)}, u32[]{:S(2)}, u32[]{:S(2)}) collective-permute-start(bf16[128,128]{1,0:T(8,128)(2,1)S(1)} %convert_element_type.60), channel_id=1, source_target_pairs={{0,16},{16,0},{32,48},{48,32},{1,17},{17,1},{33,49},{49,33},{2,18}... | collective-permute-start | bytes 98312 | tf_op jit(solution)/shard_map/ppermute | solution.py:344
  13.8 17.0 %collective-permute-start.7 = (bf16[5,512,128]{2,1,0:T(8,128)(2,1)S(1)}, bf16[5,512,128]{2,1,0:T(8,128)(2,1)S(1)}, u32[]{:S(2)}, u32[]{:S(2)}) collective-permute-start(bf16[5,512,128]{2,1,0:T(8,128)(2,1)S(1)} %get-tuple-element.40), channel_id=1, source_target_pairs={{0,4},{4,8},{8,12},{12,0},{1,5},{5,9},{9,13},{13,1},{2,6},{6,10},{... | collective-permute-start | bytes 1966088 | tf_op jit(solution)/shard_map/ppermute | solution.py:344
  15.1 15.7 %collective-permute-start.8 = (bf16[5,512,128]{2,1,0:T(8,128)(2,1)S(1)}, bf16[5,512,128]{2,1,0:T(8,128)(2,1)S(1)}, u32[]{:S(2)}, u32[]{:S(2)}) collective-permute-start(bf16[5,512,128]{2,1,0:T(8,128)(2,1)S(1)} %get-tuple-element.41), channel_id=1, source_target_pairs={{0,12},{4,0},{8,4},{12,8},{1,13},{5,1},{9,5},{13,9},{2,14},{6,2},{... | collective-permute-start | bytes 1966088 | tf_op jit(solution)/shard_map/ppermute | solution.py:344
  16.6 4.5 %collective-permute-start.4 = (bf16[128,128]{1,0:T(8,128)(2,1)S(1)}, bf16[128,128]{1,0:T(8,128)(2,1)S(1)}, u32[]{:S(2)}, u32[]{:S(2)}) collective-permute-start(bf16[128,128]{1,0:T(8,128)(2,1)S(1)} %add_convert_fusion.1), channel_id=1, source_target_pairs={{0,192},{64,0},{128,64},{192,128},{1,193},{65,1},{129,65},{193,129... | collective-permute-start | bytes 98312 | tf_op jit(solution)/shard_map/ppermute | solution.py:344
  19.4 4.3 %collective-permute-start.3 = (bf16[128,128]{1,0:T(8,128)(2,1)S(1)}, bf16[128,128]{1,0:T(8,128)(2,1)S(1)}, u32[]{:S(2)}, u32[]{:S(2)}) collective-permute-start(bf16[128,128]{1,0:T(8,128)(2,1)S(1)} %add_convert_fusion.1), channel_id=1, source_target_pairs={{0,64},{64,128},{128,192},{192,0},{1,65},{65,129},{129,193},{193,1... | collective-permute-start | bytes 98312 | tf_op jit(solution)/shard_map/ppermute | solution.py:344
  19.4 4.3 %collective-permute-start.2 = (bf16[128,128]{1,0:T(8,128)(2,1)S(1)}, bf16[128,128]{1,0:T(8,128)(2,1)S(1)}, u32[]{:S(2)}, u32[]{:S(2)}) collective-permute-start(bf16[128,128]{1,0:T(8,128)(2,1)S(1)} %add_convert_fusion.1), channel_id=1, source_target_pairs={{0,128},{64,192},{128,0},{192,64},{1,129},{65,193},{129,1},{193,65... | collective-permute-start | bytes 98312 | tf_op jit(solution)/shard_map/ppermute | solution.py:344
  23.8 4.0 %collective-permute-start.5 = (bf16[128,128]{1,0:T(8,128)(2,1)S(1)}, bf16[128,128]{1,0:T(8,128)(2,1)S(1)}, u32[]{:S(2)}, u32[]{:S(2)}) collective-permute-start(bf16[128,128]{1,0:T(8,128)(2,1)S(1)} %add_convert_fusion), channel_id=1, source_target_pairs={{0,32},{16,48},{32,0},{48,16},{1,33},{17,49},{33,1},{49,17},{2,34}... | collective-permute-start | bytes 98312 | tf_op jit(solution)/shard_map/ppermute | solution.py:344
  30.9 9.0 %collective-permute-start.10 = (bf16[1280,128]{1,0:T(8,128)(2,1)S(1)}, bf16[1280,128]{1,0:T(8,128)(2,1)S(1)}, u32[]{:S(2)}, u32[]{:S(2)}) collective-permute-start(bf16[1280,128]{1,0:T(8,128)(2,1)S(1)} %get-tuple-element.47), channel_id=1, source_target_pairs={{0,4},{4,8},{8,12},{12,0},{1,5},{5,9},{9,13},{13,1},{2,6},{6,10},{... | collective-permute-start | bytes 983048 | tf_op jit(solution)/shard_map/ppermute | solution.py:344
  31.9 8.1 %collective-permute-start.11 = (bf16[1280,128]{1,0:T(8,128)(2,1)S(1)}, bf16[1280,128]{1,0:T(8,128)(2,1)S(1)}, u32[]{:S(2)}, u32[]{:S(2)}) collective-permute-start(bf16[1280,128]{1,0:T(8,128)(2,1)S(1)} %get-tuple-element.48), channel_id=1, source_target_pairs={{0,12},{4,0},{8,4},{12,8},{1,13},{5,1},{9,5},{13,9},{2,14},{6,2},{... | collective-permute-start | bytes 983048 | tf_op jit(solution)/shard_map/ppermute | solution.py:344
  33.7 5.2 %collective-permute-start.9 = (bf16[128,128]{1,0:T(8,128)(2,1)S(1)}, bf16[128,128]{1,0:T(8,128)(2,1)S(1)}, u32[]{:S(2)}, u32[]{:S(2)}) collective-permute-start(bf16[128,128]{1,0:T(8,128)(2,1)S(1)} %convert_add_fusion.1), channel_id=1, source_target_pairs={{0,34},{2,32},{16,50},{18,48},{32,2},{34,0},{48,18},{50,16},{1,35}... | collective-permute-start | bytes 98312 | tf_op jit(solution)/shard_map/ppermute | solution.py:344
  40.0 18.2 %collective-permute-start.16 = (bf16[8,256,128]{2,1,0:T(8,128)(2,1)S(1)}, bf16[8,256,128]{2,1,0:T(8,128)(2,1)S(1)}, u32[]{:S(2)}, u32[]{:S(2)}) collective-permute-start(bf16[8,256,128]{2,1,0:T(8,128)(2,1)S(1)} %shard_map.108.refs_0_), channel_id=1, source_target_pairs={{0,192},{64,0},{128,64},{192,128},{1,193},{65,1},{129,65},{193,129... | collective-permute-start | bytes 1572872 | tf_op jit(solution)/shard_map/ppermute | solution.py:344
  42.8 15.4 %collective-permute-start.15 = (bf16[8,256,128]{2,1,0:T(8,128)(2,1)S(1)}, bf16[8,256,128]{2,1,0:T(8,128)(2,1)S(1)}, u32[]{:S(2)}, u32[]{:S(2)}) collective-permute-start(bf16[8,256,128]{2,1,0:T(8,128)(2,1)S(1)} %shard_map.108.refs_0_), channel_id=1, source_target_pairs={{0,64},{64,128},{128,192},{192,0},{1,65},{65,129},{129,193},{193,1... | collective-permute-start | bytes 1572872 | tf_op jit(solution)/shard_map/ppermute | solution.py:344
  42.8 7.6 %collective-permute-start.13 = (bf16[128,128]{1,0:T(8,128)(2,1)S(1)}, bf16[128,128]{1,0:T(8,128)(2,1)S(1)}, u32[]{:S(2)}, u32[]{:S(2)}) collective-permute-start(bf16[128,128]{1,0:T(8,128)(2,1)S(1)} %convert_add_fusion), channel_id=1, source_target_pairs={{0,4},{4,8},{8,12},{12,0},{1,5},{5,9},{9,13},{13,1},{2,6},{6,10},{... | collective-permute-start | bytes 98312 | tf_op jit(solution)/shard_map/ppermute | solution.py:344
  42.9 15.3 %collective-permute-start.17 = (bf16[1024,128]{1,0:T(8,128)(2,1)S(1)}, bf16[1024,128]{1,0:T(8,128)(2,1)S(1)}, u32[]{:S(2)}, u32[]{:S(2)}) collective-permute-start(bf16[1024,128]{1,0:T(8,128)(2,1)S(1)} %shard_map.109), channel_id=1, source_target_pairs={{0,2},{2,0},{1,3},{3,1},{4,6},{6,4},{5,7},{7,5},{8,10},{10,8},{9,1... | collective-permute-start | bytes 786440 | tf_op jit(solution)/shard_map/ppermute | solution.py:344
  46.8 4.9 %collective-permute-start.12 = (bf16[128,128]{1,0:T(8,128)(2,1)S(1)}, bf16[128,128]{1,0:T(8,128)(2,1)S(1)}, u32[]{:S(2)}, u32[]{:S(2)}) collective-permute-start(bf16[128,128]{1,0:T(8,128)(2,1)S(1)} %convert_add_fusion), channel_id=1, source_target_pairs={{0,8},{4,12},{8,0},{12,4},{1,9},{5,13},{9,1},{13,5},{2,10},{6,14},... | collective-permute-start | bytes 98312 | tf_op jit(solution)/shard_map/ppermute | solution.py:344
  50.4 3.1 %collective-permute-start.14 = (bf16[128,128]{1,0:T(8,128)(2,1)S(1)}, bf16[128,128]{1,0:T(8,128)(2,1)S(1)}, u32[]{:S(2)}, u32[]{:S(2)}) collective-permute-start(bf16[128,128]{1,0:T(8,128)(2,1)S(1)} %convert_add_fusion), channel_id=1, source_target_pairs={{0,12},{4,0},{8,4},{12,8},{1,13},{5,1},{9,5},{13,9},{2,14},{6,2},{... | collective-permute-start | bytes 98312 | tf_op jit(solution)/shard_map/ppermute | solution.py:344
  53.5 10.7 %copy-start.5 = (f32[128,128]{1,0:T(8,128)S(1)}, f32[128,128]{1,0:T(8,128)}, u32[]{:S(2)}) copy-start(f32[128,128]{1,0:T(8,128)} %constant.16.clone.refs_7_) | copy-start | bytes 196612
  58.3 7.1 %collective-permute-start.18 = (bf16[24,256,128]{2,1,0:T(8,128)(2,1)S(1)}, bf16[24,256,128]{2,1,0:T(8,128)(2,1)S(1)}, u32[]{:S(2)}, u32[]{:S(2)}) collective-permute-start(bf16[24,256,128]{2,1,0:T(8,128)(2,1)S(1)} %shard_map.110.early_ref), channel_id=1, source_target_pairs={{0,1},{1,0},{2,3},{3,2},{4,5},{5,4},{6,7},{7,6},{8,9},{9,8},{10,11... | collective-permute-start | bytes 4718600 | tf_op jit(solution)/shard_map/ppermute | solution.py:344
  60.7 9.3 %collective-permute-start.20 = (bf16[4,256,128]{2,1,0:T(8,128)(2,1)S(1)}, bf16[4,256,128]{2,1,0:T(8,128)(2,1)S(1)}, u32[]{:S(2)}, u32[]{:S(2)}) collective-permute-start(bf16[4,256,128]{2,1,0:T(8,128)(2,1)S(1)} %get-tuple-element.59), channel_id=1, source_target_pairs={{0,64},{64,128},{128,192},{192,0},{1,65},{65,129},{129,193},{193,1... | collective-permute-start | bytes 786440 | tf_op jit(solution)/shard_map/ppermute | solution.py:344
  61.0 9.1 %collective-permute-start.21 = (bf16[4,256,128]{2,1,0:T(8,128)(2,1)S(1)}, bf16[4,256,128]{2,1,0:T(8,128)(2,1)S(1)}, u32[]{:S(2)}, u32[]{:S(2)}) collective-permute-start(bf16[4,256,128]{2,1,0:T(8,128)(2,1)S(1)} %get-tuple-element.60), channel_id=1, source_target_pairs={{0,192},{64,0},{128,64},{192,128},{1,193},{65,1},{129,65},{193,129... | collective-permute-start | bytes 786440 | tf_op jit(solution)/shard_map/ppermute | solution.py:344
  63.6 1.7 %collective-permute-start.19 = (bf16[128,128]{1,0:T(8,128)(2,1)S(1)}, bf16[128,128]{1,0:T(8,128)(2,1)S(1)}, u32[]{:S(2)}, u32[]{:S(2)}) collective-permute-start(bf16[128,128]{1,0:T(8,128)(2,1)S(1)} %multiply_convert_fusion.band_ref), channel_id=1, source_target_pairs={{0,1},{1,0},{2,3},{3,2},{4,5},{5,4},{6,7},{7,6},{8,9},{9,8},{10,11... | collective-permute-start | bytes 98312 | tf_op jit(solution)/shard_map/ppermute | solution.py:344
  70.1 2.4 %collective-permute-start.22 = (bf16[8,256,128]{2,1,0:T(8,128)(2,1)S(1)}, bf16[8,256,128]{2,1,0:T(8,128)(2,1)S(1)}, u32[]{:S(2)}, u32[]{:S(2)}) collective-permute-start(bf16[8,256,128]{2,1,0:T(8,128)(2,1)S(1)} %shard_map.114.late_ref), channel_id=1, source_target_pairs={{0,1},{1,0},{2,3},{3,2},{4,5},{5,4},{6,7},{7,6},{8,9},{9,8},{10,11... | collective-permute-start | bytes 1572872 | tf_op jit(solution)/shard_map/ppermute | solution.py:344
  (7 other events, 34.9 us)
